TPU v7x, 128 devices: a whole 4x4x4 slice. The times are simulated.
128 devices in a mesh: seq: 8 (over x, core), pipe: 16 (over y, z).
Axes of the slice: x: 4, y: 4, z: 4, core: 2. Of those that a mesh axis runs over, the one named last changes fastest.
Arguments:
- queries: bfloat16 [16, 1024, 8192], P('pipe', 'seq'), may hold values from -160 to 160
- layer_key_rows: bfloat16 [16, 1024, 1024], P('pipe', 'seq'), may hold values from -4 to 4
- layer_value_rows: bfloat16 [16, 1024, 1024], P('pipe', 'seq'), may hold values from -5 to 5
- vertical_blocks: int32 [16, 64, 4], P('pipe'), may hold values from 0 to 15, as said below
- slash_offsets: int32 [16, 64, 4], P('pipe'), may hold values from 0 to 15, as said below
- prompt_lengths: int32 [4], replicated, may hold values from 1 to 512, 1024 in all
- residual: bfloat16 [1024, 8192], P('seq'), may hold values from -3 to 3
- out_weight: bfloat16 [16, 8192, 8192], P('pipe', 'seq'), may hold values from -0.5 to 0.5
- section_gain: float32 [16, 8192], P('pipe'), may hold values from 0.25 to 1.75
Outputs:
- normed_hidden: bfloat16 [16, 1024, 8192], P('pipe', 'seq')
Inputs may be any that keep to these rules, and one draw needn't show every extreme that they name: `vertical_blocks`: for each section and head the 4 entries are different and the first is block 0. `slash_offsets`: for each section and head the 4 entries are different and the first is offset 0. `prompt_lengths`: the lengths sum to 1024.
All inputs are finite; a program needn't handle non-finite values.
Results may differ from a plain program's by a relative error of at most 0.02.
Values may be sent and summed in bfloat16 or wider, within the bound.
No kernel may reach another device: no remote copies, remote signals or barrier semaphores. Data moves between devices by JAX's collectives and lax.ppermute only.
A program may use at most 192 MiB of HBM per device.

v0:
```python
import math

import jax
import jax.numpy as jnp
from jax import lax
from jax.sharding import PartitionSpec as P

QUERY_HEADS = 64
KEY_VALUE_HEADS = 8
HEAD_SIZE = 128
BLOCK = 64


def entering(value, axis, join, neutral):
    place = lax.axis_index(axis)
    gathered = lax.all_gather(value.astype(jnp.bfloat16), axis)
    state = jnp.zeros_like(value) + jnp.asarray(neutral, value.dtype)

    def one(step, state):
        return join(state, lax.dynamic_index_in_dim(gathered, step, 0, False).astype(value.dtype))

    return lax.fori_loop(0, place, one, state)


def prompt_ids(prompt_lengths, seq_len):
    starts = jnp.cumsum(prompt_lengths) - prompt_lengths
    positions = jnp.arange(seq_len, dtype=jnp.int32)
    return jnp.sum((positions[:, None] >= starts[None, 1:]).astype(jnp.int32), axis=1)


def block_permitted(vertical_pattern, slash_pattern, blocks):
    numbers = jnp.arange(blocks, dtype=jnp.int32)
    offsets = numbers[:, None] - numbers[None, :]
    vert_hit = jnp.any(vertical_pattern[:, :, None] == numbers[None, None, :], axis=1)
    slash_hit = jnp.any(slash_pattern[:, :, None, None] == offsets[None, None, :, :], axis=1)
    return (vert_hit[:, None, :] | slash_hit) & (offsets >= 0)[None, :, :]


def softmax_weights(scores, allowed, axes):
    masked = jnp.where(allowed, scores, -1e30)
    largest = jnp.max(masked, axis=axes, keepdims=True)
    exponent = jnp.where(allowed, jnp.exp(masked - largest), 0.0)
    return (exponent / jnp.sum(exponent, axis=axes, keepdims=True)).astype(jnp.bfloat16)


def dense_context(query_local, key_local, value_local, vert_local, slash_local, doc_ids):
    seq_len, heads_here = (query_local.shape[0], query_local.shape[1])
    kv_here = key_local.shape[1]
    group_index = heads_here // kv_here
    blocks = seq_len // BLOCK
    row_count = math.gcd(seq_len, 512)
    row_steps = seq_len // row_count
    positions = jnp.arange(seq_len, dtype=jnp.int32)
    tok_block = positions // BLOCK
    block_mask_table = block_permitted(vert_local, slash_local, blocks)
    scale = 1.0 / math.sqrt(HEAD_SIZE)

    def one_head(head):
        query_head = lax.dynamic_index_in_dim(query_local, head, 1, keepdims=False)
        key_head = lax.dynamic_index_in_dim(key_local, head // group_index, 1, keepdims=False)
        value_head = lax.dynamic_index_in_dim(value_local, head // group_index, 1, keepdims=False)
        mask_head = lax.dynamic_index_in_dim(block_mask_table, head, 0, keepdims=False)

        def one_rows(step):
            first = step * row_count
            query_part = lax.dynamic_slice_in_dim(query_head, first, row_count, 0)
            scores = (
                jnp.einsum("sd,td->st", query_part, key_head, preferred_element_type=jnp.float32)
                * scale
            )
            query_pos = first + jnp.arange(row_count, dtype=jnp.int32)
            allowed = mask_head[query_pos // BLOCK][:, tok_block]
            allowed = allowed & (positions[None, :] <= query_pos[:, None])
            allowed = allowed & (doc_ids[query_pos][:, None] == doc_ids[None, :])
            weights = softmax_weights(scores, allowed, (1,))
            return jnp.dot(weights, value_head, preferred_element_type=jnp.float32).astype(
                jnp.bfloat16
            )

        return lax.map(one_rows, jnp.arange(row_steps, dtype=jnp.int32)).reshape(seq_len, HEAD_SIZE)

    context = lax.map(one_head, jnp.arange(heads_here, dtype=jnp.int32))
    return context.transpose(1, 0, 2).reshape(seq_len, heads_here * HEAD_SIZE)


def local(
    queries,
    layer_key_rows,
    layer_value_rows,
    vertical_blocks,
    slash_offsets,
    prompt_lengths,
    residual,
    out_weight,
    section_gain,
):
    local_tokens = queries.shape[1]
    query_rows = queries[0].reshape(local_tokens, QUERY_HEADS, HEAD_SIZE)
    key_head_split = layer_key_rows[0].reshape(local_tokens, KEY_VALUE_HEADS, HEAD_SIZE)
    value_head_split = layer_value_rows[0].reshape(local_tokens, KEY_VALUE_HEADS, HEAD_SIZE)
    query_local, key_local, value_local = (
        lax.all_to_all(query_rows, "seq", split_axis=1, concat_axis=0, tiled=True),
        lax.all_to_all(key_head_split, "seq", split_axis=1, concat_axis=0, tiled=True),
        lax.all_to_all(value_head_split, "seq", split_axis=1, concat_axis=0, tiled=True),
    )
    seq_len, heads_here = (query_local.shape[0], query_local.shape[1])
    first_head = lax.axis_index("seq") * heads_here
    vert_local = lax.dynamic_slice_in_dim(vertical_blocks[0], first_head, heads_here, 0)
    slash_local = lax.dynamic_slice_in_dim(slash_offsets[0], first_head, heads_here, 0)
    doc_ids = prompt_ids(prompt_lengths, seq_len)
    context = dense_context(query_local, key_local, value_local, vert_local, slash_local, doc_ids)
    weight_rows = out_weight[0]
    section_term = lax.psum_scatter(
        jnp.dot(context, weight_rows, preferred_element_type=jnp.float32).astype(jnp.bfloat16),
        "seq",
        scatter_dimension=0,
        tiled=True,
    ).astype(jnp.float32)
    earlier = entering(section_term, "pipe", jnp.add, jnp.zeros_like(section_term))
    total_sum = earlier + section_term
    stream = residual.astype(jnp.float32) + total_sum
    inverse_rms = lax.rsqrt(jnp.mean(stream * stream, axis=-1, keepdims=True) + 1e-06)
    return (stream * inverse_rms * section_gain[0][None, :]).astype(jnp.bfloat16)[None]


def solution(mesh):
    placed = (
        P("pipe", "seq", None),
        P("pipe", "seq", None),
        P("pipe", "seq", None),
        P("pipe", None, None),
        P("pipe", None, None),
        P(),
        P("seq", None),
        P("pipe", "seq", None),
        P("pipe", None),
    )
    return jax.shard_map(
        local, mesh=mesh, in_specs=placed, out_specs=P("pipe", "seq", None), check_vma=False
    )
```

profile of v0, /device:TPU:121, one launch (start us, length us, event | category | flops | bytes accessed | tf_op | source)
XLA Modules:
  0.0 735.7 jit_solution(15372266941801167988)
XLA Ops:
  8.3 5.0 all-to-all-start.1
  25.8 24.8 %all-to-all-done = bf16[128,64,128]{2,0,1:T(8,128)(2,1)S(1)} async-done(((bf16[128,64,128]{2,0,1:T(8,128)(2,1)}), bf16[128,64,128]{2,0,1:T(8,128)(2,1)S(1)}, u32[]{:S(2)}, u32[]{:S(2)}) %all-to-all-start) | async-done | bytes 2097184 | tf_op jit(solution)/shard_map/all_to_all | solution.py:102
  50.7 4.8 all-to-all-start.2
  57.2 4.9 all-to-all-done.2
  62.1 261.5 %while.45 = (s32[]{:T(128)}, bf16[8,1024,128]{1,2,0:T(8,128)(2,1)}, s32[8]{0:T(128)S(1)}, bf16[1024,8,128]{2,0,1:T(8,128)(2,1)S(1)}, bf16[1024,1,128]{2,0,1:T(8,...) while((s32[]{:T(128)}, bf16[8,1024,128]{1,2,0:T(8,128)(2,1)}, ...), condition=%wide.region_9.10_spmd.clone, body=%wide.region_4.9_spmd.clone.sunk | while | flops 282157056 | bytes 12456998 | solution.py:82
  64.9 29.0 %while.46 = (s32[]{:T(128)}, bf16[2,512,128]{2,1,0:T(8,128)(2,1)S(1)}, s32[2]{0:T(128)S(1)}, pred[16,16]{1,0:T(8,128)(4,1)S(1)}, s32[1024]{0:T(1024)S(1)}, /*ind...) while((s32[]{:T(128)}, ...), condition=%wide.region_8.8_spmd, body=%wide.region_5.7_spmd.sunk | while | flops 282148864 | bytes 10875095 | solution.py:80
  97.6 29.0 %while.46 = (s32[]{:T(128)}, bf16[2,512,128]{2,1,0:T(8,128)(2,1)S(1)}, s32[2]{0:T(128)S(1)}, pred[16,16]{1,0:T(8,128)(4,1)S(1)}, s32[1024]{0:T(1024)S(1)}, /*ind...) while((s32[]{:T(128)}, ...), condition=%wide.region_8.8_spmd, body=%wide.region_5.7_spmd.sunk | while | flops 282148864 | bytes 10875095 | solution.py:80
  130.3 29.0 %while.46 = (s32[]{:T(128)}, bf16[2,512,128]{2,1,0:T(8,128)(2,1)S(1)}, s32[2]{0:T(128)S(1)}, pred[16,16]{1,0:T(8,128)(4,1)S(1)}, s32[1024]{0:T(1024)S(1)}, /*ind...) while((s32[]{:T(128)}, ...), condition=%wide.region_8.8_spmd, body=%wide.region_5.7_spmd.sunk | while | flops 282148864 | bytes 10875095 | solution.py:80
  163.0 29.0 %while.46 = (s32[]{:T(128)}, bf16[2,512,128]{2,1,0:T(8,128)(2,1)S(1)}, s32[2]{0:T(128)S(1)}, pred[16,16]{1,0:T(8,128)(4,1)S(1)}, s32[1024]{0:T(1024)S(1)}, /*ind...) while((s32[]{:T(128)}, ...), condition=%wide.region_8.8_spmd, body=%wide.region_5.7_spmd.sunk | while | flops 282148864 | bytes 10875095 | solution.py:80
  195.7 29.0 %while.46 = (s32[]{:T(128)}, bf16[2,512,128]{2,1,0:T(8,128)(2,1)S(1)}, s32[2]{0:T(128)S(1)}, pred[16,16]{1,0:T(8,128)(4,1)S(1)}, s32[1024]{0:T(1024)S(1)}, /*ind...) while((s32[]{:T(128)}, ...), condition=%wide.region_8.8_spmd, body=%wide.region_5.7_spmd.sunk | while | flops 282148864 | bytes 10875095 | solution.py:80
  228.4 29.0 %while.46 = (s32[]{:T(128)}, bf16[2,512,128]{2,1,0:T(8,128)(2,1)S(1)}, s32[2]{0:T(128)S(1)}, pred[16,16]{1,0:T(8,128)(4,1)S(1)}, s32[1024]{0:T(1024)S(1)}, /*ind...) while((s32[]{:T(128)}, ...), condition=%wide.region_8.8_spmd, body=%wide.region_5.7_spmd.sunk | while | flops 282148864 | bytes 10875095 | solution.py:80
  261.0 29.0 %while.46 = (s32[]{:T(128)}, bf16[2,512,128]{2,1,0:T(8,128)(2,1)S(1)}, s32[2]{0:T(128)S(1)}, pred[16,16]{1,0:T(8,128)(4,1)S(1)}, s32[1024]{0:T(1024)S(1)}, /*ind...) while((s32[]{:T(128)}, ...), condition=%wide.region_8.8_spmd, body=%wide.region_5.7_spmd.sunk | while | flops 282148864 | bytes 10875095 | solution.py:80
  293.7 29.0 %while.46 = (s32[]{:T(128)}, bf16[2,512,128]{2,1,0:T(8,128)(2,1)S(1)}, s32[2]{0:T(128)S(1)}, pred[16,16]{1,0:T(8,128)(4,1)S(1)}, s32[1024]{0:T(1024)S(1)}, /*ind...) while((s32[]{:T(128)}, ...), condition=%wide.region_8.8_spmd, body=%wide.region_5.7_spmd.sunk | while | flops 282148864 | bytes 10875095 | solution.py:80
  323.6 27.3 %fusion.21 = bf16[1024,8192]{1,0:T(8,128)(2,1)} fusion(bf16[1024,1024]{0,1:T(8,128)(2,1)} %bitcast.127, bf16[1,1024,8192]{2,1,0:T(8,128)(2,1)} %param.22), kind=kOutput, calls=%fused_computation.46 | convolution fusion | flops 17188257792 | bytes 35651584 | tf_op jit(solution)/shard_map/dot_general | solution.py:114
  350.9 90.8 %reduce-scatter.2.cloned.1.call-done = bf16[128,8192]{1,0:T(8,128)(2,1)} async-done(((bf16[1024,8192]{1,0:T(8,128)(2,1)}), bf16[128,8192]{1,0:T(8,128)(2,1)}) %reduce-scatter.2.cloned.1.call-update) | async-done | bytes 2097168 | tf_op jit(solution)/shard_map/reduce_scatter | solution.py:113
  441.7 197.4 %all-gather.3.cloned.1.call-done = bf16[2048,8192]{1,0:T(8,128)(2,1)} async-done(((bf16[128,8192]{1,0:T(8,128)(2,1)}), bf16[2048,8192]{1,0:T(8,128)(2,1)}) %all-gather.3.cloned.1.call-update) | async-done | bytes 33554448 | tf_op jit(solution)/shard_map/all_gather | solution.py:16
  641.7 80.1 %while.43 = (s32[]{:T(128)}, f32[128,8192]{1,0:T(8,128)}, s32[]{:T(128)}, bf16[16,128,8192]{2,1,0:T(8,128)(2,1)}, s32[]{:T(128)}, /*index=5*/s32[]{:T(128)}, s32[]{:T(128)}) while((s32[]{:T(128)}, f32[128,8192]{1,0:T(8,128)}, s32[]{:T(128)}, bf16[16,128,8192]{2,1,0:T(8,128)(2,1)}, s32[]{:T(128)}, /*index=5*/s32[]{:T(128)}, s32[]{:T(128)}) %tuple.95), condition=%wide.region_12.13_spmd, body=%wide.region_11.12_spmd.sunk | while | flops 2097157 | bytes 10485883 | solution.py:22
  641.7 5.5 convert_add_fusion.2
  647.1 5.3 convert_add_fusion.2
  652.5 5.3 convert_add_fusion.2
  657.8 5.3 convert_add_fusion.2
  663.1 5.3 convert_add_fusion.2
  668.5 5.3 convert_add_fusion.2
  673.8 5.3 convert_add_fusion.2
  679.1 5.3 convert_add_fusion.2
  684.5 5.3 convert_add_fusion.2
  689.8 5.3 convert_add_fusion.2
  695.1 5.3 convert_add_fusion.2
  700.5 5.3 convert_add_fusion.2
  705.8 5.3 convert_add_fusion.2
  711.1 5.3 convert_add_fusion.2
  716.5 5.3 convert_add_fusion.2
  (359 shorter events, 257.1 us)
Async XLA Ops:
  8.3 11.5 %all-to-all-start.1 = ((bf16[128,8,128]{2,0,1:T(8,128)(2,1)}), bf16[128,8,128]{2,0,1:T(8,128)(2,1)S(1)}, u32[]{:S(2)}, u32[]{:S(2)}) async-start(bf16[128,8,128]{2,0,1:T(8,128)(2,1)} %copy.60), calls=%async_computation.1 | async-start | bytes 524288 | tf_op jit(solution)/shard_map/all_to_all | solution.py:103
  19.4 5.0 copy-start.7
  19.4 5.2 copy-start.5
  19.4 5.2 copy-start.6
  19.4 5.4 copy-start.3
  19.7 30.9 %all-to-all-start = ((bf16[128,64,128]{2,0,1:T(8,128)(2,1)}), bf16[128,64,128]{2,0,1:T(8,128)(2,1)S(1)}, u32[]{:S(2)}, u32[]{:S(2)}) async-start(bf16[128,64,128]{2,0,1:T(8,128)(2,1)} %copy.57), calls=%async_computation | async-start | bytes 4194304 | tf_op jit(solution)/shard_map/all_to_all | solution.py:102
  50.7 11.4 %all-to-all-start.2 = ((bf16[128,8,128]{2,0,1:T(8,128)(2,1)}), bf16[128,8,128]{2,0,1:T(8,128)(2,1)}, u32[]{:S(2)}, u32[]{:S(2)}) async-start(bf16[128,8,128]{2,0,1:T(8,128)(2,1)} %copy.62), calls=%async_computation.2 | async-start | bytes 524288 | tf_op jit(solution)/shard_map/all_to_all | solution.py:104
  55.5 386.3 %reduce-scatter.2.cloned.1.call-start = ((), (), s32[]{:S(2)}) async-start(), calls=%async_computation.4 | async-start | bytes 18874368 | tf_op jit(solution)/shard_map/reduce_scatter | solution.py:113
  350.9 288.3 %all-gather.3.cloned.1.call-start = ((), (), s32[]{:S(2)}) async-start(), calls=%async_computation.5 | async-start | bytes 35651584 | tf_op jit(solution)/shard_map/all_gather | solution.py:16
  641.7 80.2 %copy-start.1 = (bf16[128,8192]{1,0:T(8,128)(2,1)S(1)}, bf16[128,8192]{1,0:T(8,128)(2,1)}, u32[]{:S(2)}) copy-start(bf16[128,8192]{1,0:T(8,128)(2,1)} %reduce-scatter.2.cloned.1.call-done) | copy-start | bytes 6291460
  721.8 4.1 copy-start
  721.8 4.7 copy-start.2
  721.8 4.7 copy-start.4
Sparse Core Ops, SparseCore 0:
  351.0 90.6 reduce-scatter.1
  443.8 195.2 all-gather.2
where the time goes:
time: 737 us; the launch traced here: 736 us
  waiting for transfers between devices  318 us (43%)
  local copies, waits for them, and re-layouts  168 us (23%)
  other arithmetic  107 us (15%)
  matrix products  84 us (11%)
  loops' own time  30 us (4%)
  starting transfers between devices  14.4 us (2%)
  between operations  13.5 us (2%)
    all_gather x1, waiting for transfers between devices, entering(): gathered = lax.all_gather(value.astype(jnp.bfloat16), axis)  197 us
    gather x64, local copies, waits for them, and re-layouts, one_rows(): allowed = mask_head[query_pos // BLOCK][:, tok_block]  94.7 us
    reduce_scatter x1, waiting for transfers between devices, local(): lax.psum_scatter(jnp.dot(context, weight_rows, preferred_element_type=jnp...  90.8 us
    add x15, other arithmetic, one(): join(state, lax.dynamic_index_in_dim(gathered, step, 0, False).astype(val...  80.1 us
    dot_general x16, matrix products, one_rows(): jnp.dot(weights, value_head, preferred_element_type=jnp.float32)  40.9 us
    gather x16, local copies, waits for them, and re-layouts, one_rows(): allowed = allowed & (doc_ids[query_pos][:, None] == doc_ids[None, :])  36.6 us
    dot_general x1, matrix products, local(): jnp.dot(context, weight_rows, preferred_element_type=jnp.float32)  27.3 us
    all_to_all x1, waiting for transfers between devices, local(): lax.all_to_all(query_rows, 'seq', split_axis=1, concat_axis=0, tiled=True)  24.8 us
  transfers between devices with their start and end apart: 5, of which 5 were waited for; matrix products, arithmetic and copies ran while one was open for 1% of the time, Pallas kernels for 0%

commit v1 on v0

v1 whole, which is shorter than its diff:
```python
import functools
import math

import jax
import jax.numpy as jnp
from jax import lax
from jax.experimental import pallas as pl
from jax.experimental.pallas import tpu as pltpu
from jax.sharding import PartitionSpec as P

QUERY_HEADS = 64
KEY_VALUE_HEADS = 8
HEAD_SIZE = 128
BLOCK = 64
LONGEST_PROMPT = 512
CHUNKS = (64, 32, 32)
NEG = -1e30


def attention_kernel(first_row, order_ref, lengths_ref, vert_ref, slash_ref, q_ref, kv_ref, out_ref):
    rows = q_ref.shape[1]
    parts, part_rows = kv_ref.shape[0], kv_ref.shape[1]
    heads = q_ref.shape[2] // HEAD_SIZE
    keys = min(LONGEST_PROMPT + part_rows, parts * part_rows)
    factor = math.log2(math.e) / math.sqrt(HEAD_SIZE)
    part = order_ref[pl.program_id(0)]
    begin_part = jnp.clip(part - LONGEST_PROMPT // part_rows, 0, parts - keys // part_rows)
    begin = begin_part * part_rows
    query_first = part * part_rows + first_row
    query_pos = query_first + lax.broadcasted_iota(jnp.int32, (rows, 1), 0)
    own_start = jnp.zeros_like(query_pos)
    start = 0
    for p in range(lengths_ref.shape[0] - 1):
        start = start + lengths_ref[p]
        own_start = jnp.where(query_pos >= start, start, own_start)
    key_pos = begin + lax.broadcasted_iota(jnp.int32, (rows, keys), 1)
    token_bias = jnp.where((key_pos <= query_pos) & (key_pos >= own_start), 0.0, NEG)
    key_block = lax.shift_right_logical(
        begin + lax.broadcasted_iota(jnp.int32, (heads, keys), 1), int(math.log2(BLOCK))
    )
    offset = lax.shift_right_logical(query_first, int(math.log2(BLOCK))) - key_block
    hit = key_block == vert_ref[:, 0:1]
    for n in range(1, vert_ref.shape[1]):
        hit = hit | (key_block == vert_ref[:, n : n + 1])
    for n in range(slash_ref.shape[1]):
        hit = hit | (offset == slash_ref[:, n : n + 1])
    head_bias = jnp.where(hit, 0.0, NEG)
    key_value = kv_ref[pl.ds(begin_part, keys // part_rows)].reshape(keys, 2 * HEAD_SIZE)
    query = jnp.concatenate(
        [q_ref[0, :, h * HEAD_SIZE : (h + 1) * HEAD_SIZE] for h in range(heads)], axis=0
    )
    scores = lax.dot_general(
        query,
        key_value[:, :HEAD_SIZE],
        (((1,), (1,)), ((), ())),
        preferred_element_type=jnp.float32,
    )
    scores = scores.reshape(heads, rows, keys) + (token_bias[None] + head_bias[:, None, :])
    largest = jnp.max(scores, axis=-1, keepdims=True)
    weights = jnp.exp2((scores - largest) * factor)
    norm = jnp.sum(weights, axis=-1, keepdims=True)
    context = jnp.dot(
        weights.astype(jnp.bfloat16).reshape(heads * rows, keys),
        key_value[:, HEAD_SIZE:],
        preferred_element_type=jnp.float32,
    )
    context = (context.reshape(heads, rows, HEAD_SIZE) / norm).astype(jnp.bfloat16)
    for h in range(heads):
        out_ref[0, :, h * HEAD_SIZE : (h + 1) * HEAD_SIZE] = context[h]


def attention(first_row, rows, order, lengths, vert, slash, exchanged):
    parts, part_rows, width = exchanged.shape
    query_width = width - 2 * HEAD_SIZE
    return pl.pallas_call(
        functools.partial(attention_kernel, first_row),
        out_shape=jax.ShapeDtypeStruct((parts, rows, query_width), jnp.bfloat16),
        grid_spec=pltpu.PrefetchScalarGridSpec(
            num_scalar_prefetch=2,
            grid=(parts,),
            in_specs=[
                pl.BlockSpec(vert.shape, lambda n, order, lengths: (0, 0)),
                pl.BlockSpec(slash.shape, lambda n, order, lengths: (0, 0)),
                pl.BlockSpec(
                    (1, rows, query_width),
                    lambda n, order, lengths: (order[n], first_row // rows, 0),
                ),
                pl.BlockSpec(
                    (parts, part_rows, 2 * HEAD_SIZE),
                    lambda n, order, lengths: (0, 0, query_width // (2 * HEAD_SIZE)),
                ),
            ],
            out_specs=pl.BlockSpec(
                (1, rows, query_width), lambda n, order, lengths: (n, 0, 0)
            ),
        ),
        compiler_params=pltpu.CompilerParams(vmem_limit_bytes=32 << 20),
        name="attention",
    )(order, lengths, vert, slash, exchanged, exchanged)


def prefix_kernel(term_ref, out_ref):
    total = term_ref[0].astype(jnp.float32)
    out_ref[0] = term_ref[0]
    for layer in range(1, term_ref.shape[0]):
        total = total + term_ref[layer].astype(jnp.float32)
        out_ref[layer] = total.astype(jnp.bfloat16)


def prefix(terms):
    vmem = pl.BlockSpec(memory_space=pltpu.VMEM)
    return pl.pallas_call(
        prefix_kernel,
        out_shape=jax.ShapeDtypeStruct(terms.shape, jnp.bfloat16),
        in_specs=[vmem],
        out_specs=vmem,
        compiler_params=pltpu.CompilerParams(vmem_limit_bytes=32 << 20),
        name="prefix",
    )(terms)


def norm_kernel(residual_ref, sums_ref, gain_ref, out_ref):
    pieces, rows, width = sums_ref.shape
    square = jnp.zeros((rows, 1), jnp.float32)
    for n in range(pieces):
        stream = residual_ref[:, n * width : (n + 1) * width].astype(jnp.float32)
        stream = stream + sums_ref[n].astype(jnp.float32)
        square = square + jnp.sum(stream * stream, axis=-1, keepdims=True)
    inverse = lax.rsqrt(square / (pieces * width) + 1e-06)
    for n in range(pieces):
        place = slice(n * width, (n + 1) * width)
        stream = residual_ref[:, place].astype(jnp.float32) + sums_ref[n].astype(jnp.float32)
        out_ref[:, place] = (stream * inverse * gain_ref[:, place]).astype(jnp.bfloat16)


def normalize(residual, sums, gain):
    vmem = pl.BlockSpec(memory_space=pltpu.VMEM)
    return pl.pallas_call(
        norm_kernel,
        out_shape=jax.ShapeDtypeStruct(residual.shape, jnp.bfloat16),
        in_specs=[vmem, vmem, vmem],
        out_specs=vmem,
        compiler_params=pltpu.CompilerParams(vmem_limit_bytes=32 << 20),
        name="normalize",
    )(residual, sums, gain)


def add(first, second):
    return (first.astype(jnp.float32) + second.astype(jnp.float32)).astype(jnp.bfloat16)


def exchange_pairs(chips):
    def near(chip):
        return chip ^ 1

    def far(chip):
        return chips - 1 - chip

    cores = [(2 * x + c, 2 * x + 1 - c) for x in range(chips) for c in range(2)]
    first = [(2 * x + c, 2 * (near(x) if c == 0 else far(x)) + c) for x in range(chips) for c in range(2)]
    second = [(2 * x + c, 2 * (far(x) if c == 0 else near(x)) + c) for x in range(chips) for c in range(2)]
    return cores, first, second


def local(
    queries,
    layer_key_rows,
    layer_value_rows,
    vertical_blocks,
    slash_offsets,
    prompt_lengths,
    residual,
    out_weight,
    section_gain,
):
    parts = lax.axis_size("seq")
    layers = lax.axis_size("pipe")
    chips = parts // 2
    model = queries.shape[2]
    heads_here = QUERY_HEADS // parts
    place = lax.axis_index("seq")
    vert = lax.dynamic_slice_in_dim(vertical_blocks[0], place * heads_here, heads_here, 0)
    slash = lax.dynamic_slice_in_dim(slash_offsets[0], place * heads_here, heads_here, 0)

    def by_head(rows_in):
        return rows_in.reshape(rows_in.shape[0], parts, -1).transpose(1, 0, 2)

    exchanged = jnp.concatenate(
        [by_head(queries[0]), by_head(layer_key_rows[0]), by_head(layer_value_rows[0])], axis=2
    )
    exchanged = lax.all_to_all(exchanged, "seq", 0, 0)

    chip, core = place // 2, place % 2
    near, far = chip ^ 1, chips - 1 - chip
    first_chip = jnp.where(core == 0, near, far)
    second_chip = jnp.where(core == 0, far, near)
    across = chips - 1 - near
    order = jnp.stack(
        [
            2 * chip + 1 - core,
            2 * first_chip + 1 - core,
            2 * second_chip + 1 - core,
            2 * across + 1 - core,
            2 * chip + core,
            2 * second_chip + core,
            2 * first_chip + core,
            2 * across + core,
        ]
    ).astype(jnp.int32)
    to_core, to_first, to_second = exchange_pairs(chips)

    outs = []
    first = 0
    for chunk in CHUNKS:
        context = attention(first, chunk, order, prompt_lengths, vert, slash, exchanged)
        context = context.reshape(2, chips * chunk, model // parts)

        def project(rows_in):
            return jnp.dot(
                rows_in, out_weight[0], preferred_element_type=jnp.float32
            ).astype(jnp.bfloat16)

        arrived = lax.ppermute(project(context[0]), "seq", to_core)
        kept = project(context[1])
        half = chips * chunk // 2
        arrived_first = lax.ppermute(add(kept[half:], arrived[half:]), "seq", to_first)
        kept = add(kept[:half], arrived[:half])
        quarter = half // 2
        arrived_second = lax.ppermute(
            add(kept[quarter:], arrived_first[quarter:]), "seq", to_second
        )
        term = add(add(kept[:quarter], arrived_first[:quarter]), arrived_second)
        term = term.reshape(chunk, layers, model // layers).transpose(1, 0, 2)
        sums = prefix(lax.all_to_all(term, "pipe", 0, 0))
        sums = lax.all_to_all(sums, "pipe", 0, 0)
        outs.append(normalize(residual[first : first + chunk], sums, section_gain))
        first += chunk
    return jnp.concatenate(outs, axis=0)[None]


def solution(mesh):
    placed = (
        P("pipe", "seq", None),
        P("pipe", "seq", None),
        P("pipe", "seq", None),
        P("pipe", None, None),
        P("pipe", None, None),
        P(),
        P("seq", None),
        P("pipe", "seq", None),
        P("pipe", None),
    )
    return jax.shard_map(
        local, mesh=mesh, in_specs=placed, out_specs=P("pipe", "seq", None), check_vma=False
    )
```

time: 737 us -> 256 us (0.35)
  the two profiles are of different devices: /device:TPU:121 before, /device:TPU:2 now
where the time goes in v1:
time: 256 us; the launch traced here: 255 us
  waiting for transfers between devices  125 us (49%)
  starting transfers between devices  42 us (16%)
  matrix products  30.5 us (12%)
  Pallas kernels  24.5 us (10%)
  other arithmetic  17.2 us (7%)
  local copies, waits for them, and re-layouts  15.8 us (6%)
    ppermute x3, waiting for transfers between devices, local(): lax.ppermute(add(kept[half:], arrived[half:]), 'seq', to_first)  39.6 us
    all_to_all x1, waiting for transfers between devices, local(): exchanged = lax.all_to_all(exchanged, 'seq', 0, 0)  31 us
    dot_general x6, matrix products, project(): jnp.dot(rows_in, out_weight[0], preferred_element_type=jnp.float32)  30.5 us
    all_to_all x3, waiting for transfers between devices, local(): sums = lax.all_to_all(sums, 'pipe', 0, 0)  27.5 us
    all_to_all x3, waiting for transfers between devices, local(): sums = prefix(lax.all_to_all(term, 'pipe', 0, 0))  26.5 us
    pallas_call x3, Pallas kernels, attention(): pl.pallas_call(functools.partial(attention_kernel, first_row), out_shape=...  20.1 us
    all_to_all x3, starting transfers between devices, local(): sums = prefix(lax.all_to_all(term, 'pipe', 0, 0))  19.8 us
    convert_element_type x9, other arithmetic, add(): (first.astype(jnp.float32) + second.astype(jnp.float32)).astype(jnp.bfloa...  14 us
  transfers between devices with their start and end apart: 16, of which 9 were waited for; matrix products, arithmetic and copies ran while one was open for 16% of the time, Pallas kernels for 7%

profile of v1, /device:TPU:2, one launch (start us, length us, event | category | flops | bytes accessed | tf_op | source)
XLA Modules:
  0.0 255.2 jit_solution(16479804861068725076)
XLA Ops:
  2.8 2.4 copy.16
  5.2 2.9 %copy.17 = bf16[128,8,1024]{2,0,1:T(8,128)(2,1)S(1)} copy(bf16[128,8,1024]{0,2,1:T(8,128)(2,1)} %bitcast.81) | data formatting | bytes 4194304 | tf_op jit(solution)/shard_map/reshape;squeeze | solution.py:186
  9.9 5.0 %all-to-all-start = ((bf16[8,128,1280]{2,1,0:T(8,128)(2,1)}), bf16[8,128,1280]{2,1,0:T(8,128)(2,1)S(1)}, u32[]{:S(2)}, u32[]{:S(2)}) async-start(bf16[8,128,1280]{2,1,0:T(8,128)(2,1)} %pad_maximum_fusion), calls=%async_computation | async-start | bytes 5242880 | tf_op jit(solution)/shard_map/all_to_all | solution.py:191
  15.2 31.0 %all-to-all-done.q_ref.kv_ref = bf16[8,128,1280]{2,1,0:T(8,128)(2,1)S(1)} async-done(((bf16[8,128,1280]{2,1,0:T(8,128)(2,1)}), bf16[8,128,1280]{2,1,0:T(8,128)(2,1)S(1)}, u32[]{:S(2)}, u32[]{:S(2)}) %all-to-all-start) | async-done | bytes 2621472 | tf_op jit(solution)/shard_map/all_to_all | solution.py:191
  46.2 5.8 %attention.5 = bf16[8,32,1024]{2,1,0:T(8,128)(2,1)S(1)} custom-call(s32[8]{0:T(128)S(1)} %stack.35.order_ref, s32[4]{0:T(128)S(1)} %copy-done.5, s32[8,4]{1,0:T(8,128)S(1)} %copy.22.vert_ref, s32[8,4]{1,0:T(8,128)S(1)} %copy.23.slash_ref, bf16[8,128,1280]{2,1,0:T(8,128)(2,1)S(1)} %all-to-all-done.q_ref.kv_ref, ...), custom_call_target="tpu_custom_call" | custom-call | tf_op jit(solution)/shard_map/attention/pallas_call | solution.py:75
  52.1 9.6 %fusion.27 = bf16[128,8192]{1,0:T(8,128)(2,1)} fusion(bf16[128,1024]{1,0:T(8,128)(2,1)S(1)} %bitcast.88, bf16[1,1024,8192]{2,1,0:T(8,128)(2,1)} %param.16), kind=kOutput, calls=%fused_computation.17 | convolution fusion | flops 2148532224 | bytes 19136512 | tf_op jit(solution)/shard_map/dot_general | solution.py:219
  61.7 5.8 %attention.4 = bf16[8,32,1024]{2,1,0:T(8,128)(2,1)S(1)} custom-call(s32[8]{0:T(128)S(1)} %stack.35.order_ref, s32[4]{0:T(128)S(1)} %copy-done.5, s32[8,4]{1,0:T(8,128)S(1)} %copy.22.vert_ref, s32[8,4]{1,0:T(8,128)S(1)} %copy.23.slash_ref, bf16[8,128,1280]{2,1,0:T(8,128)(2,1)S(1)} %all-to-all-done.q_ref.kv_ref, ...), custom_call_target="tpu_custom_call" | custom-call | tf_op jit(solution)/shard_map/attention/pallas_call | solution.py:75
  67.6 3.7 %fusion.21 = bf16[128,8192]{1,0:T(8,128)(2,1)} fusion(bf16[128,1024]{1,0:T(8,128)(2,1)S(1)} %bitcast.89, bf16[1,1024,8192]{2,1,0:T(8,128)(2,1)S(1)} %bitcast.79), kind=kOutput, calls=%fused_computation.15 | convolution fusion | flops 2148532224 | bytes 19136512 | tf_op jit(solution)/shard_map/dot_general | solution.py:219
  71.8 8.5 %attention.3 = bf16[8,64,1024]{2,1,0:T(8,128)(2,1)S(1)} custom-call(s32[8]{0:T(128)S(1)} %stack.35.order_ref, s32[4]{0:T(128)S(1)} %copy-done.5, s32[8,4]{1,0:T(8,128)S(1)} %copy.22.vert_ref, s32[8,4]{1,0:T(8,128)S(1)} %copy.23.slash_ref, bf16[8,128,1280]{2,1,0:T(8,128)(2,1)S(1)} %all-to-all-done.q_ref.kv_ref, ...), custom_call_target="tpu_custom_call" | custom-call | tf_op jit(solution)/shard_map/attention/pallas_call | solution.py:75
  80.5 6.2 %fusion.15 = bf16[256,8192]{1,0:T(8,128)(2,1)} fusion(bf16[256,1024]{1,0:T(8,128)(2,1)S(1)} %bitcast.95, bf16[1,1024,8192]{2,1,0:T(8,128)(2,1)S(1)} %bitcast.79), kind=kOutput, calls=%fused_computation.13 | convolution fusion | flops 4297064448 | bytes 21495808 | tf_op jit(solution)/shard_map/dot_general | solution.py:219
  86.6 6.2 %fusion.12 = bf16[256,8192]{1,0:T(8,128)(2,1)} fusion(bf16[256,1024]{1,0:T(8,128)(2,1)S(1)} %bitcast.94, bf16[1,1024,8192]{2,1,0:T(8,128)(2,1)S(1)} %bitcast.79), kind=kOutput, calls=%fused_computation.12 | convolution fusion | flops 4297064448 | bytes 21495808 | tf_op jit(solution)/shard_map/dot_general | solution.py:219
  92.9 2.4 fusion.24
  95.3 2.4 fusion.18
  97.7 2.1 add_convert_fusion.3
  101.3 2.2 add_convert_fusion.5
  104.2 10.5 %collective-permute-done.7 = bf16[64,8192]{1,0:T(8,128)(2,1)S(1)} collective-permute-done((bf16[64,8192]{1,0:T(8,128)(2,1)S(1)}, bf16[64,8192]{1,0:T(8,128)(2,1)S(1)}, u32[]{:S(2)}, u32[]{:S(2)}) %collective-permute-start.7) | collective-permute-done | bytes 1048608 | tf_op jit(solution)/shard_map/ppermute | solution.py:226
  114.9 3.7 %add_convert_fusion.1 = (bf16[128,8192]{1,0:T(8,128)(2,1)S(1)}, bf16[128,8192]{1,0:T(8,128)(2,1)}) fusion(bf16[256,8192]{1,0:T(8,128)(2,1)} %collective-permute-done, bf16[256,8192]{1,0:T(8,128)(2,1)S(1)} %copy-done.6), kind=kLoop, calls=%fused_computation.19 | loop fusion | flops 8388608 | bytes 12582912 | tf_op jit(solution)/shard_map/convert_element_type | solution.py:149
  118.6 2.6 %collective-permute-start.1 = (bf16[128,8192]{1,0:T(8,128)(2,1)}, bf16[128,8192]{1,0:T(8,128)(2,1)}, u32[]{:S(2)}, u32[]{:S(2)}) collective-permute-start(bf16[128,8192]{1,0:T(8,128)(2,1)} %get-tuple-element.6), channel_id=1, source_target_pairs={{0,32},{16,112},{32,0},{48,80},{64,96},{80,48},{96,64},{112,16},{1... | collective-permute-start | bytes 6291464 | tf_op jit(solution)/shard_map/ppermute | solution.py:226
  121.2 10.3 %collective-permute-done.4 = bf16[64,8192]{1,0:T(8,128)(2,1)S(1)} collective-permute-done((bf16[64,8192]{1,0:T(8,128)(2,1)S(1)}, bf16[64,8192]{1,0:T(8,128)(2,1)S(1)}, u32[]{:S(2)}, u32[]{:S(2)}) %collective-permute-start.4) | collective-permute-done | bytes 1048608 | tf_op jit(solution)/shard_map/ppermute | solution.py:226
  132.8 8.0 %all-to-all-start.5 = ((bf16[16,32,512]{2,1,0:T(8,128)(2,1)}), bf16[16,32,512]{2,1,0:T(8,128)(2,1)S(1)}, u32[]{:S(2)}, u32[]{:S(2)}) async-start(bf16[16,32,512]{2,1,0:T(8,128)(2,1)} %bitcast.75), calls=%async_computation.5 | async-start | bytes 1048576 | tf_op jit(solution)/shard_map/all_to_all | solution.py:234
  140.9 18.8 %collective-permute-done.1 = bf16[128,8192]{1,0:T(8,128)(2,1)} collective-permute-done((bf16[128,8192]{1,0:T(8,128)(2,1)}, bf16[128,8192]{1,0:T(8,128)(2,1)}, u32[]{:S(2)}, u32[]{:S(2)}) %collective-permute-start.1) | collective-permute-done | bytes 2097184 | tf_op jit(solution)/shard_map/ppermute | solution.py:226
  159.7 2.4 add_convert_fusion.7
  164.3 8.0 %all-to-all-start.3 = ((bf16[16,32,512]{2,1,0:T(8,128)(2,1)}), bf16[16,32,512]{2,1,0:T(8,128)(2,1)S(1)}, u32[]{:S(2)}, u32[]{:S(2)}) async-start(bf16[16,32,512]{2,1,0:T(8,128)(2,1)} %bitcast.83), calls=%async_computation.3 | async-start | bytes 1048576 | tf_op jit(solution)/shard_map/all_to_all | solution.py:234
  173.2 10.7 %all-to-all-done.3.term_ref = bf16[16,32,512]{2,1,0:T(8,128)(2,1)S(1)} async-done(((bf16[16,32,512]{2,1,0:T(8,128)(2,1)}), bf16[16,32,512]{2,1,0:T(8,128)(2,1)S(1)}, u32[]{:S(2)}, u32[]{:S(2)}) %all-to-all-start.3) | async-done | bytes 524320 | tf_op jit(solution)/shard_map/all_to_all | solution.py:234
  183.9 4.5 %all-to-all-start.6 = ((bf16[16,32,512]{2,1,0:T(8,128)(2,1)}), bf16[16,32,512]{2,1,0:T(8,128)(2,1)S(1)}, u32[]{:S(2)}, u32[]{:S(2)}) async-start(bf16[16,32,512]{2,1,0:T(8,128)(2,1)} %prefix.5), calls=%async_computation.6 | async-start | bytes 1048576 | tf_op jit(solution)/shard_map/all_to_all | solution.py:235
  191.5 9.1 %all-to-all-done.6.sums_ref = bf16[16,32,512]{2,1,0:T(8,128)(2,1)S(1)} async-done(((bf16[16,32,512]{2,1,0:T(8,128)(2,1)}), bf16[16,32,512]{2,1,0:T(8,128)(2,1)S(1)}, u32[]{:S(2)}, u32[]{:S(2)}) %all-to-all-start.6) | async-done | bytes 524320 | tf_op jit(solution)/shard_map/all_to_all | solution.py:235
  200.5 3.7 %all-to-all-start.1 = ((bf16[16,64,512]{2,1,0:T(8,128)(2,1)}), bf16[16,64,512]{2,1,0:T(8,128)(2,1)S(1)}, u32[]{:S(2)}, u32[]{:S(2)}) async-start(bf16[16,64,512]{2,1,0:T(8,128)(2,1)} %bitcast.73), calls=%async_computation.1 | async-start | bytes 2097152 | tf_op jit(solution)/shard_map/all_to_all | solution.py:234
  205.1 15.8 %all-to-all-done.1.term_ref = bf16[16,64,512]{2,1,0:T(8,128)(2,1)S(1)} async-done(((bf16[16,64,512]{2,1,0:T(8,128)(2,1)}), bf16[16,64,512]{2,1,0:T(8,128)(2,1)S(1)}, u32[]{:S(2)}, u32[]{:S(2)}) %all-to-all-start.1) | async-done | bytes 1048608 | tf_op jit(solution)/shard_map/all_to_all | solution.py:234
  220.9 3.6 %all-to-all-start.4 = ((bf16[16,32,512]{2,1,0:T(8,128)(2,1)}), bf16[16,32,512]{2,1,0:T(8,128)(2,1)S(1)}, u32[]{:S(2)}, u32[]{:S(2)}) async-start(bf16[16,32,512]{2,1,0:T(8,128)(2,1)} %prefix.4), calls=%async_computation.4 | async-start | bytes 1048576 | tf_op jit(solution)/shard_map/all_to_all | solution.py:235
  226.9 7.6 %all-to-all-done.4.sums_ref = bf16[16,32,512]{2,1,0:T(8,128)(2,1)S(1)} async-done(((bf16[16,32,512]{2,1,0:T(8,128)(2,1)}), bf16[16,32,512]{2,1,0:T(8,128)(2,1)S(1)}, u32[]{:S(2)}, u32[]{:S(2)}) %all-to-all-start.4) | async-done | bytes 524320 | tf_op jit(solution)/shard_map/all_to_all | solution.py:235
  234.6 3.7 %all-to-all-start.2 = ((bf16[16,64,512]{2,1,0:T(8,128)(2,1)}), bf16[16,64,512]{2,1,0:T(8,128)(2,1)S(1)}, u32[]{:S(2)}, u32[]{:S(2)}) async-start(bf16[16,64,512]{2,1,0:T(8,128)(2,1)} %prefix.3), calls=%async_computation.2 | async-start | bytes 2097152 | tf_op jit(solution)/shard_map/all_to_all | solution.py:235
  241.9 10.8 %all-to-all-done.2.sums_ref = bf16[16,64,512]{2,1,0:T(8,128)(2,1)S(1)} async-done(((bf16[16,64,512]{2,1,0:T(8,128)(2,1)}), bf16[16,64,512]{2,1,0:T(8,128)(2,1)S(1)}, u32[]{:S(2)}, u32[]{:S(2)}) %all-to-all-start.2) | async-done | bytes 1048608 | tf_op jit(solution)/shard_map/all_to_all | solution.py:235
  (81 shorter events, 24.7 us)
Async XLA Ops:
  0.0 2.8 %copy-start.9 = (bf16[1,128,8192]{2,1,0:T(8,128)(2,1)S(1)}, bf16[1,128,8192]{2,1,0:T(8,128)(2,1)}, u32[]{:S(2)}) copy-start(bf16[1,128,8192]{2,1,0:T(8,128)(2,1)} %param.9) | copy-start | bytes 6291460
  9.9 5.0 %copy-start.12 = (s32[1,64,4]{1,2,0:T(4,128)S(1)}, s32[1,64,4]{1,2,0:T(4,128)}, u32[]{:S(2)}) copy-start(s32[1,64,4]{1,2,0:T(4,128)} %param.13) | copy-start | bytes 3076
  9.9 5.0 %copy-start.13 = (s32[1,64,4]{1,2,0:T(4,128)S(1)}, s32[1,64,4]{1,2,0:T(4,128)}, u32[]{:S(2)}) copy-start(s32[1,64,4]{1,2,0:T(4,128)} %param.12) | copy-start | bytes 3076
  9.9 36.3 %copy-start.5 = (s32[4]{0:T(128)S(1)}, s32[4]{0:T(128)}, u32[]{:S(2)}) copy-start(s32[4]{0:T(128)} %lengths_ref.5) | copy-start | bytes 52
  9.9 36.3 %all-to-all-start = ((bf16[8,128,1280]{2,1,0:T(8,128)(2,1)}), bf16[8,128,1280]{2,1,0:T(8,128)(2,1)S(1)}, u32[]{:S(2)}, u32[]{:S(2)}) async-start(bf16[8,128,1280]{2,1,0:T(8,128)(2,1)} %pad_maximum_fusion), calls=%async_computation | async-start | bytes 5242880 | tf_op jit(solution)/shard_map/all_to_all | solution.py:191
  46.2 21.4 %slice-start = ((s8[16777216]{0:T(1024)(128)(4,1)}), s8[4194304]{0:T(1024)(128)(4,1)S(1)}, s32[]{:S(2)}) async-start(s8[16777216]{0:T(1024)(128)(4,1)} %bitcast.78), calls=%async_computation.7 | async-start | bytes 8388608
  52.1 15.5 %slice-start.1 = ((s8[16777216]{0:T(1024)(128)(4,1)}), s8[4194304]{0:T(1024)(128)(4,1)S(1)}, s32[]{:S(2)}) async-start(s8[16777216]{0:T(1024)(128)(4,1)} %bitcast.78), calls=%async_computation.8 | async-start | bytes 8388608
  52.1 15.5 %slice-start.2 = ((s8[16777216]{0:T(1024)(128)(4,1)}), s8[4194304]{0:T(1024)(128)(4,1)S(1)}, s32[]{:S(2)}) async-start(s8[16777216]{0:T(1024)(128)(4,1)} %bitcast.78), calls=%async_computation.9 | async-start | bytes 8388608
  52.1 15.5 %slice-start.3 = ((s8[16777216]{0:T(1024)(128)(4,1)}), s8[4194304]{0:T(1024)(128)(4,1)S(1)}, s32[]{:S(2)}) async-start(s8[16777216]{0:T(1024)(128)(4,1)} %bitcast.78), calls=%async_computation.10 | async-start | bytes 8388608
  61.7 36.0 %collective-permute-start.6 = (bf16[128,8192]{1,0:T(8,128)(2,1)}, bf16[128,8192]{1,0:T(8,128)(2,1)}, u32[]{:S(2)}, u32[]{:S(2)}) collective-permute-start(bf16[128,8192]{1,0:T(8,128)(2,1)} %fusion.27), channel_id=1, source_target_pairs={{0,16},{16,0},{32,48},{48,32},{64,80},{80,64},{96,112},{112,96},{1... | collective-permute-start | bytes 6291464 | tf_op jit(solution)/shard_map/ppermute | solution.py:223
  71.3 30.0 %collective-permute-start.3 = (bf16[128,8192]{1,0:T(8,128)(2,1)}, bf16[128,8192]{1,0:T(8,128)(2,1)}, u32[]{:S(2)}, u32[]{:S(2)}) collective-permute-start(bf16[128,8192]{1,0:T(8,128)(2,1)} %fusion.21), channel_id=1, source_target_pairs={{0,16},{16,0},{32,48},{48,32},{64,80},{80,64},{96,112},{112,96},{1... | collective-permute-start | bytes 6291464 | tf_op jit(solution)/shard_map/ppermute | solution.py:223
  86.6 28.2 %collective-permute-start = (bf16[256,8192]{1,0:T(8,128)(2,1)}, bf16[256,8192]{1,0:T(8,128)(2,1)}, u32[]{:S(2)}, u32[]{:S(2)}) collective-permute-start(bf16[256,8192]{1,0:T(8,128)(2,1)} %fusion.15), channel_id=1, source_target_pairs={{0,16},{16,0},{32,48},{48,32},{64,80},{80,64},{96,112},{112,96},{1... | collective-permute-start | bytes 12582920 | tf_op jit(solution)/shard_map/ppermute | solution.py:223
  99.8 14.9 %collective-permute-start.7 = (bf16[64,8192]{1,0:T(8,128)(2,1)S(1)}, bf16[64,8192]{1,0:T(8,128)(2,1)S(1)}, u32[]{:S(2)}, u32[]{:S(2)}) collective-permute-start(bf16[64,8192]{1,0:T(8,128)(2,1)S(1)} %get-tuple-element.10), channel_id=1, source_target_pairs={{0,32},{16,112},{32,0},{48,80},{64,96},{80,48},{96,64},{112,16},{1... | collective-permute-start | bytes 3145736 | tf_op jit(solution)/shard_map/ppermute | solution.py:226
  101.3 13.6 %copy-start.6 = (bf16[256,8192]{1,0:T(8,128)(2,1)S(1)}, bf16[256,8192]{1,0:T(8,128)(2,1)}, u32[]{:S(2)}) copy-start(bf16[256,8192]{1,0:T(8,128)(2,1)} %fusion.12) | copy-start | bytes 12582916
  103.5 28.0 %copy-start.7 = (bf16[64,8192]{1,0:T(8,128)(2,1)}, bf16[64,8192]{1,0:T(8,128)(2,1)S(1)}, u32[]{:S(2)}) copy-start(bf16[64,8192]{1,0:T(8,128)(2,1)S(1)} %get-tuple-element.7) | copy-start | bytes 3145732
  103.5 28.0 %collective-permute-start.4 = (bf16[64,8192]{1,0:T(8,128)(2,1)S(1)}, bf16[64,8192]{1,0:T(8,128)(2,1)S(1)}, u32[]{:S(2)}, u32[]{:S(2)}) collective-permute-start(bf16[64,8192]{1,0:T(8,128)(2,1)S(1)} %get-tuple-element.8), channel_id=1, source_target_pairs={{0,32},{16,112},{32,0},{48,80},{64,96},{80,48},{96,64},{112,16},{1... | collective-permute-start | bytes 3145736 | tf_op jit(solution)/shard_map/ppermute | solution.py:226
  114.8 17.0 %collective-permute-start.8 = (bf16[32,8192]{1,0:T(8,128)(2,1)S(1)}, bf16[32,8192]{1,0:T(8,128)(2,1)S(1)}, u32[]{:S(2)}, u32[]{:S(2)}) collective-permute-start(bf16[32,8192]{1,0:T(8,128)(2,1)S(1)} %add_convert_fusion.10), channel_id=1, source_target_pairs={{0,96},{16,48},{32,64},{48,16},{64,32},{80,112},{96,0},{112,80},{1... | collective-permute-start | bytes 1572872 | tf_op jit(solution)/shard_map/ppermute | solution.py:229
  118.6 41.1 %collective-permute-start.1 = (bf16[128,8192]{1,0:T(8,128)(2,1)}, bf16[128,8192]{1,0:T(8,128)(2,1)}, u32[]{:S(2)}, u32[]{:S(2)}) collective-permute-start(bf16[128,8192]{1,0:T(8,128)(2,1)} %get-tuple-element.6), channel_id=1, source_target_pairs={{0,32},{16,112},{32,0},{48,80},{64,96},{80,48},{96,64},{112,16},{1... | collective-permute-start | bytes 6291464 | tf_op jit(solution)/shard_map/ppermute | solution.py:226
  131.5 1.3 copy-start.10
  131.6 30.5 %collective-permute-start.5 = (bf16[32,8192]{1,0:T(8,128)(2,1)S(1)}, bf16[32,8192]{1,0:T(8,128)(2,1)}, u32[]{:S(2)}, u32[]{:S(2)}) collective-permute-start(bf16[32,8192]{1,0:T(8,128)(2,1)S(1)} %add_convert_fusion.13), channel_id=1, source_target_pairs={{0,96},{16,48},{32,64},{48,16},{64,32},{80,112},{96,0},{112,80},{1... | collective-permute-start | bytes 1572872 | tf_op jit(solution)/shard_map/ppermute | solution.py:229
  132.8 31.5 %all-to-all-start.5 = ((bf16[16,32,512]{2,1,0:T(8,128)(2,1)}), bf16[16,32,512]{2,1,0:T(8,128)(2,1)S(1)}, u32[]{:S(2)}, u32[]{:S(2)}) async-start(bf16[16,32,512]{2,1,0:T(8,128)(2,1)} %bitcast.75), calls=%async_computation.5 | async-start | bytes 1048576 | tf_op jit(solution)/shard_map/all_to_all | solution.py:234
  140.9 21.3 %copy-start.8 = (bf16[64,8192]{1,0:T(8,128)(2,1)S(1)}, bf16[64,8192]{1,0:T(8,128)(2,1)}, u32[]{:S(2)}) copy-start(bf16[64,8192]{1,0:T(8,128)(2,1)} %copy-done.7) | copy-start | bytes 3145732
  140.9 21.3 %copy-start.11 = (bf16[64,8192]{1,0:T(8,128)(2,1)S(1)}, bf16[64,8192]{1,0:T(8,128)(2,1)}, u32[]{:S(2)}) copy-start(bf16[64,8192]{1,0:T(8,128)(2,1)} %copy-done.10) | copy-start | bytes 3145732
  162.1 26.3 %collective-permute-start.2 = (bf16[64,8192]{1,0:T(8,128)(2,1)}, bf16[64,8192]{1,0:T(8,128)(2,1)}, u32[]{:S(2)}, u32[]{:S(2)}) collective-permute-start(bf16[64,8192]{1,0:T(8,128)(2,1)} %add_convert_fusion.7), channel_id=1, source_target_pairs={{0,96},{16,48},{32,64},{48,16},{64,32},{80,112},{96,0},{112,80},{1... | collective-permute-start | bytes 3145736 | tf_op jit(solution)/shard_map/ppermute | solution.py:229
  164.3 19.6 %all-to-all-start.3 = ((bf16[16,32,512]{2,1,0:T(8,128)(2,1)}), bf16[16,32,512]{2,1,0:T(8,128)(2,1)S(1)}, u32[]{:S(2)}, u32[]{:S(2)}) async-start(bf16[16,32,512]{2,1,0:T(8,128)(2,1)} %bitcast.83), calls=%async_computation.3 | async-start | bytes 1048576 | tf_op jit(solution)/shard_map/all_to_all | solution.py:234
  183.9 16.6 %all-to-all-start.6 = ((bf16[16,32,512]{2,1,0:T(8,128)(2,1)}), bf16[16,32,512]{2,1,0:T(8,128)(2,1)S(1)}, u32[]{:S(2)}, u32[]{:S(2)}) async-start(bf16[16,32,512]{2,1,0:T(8,128)(2,1)} %prefix.5), calls=%async_computation.6 | async-start | bytes 1048576 | tf_op jit(solution)/shard_map/all_to_all | solution.py:235
  200.5 20.4 %all-to-all-start.1 = ((bf16[16,64,512]{2,1,0:T(8,128)(2,1)}), bf16[16,64,512]{2,1,0:T(8,128)(2,1)S(1)}, u32[]{:S(2)}, u32[]{:S(2)}) async-start(bf16[16,64,512]{2,1,0:T(8,128)(2,1)} %bitcast.73), calls=%async_computation.1 | async-start | bytes 2097152 | tf_op jit(solution)/shard_map/all_to_all | solution.py:234
  220.9 13.6 %all-to-all-start.4 = ((bf16[16,32,512]{2,1,0:T(8,128)(2,1)}), bf16[16,32,512]{2,1,0:T(8,128)(2,1)S(1)}, u32[]{:S(2)}, u32[]{:S(2)}) async-start(bf16[16,32,512]{2,1,0:T(8,128)(2,1)} %prefix.4), calls=%async_computation.4 | async-start | bytes 1048576 | tf_op jit(solution)/shard_map/all_to_all | solution.py:235
  226.9 12.6 %copy-start.4 = (f32[1,8192]{1,0:T(1,128)S(1)}, f32[1,8192]{1,0:T(1,128)}, u32[]{:S(2)}) copy-start(f32[1,8192]{1,0:T(1,128)} %gain_ref.5) | copy-start | bytes 98308
  234.6 18.1 %all-to-all-start.2 = ((bf16[16,64,512]{2,1,0:T(8,128)(2,1)}), bf16[16,64,512]{2,1,0:T(8,128)(2,1)S(1)}, u32[]{:S(2)}, u32[]{:S(2)}) async-start(bf16[16,64,512]{2,1,0:T(8,128)(2,1)} %prefix.3), calls=%async_computation.2 | async-start | bytes 2097152 | tf_op jit(solution)/shard_map/all_to_all | solution.py:235
  240.7 12.7 %copy-start.1 = (bf16[32,8192]{1,0:T(8,128)(2,1)S(1)}, bf16[32,8192]{1,0:T(8,128)(2,1)}, u32[]{:S(2)}) copy-start(bf16[32,8192]{1,0:T(8,128)(2,1)} %copy-done) | copy-start | bytes 1572868
  252.7 1.0 copy-start.3
  (2 other events, 1.6 us)

commit v2 on v1

v2 whole, which is shorter than its diff:
```python
import functools
import math

import jax
import jax.numpy as jnp
from jax import lax
from jax.experimental import pallas as pl
from jax.experimental.pallas import tpu as pltpu
from jax.sharding import PartitionSpec as P

QUERY_HEADS = 64
HEAD_SIZE = 128
BLOCK = 64
LONGEST_PROMPT = 512
CHUNKS = (((0, 48),), ((64, 48),), ((48, 16), (112, 16)))
GROUP = 32
PACK_STEPS = 2
ROW_TILE = 16
LEAD = 48
PIECES = 4
COLUMNS = 1024
AHEAD = 4
FETCHES = 2
NEG = -1e30
COST = pl.CostEstimate(flops=0, transcendentals=0, bytes_accessed=0)
PARAMS = pltpu.CompilerParams(vmem_limit_bytes=16 << 20)


def pack_kernel(q_ref, k_ref, v_ref, first_ref, rest_ref):
    dests, lead_rows, width = first_ref.shape
    rows = lead_rows - GROUP
    for dest in range(dests):
        place = slice(dest * width, (dest + 1) * width)
        first_ref[dest, :rows] = q_ref[:rows, place]
        rest_ref[dest] = q_ref[rows:, place]
        column = 0
        for ref in (k_ref, v_ref):
            for begin in range(0, ref.shape[0], GROUP):
                first_ref[dest, rows:, column : column + HEAD_SIZE] = ref[
                    begin : begin + GROUP, dest * HEAD_SIZE : (dest + 1) * HEAD_SIZE
                ]
                column += HEAD_SIZE


def pack(parts, rows, queries, keys, values):
    tokens, model = queries.shape
    width = model // parts
    dests = parts // PACK_STEPS
    return pl.pallas_call(
        pack_kernel,
        out_shape=(
            pltpu.HBM((parts, rows + GROUP, width), jnp.bfloat16),
            pltpu.HBM((parts, tokens - rows, width), jnp.bfloat16),
        ),
        grid=(PACK_STEPS,),
        in_specs=[
            pl.BlockSpec((tokens, dests * width), lambda n: (0, n)),
            pl.BlockSpec((tokens, dests * HEAD_SIZE), lambda n: (0, n)),
            pl.BlockSpec((tokens, dests * HEAD_SIZE), lambda n: (0, n)),
        ],
        out_specs=(
            pl.BlockSpec((dests, rows + GROUP, width), lambda n: (n, 0, 0)),
            pl.BlockSpec((dests, tokens - rows, width), lambda n: (n, 0, 0)),
        ),
        compiler_params=PARAMS,
        cost_estimate=COST,
        name="pack",
    )(queries, keys, values)


def attend(queries, key, value, bias):
    heads, rows, _ = bias.shape
    factor = math.log2(math.e) / math.sqrt(HEAD_SIZE)
    scores = lax.dot_general(
        queries, key, (((1,), (1,)), ((), ())), preferred_element_type=jnp.float32
    )
    scores = scores.reshape(bias.shape) + bias
    largest = jnp.max(scores, axis=-1, keepdims=True)
    weights = jnp.exp2((scores - largest) * factor)
    norm = jnp.sum(weights, axis=-1, keepdims=True)
    context = jnp.dot(
        weights.astype(jnp.bfloat16).reshape(heads * rows, -1),
        value,
        preferred_element_type=jnp.float32,
    )
    return (context.reshape(heads, rows, HEAD_SIZE) / norm).astype(jnp.bfloat16)


def gather_keys(kv_ref, kv_scratch, part_rows):
    parts, lead_rows = kv_ref.shape[0], kv_ref.shape[1]
    groups = part_rows // GROUP
    for part in range(parts):
        for group in range(groups):
            begin = part * part_rows + group * GROUP
            for which in range(2):
                column = (which * groups + group) * HEAD_SIZE
                kv_scratch[begin : begin + GROUP, which * HEAD_SIZE : (which + 1) * HEAD_SIZE] = kv_ref[
                    part, lead_rows - GROUP :, column : column + HEAD_SIZE
                ]


def attend_part(
    lead, segments, part, parts, part_rows, lengths_ref, vert_ref, slash_ref, q_ref, kv_scratch, store
):
    heads = vert_ref.shape[0]
    lowest = jnp.int32(0)
    starts = []
    start = 0
    for p in range(lengths_ref.shape[0] - 1):
        start = start + lengths_ref[p]
        starts.append(start)
        lowest = jnp.where(part * part_rows + segments[0][0] >= start, start, lowest)
    shift = int(math.log2(BLOCK))
    rest = lead if segments[0][0] >= lead else 0
    queries = jnp.concatenate(
        [
            q_ref[0, first - rest : first - rest + count, h * HEAD_SIZE : (h + 1) * HEAD_SIZE]
            for h in range(heads)
            for first, count in segments
        ],
        axis=0,
    )
    needed = part + 1 - lax.div(lowest, part_rows)

    def window(count):
        keys = count * part_rows
        begin_part = jnp.clip(part + 1 - count, 0, parts - count)
        begin = pl.multiple_of(begin_part * part_rows, part_rows)
        key_block = lax.shift_right_logical(
            begin + lax.broadcasted_iota(jnp.int32, (heads, keys), 1), shift
        )
        vertical = key_block == vert_ref[:, 0:1]
        for n in range(1, vert_ref.shape[1]):
            vertical = vertical | (key_block == vert_ref[:, n : n + 1])
        biases = []
        for first, count in segments:
            query_first = part * part_rows + first
            query_pos = query_first + lax.broadcasted_iota(jnp.int32, (count, 1), 0)
            own_start = jnp.zeros_like(query_pos)
            for start in starts:
                own_start = jnp.where(query_pos >= start, start, own_start)
            key_pos = begin + lax.broadcasted_iota(jnp.int32, (count, keys), 1)
            token_bias = jnp.where((key_pos <= query_pos) & (key_pos >= own_start), 0.0, NEG)
            offset = lax.shift_right_logical(query_first, shift) - key_block
            hit = vertical
            for n in range(slash_ref.shape[1]):
                hit = hit | (offset == slash_ref[:, n : n + 1])
            head_bias = jnp.where(hit, 0.0, NEG)
            biases.append(token_bias[None] + head_bias[:, None, :])
        key_value = kv_scratch[pl.ds(begin, keys)]
        context = attend(
            queries,
            key_value[:, :HEAD_SIZE],
            key_value[:, HEAD_SIZE:],
            biases[0] if len(biases) == 1 else jnp.concatenate(biases, axis=1),
        )
        for h in range(heads):
            store(h, context[h])

    counts = [2, 3, min(LONGEST_PROMPT // part_rows + 1, parts)]
    for n, count in enumerate(counts):
        fits = needed > counts[n - 1] if n else needed <= count
        if 0 < n < len(counts) - 1:
            fits = fits & (needed <= count)
        pl.when(fits)(functools.partial(window, count))


def context_kernel(
    lead, segments, part_rows, order_ref, lengths_ref, vert_ref, slash_ref, q_ref, kv_ref, out_ref, kv_scratch
):
    step = pl.program_id(0)
    pl.when(step == 0)(lambda: gather_keys(kv_ref, kv_scratch, part_rows))

    def store(head, rows):
        out_ref[0, :, head * HEAD_SIZE : (head + 1) * HEAD_SIZE] = rows

    attend_part(
        lead, segments, order_ref[step], kv_ref.shape[0], part_rows, lengths_ref, vert_ref, slash_ref,
        q_ref, kv_scratch, store,
    )


def attention(lead, segments, part_rows, order, lengths, vert, slash, queries, key_value):
    parts, query_rows = queries.shape[:2]
    blocks = order.shape[0]
    rows = sum(count for _, count in segments)
    width = vert.shape[0] * HEAD_SIZE
    return pl.pallas_call(
        functools.partial(context_kernel, lead, segments, part_rows),
        out_shape=jax.ShapeDtypeStruct((blocks, rows, width), jnp.bfloat16),
        grid_spec=pltpu.PrefetchScalarGridSpec(
            num_scalar_prefetch=2,
            grid=(blocks,),
            in_specs=[
                pl.BlockSpec(vert.shape, lambda n, order, lengths: (0, 0)),
                pl.BlockSpec(slash.shape, lambda n, order, lengths: (0, 0)),
                pl.BlockSpec((1, query_rows, width), lambda n, order, lengths: (order[n], 0, 0)),
                pl.BlockSpec(key_value.shape, lambda n, order, lengths: (0, 0, 0)),
            ],
            out_specs=pl.BlockSpec((1, rows, width), lambda n, order, lengths: (n, 0, 0)),
            scratch_shapes=[pltpu.VMEM((parts * part_rows, 2 * HEAD_SIZE), jnp.bfloat16)],
        ),
        compiler_params=PARAMS,
        cost_estimate=COST,
        name="attention",
    )(order, lengths, vert, slash, queries, key_value)


def project_kernel(context_ref, weight_ref, *refs):
    *send_refs, keep_ref, weight_scratch, sems = refs
    tile = pl.program_id(0)
    tiles = weight_scratch.shape[0]

    def fetch(number):
        rows = weight_ref.shape[0] // FETCHES
        return [
            pltpu.make_async_copy(
                weight_ref.at[pl.ds(n * rows, rows), pl.ds(number * COLUMNS, COLUMNS)],
                weight_scratch.at[number, pl.ds(n * rows, rows)],
                sems.at[number, n],
            )
            for n in range(FETCHES)
        ]

    @pl.when(tile == 0)
    def _():
        for number in range(AHEAD):
            for copy in fetch(number):
                copy.start()

    @pl.when(tile + AHEAD < tiles)
    def _():
        for copy in fetch(tile + AHEAD):
            copy.start()

    for copy in fetch(tile):
        copy.wait()
    term = jnp.dot(
        context_ref[...].reshape(-1, context_ref.shape[2]),
        weight_scratch[tile],
        preferred_element_type=jnp.float32,
    ).astype(jnp.bfloat16)
    half = keep_ref.shape[0]
    keep_ref[...] = term[half:]
    per_piece = pl.num_programs(0) // len(send_refs)
    for piece, send_ref in enumerate(send_refs):

        @pl.when((tile >= piece * per_piece) & (tile < (piece + 1) * per_piece))
        def _():
            send_ref[...] = term[:half]


def project(context, weight):
    blocks, block_rows, width = context.shape
    half = blocks * block_rows // 2
    model = weight.shape[1]
    tiles = model // COLUMNS
    per_piece = tiles // PIECES

    def out_spec(piece, count):
        return pl.BlockSpec((half, COLUMNS), lambda n: (0, jnp.clip(n - piece * count, 0, count - 1)))

    return pl.pallas_call(
        project_kernel,
        out_shape=tuple(
            jax.ShapeDtypeStruct((half, model // PIECES), jnp.bfloat16) for _ in range(PIECES)
        )
        + (pltpu.HBM((half, model), jnp.bfloat16),),
        grid=(tiles,),
        in_specs=[
            pl.BlockSpec(context.shape, lambda n: (0, 0, 0)),
            pl.BlockSpec(memory_space=pl.ANY),
        ],
        out_specs=tuple(out_spec(piece, per_piece) for piece in range(PIECES)) + (out_spec(0, tiles),),
        scratch_shapes=[
            pltpu.VMEM((tiles, width, COLUMNS), jnp.bfloat16),
            pltpu.SemaphoreType.DMA((tiles, FETCHES)),
        ],
        compiler_params=pltpu.CompilerParams(vmem_limit_bytes=34 << 20),
        cost_estimate=COST,
        name="project",
    )(context, weight)


def join_kernel(kept_ref, *refs):
    *arrived_refs, keep_ref, send_ref = refs
    rows = keep_ref.shape[0]
    for piece, arrived_ref in enumerate(arrived_refs):

        @pl.when(pl.program_id(0) == piece)
        def _():
            total = kept_ref[...].astype(jnp.float32) + arrived_ref[...].astype(jnp.float32)
            total = total.astype(jnp.bfloat16)
            keep_ref[...] = total[:rows]
            send_ref[...] = total[rows:]


def join(kept, arrived):
    rows, model = kept.shape
    pieces = len(arrived)
    columns = model // pieces
    half = pltpu.HBM((rows // 2, model), jnp.bfloat16)
    half_spec = pl.BlockSpec((rows // 2, columns), lambda n: (0, n))
    whole = pl.BlockSpec((rows, columns), lambda n: (0, 0))
    return pl.pallas_call(
        join_kernel,
        out_shape=(half, half),
        grid=(pieces,),
        in_specs=[pl.BlockSpec((rows, columns), lambda n: (0, n))] + [whole] * pieces,
        out_specs=(half_spec, half_spec),
        compiler_params=PARAMS,
        cost_estimate=COST,
        name="join",
    )(kept, *arrived)


def finish_kernel(*refs):
    *term_refs, out_ref = refs
    layers, _, width = out_ref.shape
    begin = 0
    for kept_ref, first_ref, second_ref in zip(term_refs[::3], term_refs[1::3], term_refs[2::3]):
        rows = second_ref.shape[0]
        total = kept_ref[...].astype(jnp.float32) + first_ref[...].astype(jnp.float32)
        total = (total + second_ref[...].astype(jnp.float32)).astype(jnp.bfloat16)
        for n in range(layers):
            out_ref[n, begin : begin + rows] = total[:, n * width : (n + 1) * width]
        begin += rows


def finish(layers, *chunks):
    model = chunks[0][2].shape[1]
    width = model // layers
    group = layers // 2
    operands, in_specs = [], []
    for kept, first, second in chunks:
        rows = second.shape[0]
        operands += [kept, first, second]
        in_specs += [pl.BlockSpec((rows, group * width), lambda n: (0, n))] * 3
    rows = sum(second.shape[0] for _, _, second in chunks)
    return pl.pallas_call(
        finish_kernel,
        out_shape=pltpu.HBM((layers, rows, width), jnp.bfloat16),
        grid=(layers // group,),
        in_specs=in_specs,
        out_specs=pl.BlockSpec((group, rows, width), lambda n: (n, 0, 0)),
        compiler_params=PARAMS,
        cost_estimate=COST,
        name="finish",
    )(*operands)


def prefix_kernel(term_ref, out_ref):
    total = term_ref[0].astype(jnp.float32)
    out_ref[0] = term_ref[0]
    for layer in range(1, term_ref.shape[0]):
        total = total + term_ref[layer].astype(jnp.float32)
        out_ref[layer] = total.astype(jnp.bfloat16)


def prefix(terms):
    layers, rows, width = terms.shape
    spec = pl.BlockSpec((layers, rows // 2, width), lambda n: (0, n, 0))
    return pl.pallas_call(
        prefix_kernel,
        out_shape=pltpu.HBM(terms.shape, jnp.bfloat16),
        grid=(2,),
        in_specs=[spec],
        out_specs=spec,
        compiler_params=PARAMS,
        cost_estimate=COST,
        name="prefix",
    )(terms)


def norm_kernel(residual_ref, sums_ref, gain_ref, *refs):
    out_ref = refs[-1]
    pieces, rows, width = sums_ref.shape
    square = jnp.zeros((rows, 1), jnp.float32)
    for n in range(pieces):
        stream = residual_ref[:, n * width : (n + 1) * width].astype(jnp.float32)
        stream = stream + sums_ref[n].astype(jnp.float32)
        square = square + jnp.sum(stream * stream, axis=-1, keepdims=True)
    inverse = lax.rsqrt(square / (pieces * width) + 1e-06)
    for n in range(pieces):
        place = slice(n * width, (n + 1) * width)
        stream = residual_ref[:, place].astype(jnp.float32) + sums_ref[n].astype(jnp.float32)
        out_ref[:, place] = (stream * inverse * gain_ref[:, place]).astype(jnp.bfloat16)


def normalize(segments, residual, sums, gain, filled):
    model = residual.shape[1]
    tiles = [
        (first + begin) // ROW_TILE for first, count in segments for begin in range(0, count, ROW_TILE)
    ]

    def row_tile(n):
        tile = jnp.int32(tiles[0])
        for place, number in enumerate(tiles[1:], 1):
            tile = jnp.where(n == place, number, tile)
        return tile

    row_spec = pl.BlockSpec((ROW_TILE, model), lambda n: (row_tile(n), 0))
    layers, _, width = sums.shape
    in_specs = [
        row_spec,
        pl.BlockSpec((layers, ROW_TILE, width), lambda n: (0, n, 0)),
        pl.BlockSpec(gain.shape, lambda n: (0, 0)),
    ]
    operands = [residual, sums, gain]
    aliases = {}
    if filled is not None:
        in_specs.append(pl.BlockSpec(memory_space=pl.ANY))
        operands.append(filled)
        aliases = {3: 0}
    return pl.pallas_call(
        norm_kernel,
        out_shape=jax.ShapeDtypeStruct(residual.shape, jnp.bfloat16),
        grid=(len(tiles),),
        in_specs=in_specs,
        out_specs=row_spec,
        input_output_aliases=aliases,
        compiler_params=PARAMS,
        cost_estimate=COST,
        name="normalize",
    )(*operands)


def add(first, second):
    return (first.astype(jnp.float32) + second.astype(jnp.float32)).astype(jnp.bfloat16)


def after(value, *others):
    return lax.optimization_barrier((value, *others))[0]


def exchange_pairs(chips):
    def near(chip):
        return chip ^ 1

    def far(chip):
        return chips - 1 - chip

    every = [(x, c) for x in range(chips) for c in range(2)]
    cores = [(2 * x + c, 2 * x + 1 - c) for x, c in every]
    first = [(2 * x + c, 2 * (near(x) if c == 0 else far(x)) + c) for x, c in every]
    second = [(2 * x + c, 2 * (far(x) if c == 0 else near(x)) + c) for x, c in every]
    return cores, first, second


def local(
    queries,
    layer_key_rows,
    layer_value_rows,
    vertical_blocks,
    slash_offsets,
    prompt_lengths,
    residual,
    out_weight,
    section_gain,
):
    parts = lax.axis_size("seq")
    layers = lax.axis_size("pipe")
    chips = parts // 2
    tokens, model = queries.shape[1:]
    heads_here = QUERY_HEADS // parts
    place = lax.axis_index("seq")
    vert = lax.dynamic_slice_in_dim(vertical_blocks[0], place * heads_here, heads_here, 0)
    slash = lax.dynamic_slice_in_dim(slash_offsets[0], place * heads_here, heads_here, 0)

    lead = LEAD
    def in_hbm(array):
        return pltpu.with_memory_space_constraint(array, pltpu.HBM)

    lead_block, rest_block = pack(
        parts, lead, in_hbm(queries[0]), in_hbm(layer_key_rows[0]), in_hbm(layer_value_rows[0])
    )
    lead_block = lax.all_to_all(lead_block, "seq", 0, 0)
    rest_block = after(rest_block, lead_block)
    rest_block = lax.all_to_all(rest_block, "seq", 0, 0)

    chip, core = place // 2, place % 2
    near, far = chip ^ 1, chips - 1 - chip
    first_chip = jnp.where(core == 0, near, far)
    second_chip = jnp.where(core == 0, far, near)
    across = chips - 1 - near
    send = jnp.stack([chip, first_chip, second_chip, across]) * 2 + (1 - core)
    keep = jnp.stack([chip, second_chip, first_chip, across]) * 2 + core
    send, keep = send.astype(jnp.int32), keep.astype(jnp.int32)
    to_core, to_first, to_second = exchange_pairs(chips)

    weight = in_hbm(out_weight[0])
    order = jnp.concatenate([send, keep])

    def attend_chunk(segments, *others):
        source = lead_block if segments[0][0] < lead else rest_block
        return attention(
            lead, segments, tokens, after(order, *others), prompt_lengths, vert, slash, source, lead_block
        )

    def project_chunk(context, *others):
        *sent, kept = project(after(context, *others), weight)
        return kept, [lax.ppermute(piece, "seq", to_core) for piece in sent], sent[0]

    def reduce_next(kept, arrived_first, *others):
        rows = kept.shape[0] // 2
        to_send = after(add(kept[rows:], arrived_first[rows:]), *others)
        return lax.ppermute(to_send, "seq", to_second), to_send

    chunk_a, chunk_b, chunk_c = CHUNKS
    context_a = attend_chunk(chunk_a)
    kept_a, pieces_a, token_a = project_chunk(context_a)
    context_b = attend_chunk(chunk_b, token_a)
    kept_a, sent_a = join(after(kept_a, context_b), pieces_a)
    first_a = lax.ppermute(sent_a, "seq", to_first)
    kept_b, pieces_b, token_b = project_chunk(context_b, sent_a)
    context_c = attend_chunk(chunk_c, token_b)
    second_a, next_a = reduce_next(kept_a, first_a, context_c)
    kept_c, pieces_c, token_c = project_chunk(context_c, next_a)
    kept_b, sent_b = join(after(kept_b, token_c, second_a), pieces_b)
    first_b = lax.ppermute(sent_b, "seq", to_first)
    kept_c, sent_c = join(kept_c, pieces_c)
    first_c = lax.ppermute(sent_c, "seq", to_first)
    term_a = finish(layers, (kept_a, first_a, after(second_a, sent_c)))
    terms_a = lax.all_to_all(term_a, "pipe", 0, 0)
    second_b, next_b = reduce_next(kept_b, first_b, term_a)
    prefix_a = prefix(after(terms_a, next_b))
    sums_a = lax.all_to_all(prefix_a, "pipe", 0, 0)
    second_c, next_c = reduce_next(kept_c, first_c, prefix_a)
    term_bc = finish(layers, (kept_b, first_b, second_b), (kept_c, first_c, second_c))
    terms_bc = lax.all_to_all(after(term_bc, sums_a), "pipe", 0, 0)
    sums_bc = lax.all_to_all(prefix(terms_bc), "pipe", 0, 0)
    residual = in_hbm(residual)
    out = None
    for segments, sums in ((chunk_a, sums_a), (chunk_b + chunk_c, sums_bc)):
        out = normalize(segments, residual, sums, section_gain, out)
    return out[None]


def solution(mesh):
    placed = (
        P("pipe", "seq", None),
        P("pipe", "seq", None),
        P("pipe", "seq", None),
        P("pipe", None, None),
        P("pipe", None, None),
        P(),
        P("seq", None),
        P("pipe", "seq", None),
        P("pipe", None),
    )
    return jax.shard_map(
        local, mesh=mesh, in_specs=placed, out_specs=P("pipe", "seq", None), check_vma=False
    )
```

time: 256 us -> 201 us (0.79)
  waiting for transfers between devices: 125 us -> 43.6 us
  Pallas kernels: 24.5 us -> 74.2 us
  blocking collectives: 0 us -> 46.4 us
  matrix products: 30.5 us -> 0 us
  local copies, waits for them, and re-layouts: 15.8 us -> 0.28 us
  other arithmetic: 17.2 us -> 2.82 us
  starting transfers between devices: 42 us -> 32.7 us
    all_to_all x7 -> x4, waiting for transfers between devices: 85.1 us -> 25.9 us  [the longest x1 14 us: local(): sums_bc = lax.all_to_all(prefix(terms_bc), 'pipe', 0, 0)]
    all_to_all x0 -> x2, blocking collectives: none -> 46.4 us  [the longest x1 24.1 us: local(): terms_bc = lax.all_to_all(after(term_bc, sums_a), 'pipe', 0, 0)]
    pallas_call x6 -> x14, Pallas kernels: 23 us -> 66.4 us  [the longest x3 32.7 us: project(): pl.pallas_call(project_kernel, out_shape=tuple((jax.ShapeDtypeStruct((hal...]
    dot_general x6 -> x0, matrix products: 30.5 us -> none  [project(): jnp.dot(rows_in, out_weight[0], preferred_element_type=jnp.float32)]
    ppermute x9 -> x18, waiting for transfers between devices: 39.6 us -> 17.7 us  [the longest x3 7.4 us: reduce_next(): return (lax.ppermute(to_send, 'seq', to_second), to_send)]
    all_to_all x7 -> x4, starting transfers between devices: 36.5 us -> 21.4 us  [the longest x1 8.22 us: local(): terms_a = lax.all_to_all(term_a, 'pipe', 0, 0)]
    convert_element_type x9 -> x3, other arithmetic: 14 us -> 2.66 us  [add(): (first.astype(jnp.float32) + second.astype(jnp.float32)).astype(jnp.bfloa...]
    unnamed x39 -> x20, local copies, waits for them, and re-layouts: 6.78 us -> 0.04 us
  transfers between devices with their start and end apart: 16 -> 22, of which waited for: 9 -> 11; matrix products, arithmetic and copies ran while one was open for 16% -> 1% of each run, Pallas kernels for 7% -> 29%
where the time goes in v2:
time: 201 us; the launch traced here: 200 us
  Pallas kernels  74.2 us (37%)
  blocking collectives  46.4 us (23%)
  waiting for transfers between devices  43.6 us (22%)
  starting transfers between devices  32.7 us (16%)
  other arithmetic  2.82 us (1%)
    pallas_call x3, Pallas kernels, project(): pl.pallas_call(project_kernel, out_shape=tuple((jax.ShapeDtypeStruct((hal...  32.7 us
    all_to_all x1, blocking collectives, local(): terms_bc = lax.all_to_all(after(term_bc, sums_a), 'pipe', 0, 0)  24.1 us
    all_to_all x1, blocking collectives, local(): lead_block = lax.all_to_all(lead_block, 'seq', 0, 0)  22.3 us
    pallas_call x3, Pallas kernels, attention(): pl.pallas_call(functools.partial(context_kernel, lead, segments, part_row...  14.6 us
    all_to_all x1, waiting for transfers between devices, local(): sums_bc = lax.all_to_all(prefix(terms_bc), 'pipe', 0, 0)  14 us
    all_to_all x1, waiting for transfers between devices, local(): terms_a = lax.all_to_all(term_a, 'pipe', 0, 0)  10.1 us
    pallas_call x3, Pallas kernels, join(): pl.pallas_call(join_kernel, out_shape=(half, half), grid=(pieces,), in_sp...  9.16 us
    all_to_all x1, starting transfers between devices, local(): terms_a = lax.all_to_all(term_a, 'pipe', 0, 0)  8.22 us
  transfers between devices with their start and end apart: 22, of which 11 were waited for; matrix products, arithmetic and copies ran while one was open for 1% of the time, Pallas kernels for 29%

profile of v2, /device:TPU:2, one launch (start us, length us, event | category | flops | bytes accessed | tf_op | source)
XLA Modules:
  0.0 200.1 jit_solution(7538445707495430242)
XLA Ops:
  0.0 2.9 %pack.1 = (bf16[8,80,1024]{2,1,0:T(8,128)(2,1)}, bf16[8,80,1024]{2,1,0:T(8,128)(2,1)}) custom-call(bf16[128,8192]{1,0:T(8,128)(2,1)} %bitcast.16, bf16[128,1024]{1,0:T(8,128)(2,1)} %bitcast.17, bf16[128,1024]{1,0:T(8,128)(2,1)} %bitcast.18), custom_call_target="tpu_custom_call" | custom-call | tf_op jit(solution)/shard_map/pack/pallas_call | solution.py:49
  2.9 22.3 %all_to_all.30.q_ref.kv_ref = bf16[8,80,1024]{2,1,0:T(8,128)(2,1)S(1)} all-to-all(bf16[8,80,1024]{2,1,0:T(8,128)(2,1)} %get-tuple-element.41), channel_id=1, replica_groups=mesh['seq'=8,'pipe'=16] {'seq'}, dimensions={0} | all-to-all | bytes 2621440 | tf_op jit(solution)/shard_map/all_to_all | solution.py:477
  25.2 5.1 %all-to-all-start.1 = ((bf16[8,80,1024]{2,1,0:T(8,128)(2,1)}), bf16[8,80,1024]{2,1,0:T(8,128)(2,1)S(1)}, u32[]{:S(2)}, u32[]{:S(2)}) async-start(bf16[8,80,1024]{2,1,0:T(8,128)(2,1)} %get-tuple-element.45), calls=%async_computation.1 | async-start | bytes 2621440 | tf_op jit(solution)/shard_map/all_to_all | solution.py:479
  30.7 5.0 %attention.3.context_ref = bf16[8,48,1024]{2,1,0:T(8,128)(2,1)S(1)} custom-call(s32[8]{0:T(128)S(1)} %pad_add_fusion.order_ref, s32[4]{0:T(128)S(1)} %copy-done.7, s32[8,4]{1,0:T(8,128)S(1)} %copy.11.vert_ref, s32[8,4]{1,0:T(8,128)S(1)} %copy.12.slash_ref, bf16[8,80,1024]{2,1,0:T(8,128)(2,1)S(1)} %all_to_all.30.q_ref.kv_ref, ...), custom_call_target="tpu_custom_call" | custom-call | tf_op jit(solution)/shard_map/attention/pallas_call | solution.py:188
  35.7 12.0 %project.3 = (bf16[192,2048]{1,0:T(8,128)(2,1)}, bf16[192,2048]{1,0:T(8,128)(2,1)}, bf16[192,2048]{1,0:T(8,128)(2,1)}, bf16[192,2048]{1,0:T(8,128)(2,1)}, bf16[192,8192]{1,0:T(8,128)(2,1)}) custom-call(bf16[8,48,1024]{2,1,0:T(8,128)(2,1)S(1)} %attention.3.context_ref, bf16[1024,8192]{1,0:T(8,128)(2,1)} %bitcast.13), custom_call_target="tpu_custom_call" | custom-call | tf_op jit(solution)/shard_map/project/pallas_call | solution.py:263
  48.9 5.0 %attention.4.context_ref = bf16[8,48,1024]{2,1,0:T(8,128)(2,1)S(1)} custom-call(s32[8]{0:T(128)S(1)} %pad_add_fusion.order_ref, s32[4]{0:T(128)S(1)} %copy-done.7, s32[8,4]{1,0:T(8,128)S(1)} %copy.11.vert_ref, s32[8,4]{1,0:T(8,128)S(1)} %copy.12.slash_ref, bf16[8,80,1024]{2,1,0:T(8,128)(2,1)S(1)} %all-to-all-done.1.q_ref, ...), custom_call_target="tpu_custom_call" | custom-call | tf_op jit(solution)/shard_map/attention/pallas_call | solution.py:188
  53.9 4.3 %join.3 = (bf16[96,8192]{1,0:T(8,128)(2,1)}, bf16[96,8192]{1,0:T(8,128)(2,1)}) custom-call(bf16[192,8192]{1,0:T(8,128)(2,1)S(1)} %copy-done.3, bf16[192,2048]{1,0:T(8,128)(2,1)S(1)} %collective-permute-done.refs_0_, bf16[192,2048]{1,0:T(8,128)(2,1)} %collective-permute-done.1.refs_1_, bf16[192,2048]{1,0:T(8,128)(2,1)} %collective-permute-done.2.refs_2_, ...), custom_call_target="tpu_custom_call" | custom-call | tf_op jit(solution)/shard_map/join/pallas_call | solution.py:305
  58.4 11.5 %project.4 = (bf16[192,2048]{1,0:T(8,128)(2,1)S(1)}, bf16[192,2048]{1,0:T(8,128)(2,1)S(1)}, bf16[192,2048]{1,0:T(8,128)(2,1)S(1)}, bf16[192,2048]{1,0:T(8,128)(2,1)S(1)}, bf16[192,8192]{1,0:T(8,128)(2,1)}) custom-call(bf16[8,48,1024]{2,1,0:T(8,128)(2,1)S(1)} %attention.4.context_ref, bf16[1024,8192]{1,0:T(8,128)(2,1)} %bitcast.14), custom_call_target="tpu_custom_call" | custom-call | tf_op jit(solution)/shard_map/project/pallas_call | solution.py:263
  69.9 4.5 %attention.5.context_ref = bf16[8,32,1024]{2,1,0:T(8,128)(2,1)S(1)} custom-call(s32[8]{0:T(128)S(1)} %pad_add_fusion.order_ref, s32[4]{0:T(128)S(1)} %copy-done.7, s32[8,4]{1,0:T(8,128)S(1)} %copy.11.vert_ref, s32[8,4]{1,0:T(8,128)S(1)} %copy.12.slash_ref, bf16[8,80,1024]{2,1,0:T(8,128)(2,1)S(1)} %all-to-all-done.1.q_ref, ...), custom_call_target="tpu_custom_call" | custom-call | tf_op jit(solution)/shard_map/attention/pallas_call | solution.py:188
  74.5 4.4 %collective-permute-done.4.refs_1_ = bf16[96,8192]{1,0:T(8,128)(2,1)S(1)} collective-permute-done((bf16[96,8192]{1,0:T(8,128)(2,1)}, bf16[96,8192]{1,0:T(8,128)(2,1)S(1)}, u32[]{:S(2)}, u32[]{:S(2)}) %collective-permute-start.4) | collective-permute-done | bytes 1572896 | tf_op jit(solution)/shard_map/ppermute | solution.py:514
  79.0 1.6 collective-permute-start.5
  81.6 9.3 %project.5 = (bf16[128,2048]{1,0:T(8,128)(2,1)S(1)}, bf16[128,2048]{1,0:T(8,128)(2,1)S(1)}, bf16[128,2048]{1,0:T(8,128)(2,1)S(1)}, bf16[128,2048]{1,0:T(8,128)(2,1)S(1)}, bf16[128,8192]{1,0:T(8,128)(2,1)}) custom-call(bf16[8,32,1024]{2,1,0:T(8,128)(2,1)S(1)} %attention.5.context_ref, bf16[1024,8192]{1,0:T(8,128)(2,1)} %bitcast.15), custom_call_target="tpu_custom_call" | custom-call | tf_op jit(solution)/shard_map/project/pallas_call | solution.py:263
  91.1 2.7 %join.4 = (bf16[96,8192]{1,0:T(8,128)(2,1)}, bf16[96,8192]{1,0:T(8,128)(2,1)}) custom-call(bf16[192,8192]{1,0:T(8,128)(2,1)S(1)} %copy-done.2, bf16[192,2048]{1,0:T(8,128)(2,1)S(1)} %collective-permute-done.6.refs_0_, bf16[192,2048]{1,0:T(8,128)(2,1)S(1)} %collective-permute-done.7.refs_1_, bf16[192,2048]{1,0:T(8,128)(2,1)S(1)} %collective-permute-done.8.refs_2_, ...), custom_call_target="tpu_custom_call" | custom-call | tf_op jit(solution)/shard_map/join/pallas_call | solution.py:305
  93.8 1.6 collective-permute-start.10
  99.6 2.2 %join.5 = (bf16[64,8192]{1,0:T(8,128)(2,1)}, bf16[64,8192]{1,0:T(8,128)(2,1)}) custom-call(bf16[128,8192]{1,0:T(8,128)(2,1)S(1)} %copy-done.5, bf16[128,2048]{1,0:T(8,128)(2,1)S(1)} %collective-permute-done.11.refs_0_, bf16[128,2048]{1,0:T(8,128)(2,1)S(1)} %collective-permute-done.12.refs_1_, bf16[128,2048]{1,0:T(8,128)(2,1)S(1)} %collective-permute-done.13.refs_2_, ...), custom_call_target="tpu_custom_call" | custom-call | tf_op jit(solution)/shard_map/join/pallas_call | solution.py:305
  103.5 8.2 %all-to-all-start.2 = ((bf16[16,48,512]{2,1,0:T(8,128)(2,1)}), bf16[16,48,512]{2,1,0:T(8,128)(2,1)}, u32[]{:S(2)}, u32[]{:S(2)}) async-start(bf16[16,48,512]{2,1,0:T(8,128)(2,1)} %finish.2), calls=%async_computation.2 | async-start | bytes 1572864 | tf_op jit(solution)/shard_map/all_to_all | solution.py:524
  111.7 2.8 %collective-permute-done.10.refs_1_ = bf16[96,8192]{1,0:T(8,128)(2,1)S(1)} collective-permute-done((bf16[96,8192]{1,0:T(8,128)(2,1)}, bf16[96,8192]{1,0:T(8,128)(2,1)S(1)}, u32[]{:S(2)}, u32[]{:S(2)}) %collective-permute-start.10) | collective-permute-done | bytes 1572896 | tf_op jit(solution)/shard_map/ppermute | solution.py:520
  115.5 1.8 collective-permute-start.15
  117.4 10.1 %all-to-all-done.2.term_ref = bf16[16,48,512]{2,1,0:T(8,128)(2,1)} async-done(((bf16[16,48,512]{2,1,0:T(8,128)(2,1)}), bf16[16,48,512]{2,1,0:T(8,128)(2,1)}, u32[]{:S(2)}, u32[]{:S(2)}) %all-to-all-start.2) | async-done | bytes 786464 | tf_op jit(solution)/shard_map/all_to_all | solution.py:524
  127.5 2.0 prefix.2
  129.5 4.3 %all-to-all-start.3 = ((bf16[16,48,512]{2,1,0:T(8,128)(2,1)}), bf16[16,48,512]{2,1,0:T(8,128)(2,1)}, u32[]{:S(2)}, u32[]{:S(2)}) async-start(bf16[16,48,512]{2,1,0:T(8,128)(2,1)} %prefix.2), calls=%async_computation.3 | async-start | bytes 1572864 | tf_op jit(solution)/shard_map/all_to_all | solution.py:527
  133.8 1.4 add_convert_fusion.2
  135.2 2.5 %collective-permute-start.17 = (bf16[32,8192]{1,0:T(8,128)(2,1)S(1)}, bf16[32,8192]{1,0:T(8,128)(2,1)S(1)}, u32[]{:S(2)}, u32[]{:S(2)}) collective-permute-start(bf16[32,8192]{1,0:T(8,128)(2,1)S(1)} %add_convert_fusion.2), channel_id=1, source_target_pairs={{0,96},{16,48},{32,64},{48,16},{64,32},{80,112},{96,0},{112,80},{1... | collective-permute-start | bytes 1572872 | tf_op jit(solution)/shard_map/ppermute | solution.py:507
  137.7 7.2 %collective-permute-done.17.refs_5_ = bf16[32,8192]{1,0:T(8,128)(2,1)S(1)} collective-permute-done((bf16[32,8192]{1,0:T(8,128)(2,1)S(1)}, bf16[32,8192]{1,0:T(8,128)(2,1)S(1)}, u32[]{:S(2)}, u32[]{:S(2)}) %collective-permute-start.17) | collective-permute-done | bytes 524320 | tf_op jit(solution)/shard_map/ppermute | solution.py:507
  144.8 2.5 %finish.3 = bf16[16,80,512]{2,1,0:T(8,128)(2,1)} custom-call(bf16[96,8192]{1,0:T(8,128)(2,1)S(1)} %copy-done.1, bf16[96,8192]{1,0:T(8,128)(2,1)S(1)} %collective-permute-done.10.refs_1_, bf16[48,8192]{1,0:T(8,128)(2,1)} %collective-permute-done.15.refs_2_, bf16[64,8192]{1,0:T(8,128)(2,1)S(1)} %copy-done.4, bf16[64,8192]{1,0:T(8,128)(2,1)} %collective-permute-done.16.refs_4_, ...), custom_call_target="tpu_custom_call" | custom-call | tf_op jit(solution)/shard_map/finish/pallas_call | solution.py:340
  147.3 1.8 all-to-all-done.3.sums_ref
  149.1 24.1 %all_to_all.31.term_ref = bf16[16,80,512]{2,1,0:T(8,128)(2,1)S(1)} all-to-all(bf16[16,80,512]{2,1,0:T(8,128)(2,1)} %finish.3), channel_id=1, replica_groups=mesh['seq'=8,'pipe'=16] {'pipe'}, dimensions={0} | all-to-all | bytes 2621440 | tf_op jit(solution)/shard_map/all_to_all | solution.py:530
  173.1 1.3 prefix.3
  174.5 3.8 %all-to-all-start.5 = ((bf16[16,80,512]{2,1,0:T(8,128)(2,1)}), bf16[16,80,512]{2,1,0:T(8,128)(2,1)S(1)}, u32[]{:S(2)}, u32[]{:S(2)}) async-start(bf16[16,80,512]{2,1,0:T(8,128)(2,1)} %prefix.3), calls=%async_computation.5 | async-start | bytes 2621440 | tf_op jit(solution)/shard_map/all_to_all | solution.py:531
  178.3 3.3 %normalize.2.refs_0_ = bf16[128,8192]{1,0:T(8,128)(2,1)} custom-call(bf16[128,8192]{1,0:T(8,128)(2,1)} %residual_ref.3, bf16[16,48,512]{2,1,0:T(8,128)(2,1)} %all-to-all-done.3.sums_ref, f32[1,8192]{1,0:T(1,128)S(1)} %copy-done.6), custom_call_target="tpu_custom_call" | custom-call | tf_op jit(solution)/shard_map/normalize/pallas_call | solution.py:415
  181.7 14.0 %all-to-all-done.5.sums_ref = bf16[16,80,512]{2,1,0:T(8,128)(2,1)S(1)} async-done(((bf16[16,80,512]{2,1,0:T(8,128)(2,1)}), bf16[16,80,512]{2,1,0:T(8,128)(2,1)S(1)}, u32[]{:S(2)}, u32[]{:S(2)}) %all-to-all-start.5) | async-done | bytes 1310752 | tf_op jit(solution)/shard_map/all_to_all | solution.py:531
  195.7 4.4 %normalize.3 = bf16[128,8192]{1,0:T(8,128)(2,1)} custom-call(bf16[128,8192]{1,0:T(8,128)(2,1)} %residual_ref.3, bf16[16,80,512]{2,1,0:T(8,128)(2,1)S(1)} %all-to-all-done.5.sums_ref, f32[1,8192]{1,0:T(1,128)S(1)} %copy-done.6, bf16[128,8192]{1,0:T(8,128)(2,1)} %normalize.2.refs_0_), custom_call_target="tpu_custom_call", output_to_operand_aliasing={{}: (3, {})} | custom-call | tf_op jit(solution)/shard_map/normalize/pallas_call | solution.py:415
  (58 shorter events, 10.2 us)
Async XLA Ops:
  25.2 5.2 %copy-start.8 = (s32[1,64,4]{1,2,0:T(4,128)S(1)}, s32[1,64,4]{1,2,0:T(4,128)}, u32[]{:S(2)}) copy-start(s32[1,64,4]{1,2,0:T(4,128)} %param.13) | copy-start | bytes 3076
  25.2 5.2 %copy-start.9 = (s32[1,64,4]{1,2,0:T(4,128)S(1)}, s32[1,64,4]{1,2,0:T(4,128)}, u32[]{:S(2)}) copy-start(s32[1,64,4]{1,2,0:T(4,128)} %param.12) | copy-start | bytes 3076
  25.2 5.5 %copy-start.7 = (s32[4]{0:T(128)S(1)}, s32[4]{0:T(128)}, u32[]{:S(2)}) copy-start(s32[4]{0:T(128)} %lengths_ref.5) | copy-start | bytes 52
  25.2 23.6 %all-to-all-start.1 = ((bf16[8,80,1024]{2,1,0:T(8,128)(2,1)}), bf16[8,80,1024]{2,1,0:T(8,128)(2,1)S(1)}, u32[]{:S(2)}, u32[]{:S(2)}) async-start(bf16[8,80,1024]{2,1,0:T(8,128)(2,1)} %get-tuple-element.45), calls=%async_computation.1 | async-start | bytes 2621440 | tf_op jit(solution)/shard_map/all_to_all | solution.py:479
  47.8 6.1 %collective-permute-start = (bf16[192,2048]{1,0:T(8,128)(2,1)}, bf16[192,2048]{1,0:T(8,128)(2,1)S(1)}, u32[]{:S(2)}, u32[]{:S(2)}) collective-permute-start(bf16[192,2048]{1,0:T(8,128)(2,1)} %get-tuple-element.42), channel_id=1, source_target_pairs={{0,16},{16,0},{32,48},{48,32},{64,80},{80,64},{96,112},{112,96},{1... | collective-permute-start | bytes 2359304 | tf_op jit(solution)/shard_map/ppermute | solution.py:502
  48.0 5.9 %collective-permute-start.1 = (bf16[192,2048]{1,0:T(8,128)(2,1)}, bf16[192,2048]{1,0:T(8,128)(2,1)}, u32[]{:S(2)}, u32[]{:S(2)}) collective-permute-start(bf16[192,2048]{1,0:T(8,128)(2,1)} %get-tuple-element.48), channel_id=1, source_target_pairs={{0,16},{16,0},{32,48},{48,32},{64,80},{80,64},{96,112},{112,96},{1... | collective-permute-start | bytes 2359304 | tf_op jit(solution)/shard_map/ppermute | solution.py:502
  48.4 5.6 %collective-permute-start.2 = (bf16[192,2048]{1,0:T(8,128)(2,1)}, bf16[192,2048]{1,0:T(8,128)(2,1)}, u32[]{:S(2)}, u32[]{:S(2)}) collective-permute-start(bf16[192,2048]{1,0:T(8,128)(2,1)} %get-tuple-element.49), channel_id=1, source_target_pairs={{0,16},{16,0},{32,48},{48,32},{64,80},{80,64},{96,112},{112,96},{1... | collective-permute-start | bytes 2359304 | tf_op jit(solution)/shard_map/ppermute | solution.py:502
  48.5 5.4 %collective-permute-start.3 = (bf16[192,2048]{1,0:T(8,128)(2,1)}, bf16[192,2048]{1,0:T(8,128)(2,1)}, u32[]{:S(2)}, u32[]{:S(2)}) collective-permute-start(bf16[192,2048]{1,0:T(8,128)(2,1)} %get-tuple-element.50), channel_id=1, source_target_pairs={{0,16},{16,0},{32,48},{48,32},{64,80},{80,64},{96,112},{112,96},{1... | collective-permute-start | bytes 2359304 | tf_op jit(solution)/shard_map/ppermute | solution.py:502
  48.9 5.1 %copy-start.3 = (bf16[192,8192]{1,0:T(8,128)(2,1)S(1)}, bf16[192,8192]{1,0:T(8,128)(2,1)}, u32[]{:S(2)}) copy-start(bf16[192,8192]{1,0:T(8,128)(2,1)} %get-tuple-element.47.kept_ref) | copy-start | bytes 9437188
  58.2 20.6 %collective-permute-start.4 = (bf16[96,8192]{1,0:T(8,128)(2,1)}, bf16[96,8192]{1,0:T(8,128)(2,1)S(1)}, u32[]{:S(2)}, u32[]{:S(2)}) collective-permute-start(bf16[96,8192]{1,0:T(8,128)(2,1)} %get-tuple-element.51), channel_id=1, source_target_pairs={{0,32},{16,112},{32,0},{48,80},{64,96},{80,48},{96,64},{112,16},{1... | collective-permute-start | bytes 4718600 | tf_op jit(solution)/shard_map/ppermute | solution.py:514
  69.9 8.9 %copy-start = (bf16[96,8192]{1,0:T(8,128)(2,1)S(1)}, bf16[96,8192]{1,0:T(8,128)(2,1)}, u32[]{:S(2)}) copy-start(bf16[96,8192]{1,0:T(8,128)(2,1)} %get-tuple-element.56.refs_0_) | copy-start | bytes 4718596
  79.0 12.1 %collective-permute-start.5 = (bf16[48,8192]{1,0:T(8,128)(2,1)S(1)}, bf16[48,8192]{1,0:T(8,128)(2,1)S(1)}, u32[]{:S(2)}, u32[]{:S(2)}) collective-permute-start(bf16[48,8192]{1,0:T(8,128)(2,1)S(1)} %add_convert_fusion.1), channel_id=1, source_target_pairs={{0,96},{16,48},{32,64},{48,16},{64,32},{80,112},{96,0},{112,80},{1... | collective-permute-start | bytes 2359304 | tf_op jit(solution)/shard_map/ppermute | solution.py:507
  80.6 10.5 %collective-permute-start.6 = (bf16[192,2048]{1,0:T(8,128)(2,1)S(1)}, bf16[192,2048]{1,0:T(8,128)(2,1)S(1)}, u32[]{:S(2)}, u32[]{:S(2)}) collective-permute-start(bf16[192,2048]{1,0:T(8,128)(2,1)S(1)} %get-tuple-element.54), channel_id=1, source_target_pairs={{0,16},{16,0},{32,48},{48,32},{64,80},{80,64},{96,112},{112,96},{1... | collective-permute-start | bytes 2359304 | tf_op jit(solution)/shard_map/ppermute | solution.py:502
  80.6 10.5 %collective-permute-start.7 = (bf16[192,2048]{1,0:T(8,128)(2,1)S(1)}, bf16[192,2048]{1,0:T(8,128)(2,1)S(1)}, u32[]{:S(2)}, u32[]{:S(2)}) collective-permute-start(bf16[192,2048]{1,0:T(8,128)(2,1)S(1)} %get-tuple-element.61), channel_id=1, source_target_pairs={{0,16},{16,0},{32,48},{48,32},{64,80},{80,64},{96,112},{112,96},{1... | collective-permute-start | bytes 2359304 | tf_op jit(solution)/shard_map/ppermute | solution.py:502
  81.1 10.0 %collective-permute-start.8 = (bf16[192,2048]{1,0:T(8,128)(2,1)S(1)}, bf16[192,2048]{1,0:T(8,128)(2,1)S(1)}, u32[]{:S(2)}, u32[]{:S(2)}) collective-permute-start(bf16[192,2048]{1,0:T(8,128)(2,1)S(1)} %get-tuple-element.62), channel_id=1, source_target_pairs={{0,16},{16,0},{32,48},{48,32},{64,80},{80,64},{96,112},{112,96},{1... | collective-permute-start | bytes 2359304 | tf_op jit(solution)/shard_map/ppermute | solution.py:502
  81.1 10.0 %collective-permute-start.9 = (bf16[192,2048]{1,0:T(8,128)(2,1)S(1)}, bf16[192,2048]{1,0:T(8,128)(2,1)S(1)}, u32[]{:S(2)}, u32[]{:S(2)}) collective-permute-start(bf16[192,2048]{1,0:T(8,128)(2,1)S(1)} %get-tuple-element.63), channel_id=1, source_target_pairs={{0,16},{16,0},{32,48},{48,32},{64,80},{80,64},{96,112},{112,96},{1... | collective-permute-start | bytes 2359304 | tf_op jit(solution)/shard_map/ppermute | solution.py:502
  81.6 9.5 %copy-start.2 = (bf16[192,8192]{1,0:T(8,128)(2,1)S(1)}, bf16[192,8192]{1,0:T(8,128)(2,1)}, u32[]{:S(2)}) copy-start(bf16[192,8192]{1,0:T(8,128)(2,1)} %get-tuple-element.60.kept_ref) | copy-start | bytes 9437188
  91.1 8.5 %copy-start.5 = (bf16[128,8192]{1,0:T(8,128)(2,1)S(1)}, bf16[128,8192]{1,0:T(8,128)(2,1)}, u32[]{:S(2)}) copy-start(bf16[128,8192]{1,0:T(8,128)(2,1)} %get-tuple-element.66.kept_ref) | copy-start | bytes 6291460
  93.8 20.6 %collective-permute-start.10 = (bf16[96,8192]{1,0:T(8,128)(2,1)}, bf16[96,8192]{1,0:T(8,128)(2,1)S(1)}, u32[]{:S(2)}, u32[]{:S(2)}) collective-permute-start(bf16[96,8192]{1,0:T(8,128)(2,1)} %get-tuple-element.65), channel_id=1, source_target_pairs={{0,32},{16,112},{32,0},{48,80},{64,96},{80,48},{96,64},{112,16},{1... | collective-permute-start | bytes 4718600 | tf_op jit(solution)/shard_map/ppermute | solution.py:520
  95.4 1.9 collective-permute-start.11
  95.4 2.7 %collective-permute-start.12 = (bf16[128,2048]{1,0:T(8,128)(2,1)S(1)}, bf16[128,2048]{1,0:T(8,128)(2,1)S(1)}, u32[]{:S(2)}, u32[]{:S(2)}) collective-permute-start(bf16[128,2048]{1,0:T(8,128)(2,1)S(1)} %get-tuple-element.67), channel_id=1, source_target_pairs={{0,16},{16,0},{32,48},{48,32},{64,80},{80,64},{96,112},{112,96},{1... | collective-permute-start | bytes 1572872 | tf_op jit(solution)/shard_map/ppermute | solution.py:502
  95.9 2.9 %collective-permute-start.13 = (bf16[128,2048]{1,0:T(8,128)(2,1)S(1)}, bf16[128,2048]{1,0:T(8,128)(2,1)S(1)}, u32[]{:S(2)}, u32[]{:S(2)}) collective-permute-start(bf16[128,2048]{1,0:T(8,128)(2,1)S(1)} %get-tuple-element.68), channel_id=1, source_target_pairs={{0,16},{16,0},{32,48},{48,32},{64,80},{80,64},{96,112},{112,96},{1... | collective-permute-start | bytes 1572872 | tf_op jit(solution)/shard_map/ppermute | solution.py:502
  95.9 3.6 %collective-permute-start.14 = (bf16[128,2048]{1,0:T(8,128)(2,1)S(1)}, bf16[128,2048]{1,0:T(8,128)(2,1)S(1)}, u32[]{:S(2)}, u32[]{:S(2)}) collective-permute-start(bf16[128,2048]{1,0:T(8,128)(2,1)S(1)} %get-tuple-element.69), channel_id=1, source_target_pairs={{0,16},{16,0},{32,48},{48,32},{64,80},{80,64},{96,112},{112,96},{1... | collective-permute-start | bytes 1572872 | tf_op jit(solution)/shard_map/ppermute | solution.py:502
  101.8 32.0 %collective-permute-start.16 = (bf16[64,8192]{1,0:T(8,128)(2,1)}, bf16[64,8192]{1,0:T(8,128)(2,1)}, u32[]{:S(2)}, u32[]{:S(2)}) collective-permute-start(bf16[64,8192]{1,0:T(8,128)(2,1)} %get-tuple-element.70), channel_id=1, source_target_pairs={{0,32},{16,112},{32,0},{48,80},{64,96},{80,48},{96,64},{112,16},{1... | collective-permute-start | bytes 3145736 | tf_op jit(solution)/shard_map/ppermute | solution.py:522
  103.5 11.0 %copy-start.1 = (bf16[96,8192]{1,0:T(8,128)(2,1)S(1)}, bf16[96,8192]{1,0:T(8,128)(2,1)}, u32[]{:S(2)}) copy-start(bf16[96,8192]{1,0:T(8,128)(2,1)} %get-tuple-element.64.refs_0_) | copy-start | bytes 4718596
  103.5 24.0 %all-to-all-start.2 = ((bf16[16,48,512]{2,1,0:T(8,128)(2,1)}), bf16[16,48,512]{2,1,0:T(8,128)(2,1)}, u32[]{:S(2)}, u32[]{:S(2)}) async-start(bf16[16,48,512]{2,1,0:T(8,128)(2,1)} %finish.2), calls=%async_computation.2 | async-start | bytes 1572864 | tf_op jit(solution)/shard_map/all_to_all | solution.py:524
  115.5 29.3 %collective-permute-start.15 = (bf16[48,8192]{1,0:T(8,128)(2,1)}, bf16[48,8192]{1,0:T(8,128)(2,1)}, u32[]{:S(2)}, u32[]{:S(2)}) collective-permute-start(bf16[48,8192]{1,0:T(8,128)(2,1)} %add_convert_fusion), channel_id=1, source_target_pairs={{0,96},{16,48},{32,64},{48,16},{64,32},{80,112},{96,0},{112,80},{1... | collective-permute-start | bytes 2359304 | tf_op jit(solution)/shard_map/ppermute | solution.py:507
  129.5 19.6 %all-to-all-start.3 = ((bf16[16,48,512]{2,1,0:T(8,128)(2,1)}), bf16[16,48,512]{2,1,0:T(8,128)(2,1)}, u32[]{:S(2)}, u32[]{:S(2)}) async-start(bf16[16,48,512]{2,1,0:T(8,128)(2,1)} %prefix.2), calls=%async_computation.3 | async-start | bytes 1572864 | tf_op jit(solution)/shard_map/all_to_all | solution.py:527
  133.8 11.1 %copy-start.4 = (bf16[64,8192]{1,0:T(8,128)(2,1)S(1)}, bf16[64,8192]{1,0:T(8,128)(2,1)}, u32[]{:S(2)}) copy-start(bf16[64,8192]{1,0:T(8,128)(2,1)} %get-tuple-element.73.refs_3_) | copy-start | bytes 3145732
  135.2 9.6 %collective-permute-start.17 = (bf16[32,8192]{1,0:T(8,128)(2,1)S(1)}, bf16[32,8192]{1,0:T(8,128)(2,1)S(1)}, u32[]{:S(2)}, u32[]{:S(2)}) collective-permute-start(bf16[32,8192]{1,0:T(8,128)(2,1)S(1)} %add_convert_fusion.2), channel_id=1, source_target_pairs={{0,96},{16,48},{32,64},{48,16},{64,32},{80,112},{96,0},{112,80},{1... | collective-permute-start | bytes 1572872 | tf_op jit(solution)/shard_map/ppermute | solution.py:507
  174.5 3.8 %copy-start.6 = (f32[1,8192]{1,0:T(1,128)S(1)}, f32[1,8192]{1,0:T(1,128)}, u32[]{:S(2)}) copy-start(f32[1,8192]{1,0:T(1,128)} %gain_ref.3) | copy-start | bytes 98308
  174.5 21.2 %all-to-all-start.5 = ((bf16[16,80,512]{2,1,0:T(8,128)(2,1)}), bf16[16,80,512]{2,1,0:T(8,128)(2,1)S(1)}, u32[]{:S(2)}, u32[]{:S(2)}) async-start(bf16[16,80,512]{2,1,0:T(8,128)(2,1)} %prefix.3), calls=%async_computation.5 | async-start | bytes 2621440 | tf_op jit(solution)/shard_map/all_to_all | solution.py:531

commit v3 on v2

--- a/solution.py
+++ b/solution.py
@@ -26,46 +26,60 @@
 PARAMS = pltpu.CompilerParams(vmem_limit_bytes=16 << 20)
 
 
-def pack_kernel(q_ref, k_ref, v_ref, first_ref, rest_ref):
-    dests, lead_rows, width = first_ref.shape
+def pack_lead_kernel(q_ref, k_ref, v_ref, out_ref):
+    dests, lead_rows, width = out_ref.shape
     rows = lead_rows - GROUP
     for dest in range(dests):
-        place = slice(dest * width, (dest + 1) * width)
-        first_ref[dest, :rows] = q_ref[:rows, place]
-        rest_ref[dest] = q_ref[rows:, place]
+        out_ref[dest, :rows] = q_ref[:, dest * width : (dest + 1) * width]
         column = 0
         for ref in (k_ref, v_ref):
             for begin in range(0, ref.shape[0], GROUP):
-                first_ref[dest, rows:, column : column + HEAD_SIZE] = ref[
+                out_ref[dest, rows:, column : column + HEAD_SIZE] = ref[
                     begin : begin + GROUP, dest * HEAD_SIZE : (dest + 1) * HEAD_SIZE
                 ]
                 column += HEAD_SIZE
 
 
-def pack(parts, rows, queries, keys, values):
+def pack_lead(parts, rows, queries, keys, values):
     tokens, model = queries.shape
     width = model // parts
     dests = parts // PACK_STEPS
     return pl.pallas_call(
-        pack_kernel,
-        out_shape=(
-            pltpu.HBM((parts, rows + GROUP, width), jnp.bfloat16),
-            pltpu.HBM((parts, tokens - rows, width), jnp.bfloat16),
-        ),
+        pack_lead_kernel,
+        out_shape=pltpu.HBM((parts, rows + GROUP, width), jnp.bfloat16),
         grid=(PACK_STEPS,),
         in_specs=[
-            pl.BlockSpec((tokens, dests * width), lambda n: (0, n)),
+            pl.BlockSpec((rows, dests * width), lambda n: (0, n)),
             pl.BlockSpec((tokens, dests * HEAD_SIZE), lambda n: (0, n)),
             pl.BlockSpec((tokens, dests * HEAD_SIZE), lambda n: (0, n)),
         ],
-        out_specs=(
-            pl.BlockSpec((dests, rows + GROUP, width), lambda n: (n, 0, 0)),
-            pl.BlockSpec((dests, tokens - rows, width), lambda n: (n, 0, 0)),
-        ),
-        compiler_params=PARAMS,
-        cost_estimate=COST,
-        name="pack",
+        out_specs=pl.BlockSpec((dests, rows + GROUP, width), lambda n: (n, 0, 0)),
+        compiler_params=PARAMS,
+        cost_estimate=COST,
+        name="pack_lead",
     )(queries, keys, values)
+
+
+def pack_rest_kernel(q_ref, out_ref):
+    dests, rows, width = out_ref.shape
+    for dest in range(dests):
+        out_ref[dest] = q_ref[q_ref.shape[0] - rows :, dest * width : (dest + 1) * width]
+
+
+def pack_rest(parts, rows, queries):
+    tokens, model = queries.shape
+    width = model // parts
+    dests = parts // PACK_STEPS
+    return pl.pallas_call(
+        pack_rest_kernel,
+        out_shape=pltpu.HBM((parts, tokens - rows, width), jnp.bfloat16),
+        grid=(PACK_STEPS,),
+        in_specs=[pl.BlockSpec((tokens, dests * width), lambda n: (0, n))],
+        out_specs=pl.BlockSpec((dests, tokens - rows, width), lambda n: (n, 0, 0)),
+        compiler_params=PARAMS,
+        cost_estimate=COST,
+        name="pack_rest",
+    )(queries)
 
 
 def attend(queries, key, value, bias):
@@ -209,15 +223,18 @@
 def project_kernel(context_ref, weight_ref, *refs):
     *send_refs, keep_ref, weight_scratch, sems = refs
     tile = pl.program_id(0)
-    tiles = weight_scratch.shape[0]
+    tiles = pl.num_programs(0)
+
+    def slot(number):
+        return lax.rem(number, weight_scratch.shape[0])
 
     def fetch(number):
         rows = weight_ref.shape[0] // FETCHES
         return [
             pltpu.make_async_copy(
                 weight_ref.at[pl.ds(n * rows, rows), pl.ds(number * COLUMNS, COLUMNS)],
-                weight_scratch.at[number, pl.ds(n * rows, rows)],
-                sems.at[number, n],
+                weight_scratch.at[slot(number), pl.ds(n * rows, rows)],
+                sems.at[slot(number), n],
             )
             for n in range(FETCHES)
         ]
@@ -225,7 +242,7 @@
     @pl.when(tile == 0)
     def _():
         for number in range(AHEAD):
-            for copy in fetch(number):
+            for copy in fetch(jnp.int32(number)):
                 copy.start()
 
     @pl.when(tile + AHEAD < tiles)
@@ -237,7 +254,7 @@
         copy.wait()
     term = jnp.dot(
         context_ref[...].reshape(-1, context_ref.shape[2]),
-        weight_scratch[tile],
+        weight_scratch[slot(tile)],
         preferred_element_type=jnp.float32,
     ).astype(jnp.bfloat16)
     half = keep_ref.shape[0]
@@ -263,7 +280,7 @@
     return pl.pallas_call(
         project_kernel,
         out_shape=tuple(
-            jax.ShapeDtypeStruct((half, model // PIECES), jnp.bfloat16) for _ in range(PIECES)
+            pltpu.VMEM((half, model // PIECES), jnp.bfloat16) for _ in range(PIECES)
         )
         + (pltpu.HBM((half, model), jnp.bfloat16),),
         grid=(tiles,),
@@ -273,10 +290,10 @@
         ],
         out_specs=tuple(out_spec(piece, per_piece) for piece in range(PIECES)) + (out_spec(0, tiles),),
         scratch_shapes=[
-            pltpu.VMEM((tiles, width, COLUMNS), jnp.bfloat16),
-            pltpu.SemaphoreType.DMA((tiles, FETCHES)),
+            pltpu.VMEM((AHEAD + 1, width, COLUMNS), jnp.bfloat16),
+            pltpu.SemaphoreType.DMA((AHEAD + 1, FETCHES)),
         ],
-        compiler_params=pltpu.CompilerParams(vmem_limit_bytes=34 << 20),
+        compiler_params=pltpu.CompilerParams(vmem_limit_bytes=24 << 20),
         cost_estimate=COST,
         name="project",
     )(context, weight)
@@ -314,8 +331,12 @@
     )(kept, *arrived)
 
 
-def finish_kernel(*refs):
-    *term_refs, out_ref = refs
+def finish_kernel(chunks, *refs):
+    term_refs, rest = refs[: 3 * chunks], refs[3 * chunks :]
+    if len(rest) == 1:
+        out_ref = rest[0]
+    else:
+        before_ref, out_ref, total_ref = rest
     layers, _, width = out_ref.shape
     begin = 0
     for kept_ref, first_ref, second_ref in zip(term_refs[::3], term_refs[1::3], term_refs[2::3]):
@@ -325,24 +346,42 @@
         for n in range(layers):
             out_ref[n, begin : begin + rows] = total[:, n * width : (n + 1) * width]
         begin += rows
-
-
-def finish(layers, *chunks):
+    if len(rest) == 1:
+        return
+
+    @pl.when(pl.program_id(0) == 0)
+    def _():
+        total_ref[...] = jnp.zeros_like(total_ref)
+
+    total = total_ref[...]
+    for n in range(layers):
+        total = total + before_ref[n].astype(jnp.float32)
+        out_ref[n, begin:] = total.astype(jnp.bfloat16)
+    total_ref[...] = total
+
+
+def finish(layers, *chunks, before=None):
     model = chunks[0][2].shape[1]
     width = model // layers
     group = layers // 2
-    operands, in_specs = [], []
+    operands, in_specs, scratch = [], [], []
     for kept, first, second in chunks:
-        rows = second.shape[0]
         operands += [kept, first, second]
-        in_specs += [pl.BlockSpec((rows, group * width), lambda n: (0, n))] * 3
+        in_specs += [pl.BlockSpec((second.shape[0], group * width), lambda n: (0, n))] * 3
     rows = sum(second.shape[0] for _, _, second in chunks)
-    return pl.pallas_call(
-        finish_kernel,
+    if before is not None:
+        more = before.shape[1]
+        operands.append(before)
+        in_specs.append(pl.BlockSpec((group, more, width), lambda n: (n, 0, 0)))
+        scratch.append(pltpu.VMEM((more, width), jnp.float32))
+        rows += more
+    return pl.pallas_call(
+        functools.partial(finish_kernel, len(chunks)),
         out_shape=pltpu.HBM((layers, rows, width), jnp.bfloat16),
         grid=(layers // group,),
         in_specs=in_specs,
         out_specs=pl.BlockSpec((group, rows, width), lambda n: (n, 0, 0)),
+        scratch_shapes=scratch,
         compiler_params=PARAMS,
         cost_estimate=COST,
         name="finish",
@@ -357,13 +396,13 @@
         out_ref[layer] = total.astype(jnp.bfloat16)
 
 
-def prefix(terms):
-    layers, rows, width = terms.shape
-    spec = pl.BlockSpec((layers, rows // 2, width), lambda n: (0, n, 0))
+def prefix(terms, rows):
+    layers, _, width = terms.shape
+    spec = pl.BlockSpec((layers, rows, width), lambda n: (0, 0, 0))
     return pl.pallas_call(
         prefix_kernel,
-        out_shape=pltpu.HBM(terms.shape, jnp.bfloat16),
-        grid=(2,),
+        out_shape=pltpu.HBM((layers, rows, width), jnp.bfloat16),
+        grid=(1,),
         in_specs=[spec],
         out_specs=spec,
         compiler_params=PARAMS,
@@ -387,10 +426,10 @@
         out_ref[:, place] = (stream * inverse * gain_ref[:, place]).astype(jnp.bfloat16)
 
 
-def normalize(segments, residual, sums, gain, filled):
+def normalize(segments, residual, sums, begin, gain, filled):
     model = residual.shape[1]
     tiles = [
-        (first + begin) // ROW_TILE for first, count in segments for begin in range(0, count, ROW_TILE)
+        (first + row) // ROW_TILE for first, count in segments for row in range(0, count, ROW_TILE)
     ]
 
     def row_tile(n):
@@ -403,7 +442,7 @@
     layers, _, width = sums.shape
     in_specs = [
         row_spec,
-        pl.BlockSpec((layers, ROW_TILE, width), lambda n: (0, n, 0)),
+        pl.BlockSpec((layers, ROW_TILE, width), lambda n: (0, begin // ROW_TILE + n, 0)),
         pl.BlockSpec(gain.shape, lambda n: (0, 0)),
     ]
     operands = [residual, sums, gain]
@@ -471,9 +510,9 @@
     def in_hbm(array):
         return pltpu.with_memory_space_constraint(array, pltpu.HBM)
 
-    lead_block, rest_block = pack(
-        parts, lead, in_hbm(queries[0]), in_hbm(layer_key_rows[0]), in_hbm(layer_value_rows[0])
-    )
+    queries = in_hbm(queries[0])
+    lead_block = pack_lead(parts, lead, queries, in_hbm(layer_key_rows[0]), in_hbm(layer_value_rows[0]))
+    rest_block = pack_rest(parts, lead, after(queries, lead_block))
     lead_block = lax.all_to_all(lead_block, "seq", 0, 0)
     rest_block = after(rest_block, lead_block)
     rest_block = lax.all_to_all(rest_block, "seq", 0, 0)
@@ -523,16 +562,14 @@
     term_a = finish(layers, (kept_a, first_a, after(second_a, sent_c)))
     terms_a = lax.all_to_all(term_a, "pipe", 0, 0)
     second_b, next_b = reduce_next(kept_b, first_b, term_a)
-    prefix_a = prefix(after(terms_a, next_b))
+    prefix_a = prefix(after(terms_a, next_b), terms_a.shape[1])
     sums_a = lax.all_to_all(prefix_a, "pipe", 0, 0)
-    second_c, next_c = reduce_next(kept_c, first_c, prefix_a)
+    second_c, next_c = reduce_next(kept_c, first_c, next_b)
     term_bc = finish(layers, (kept_b, first_b, second_b), (kept_c, first_c, second_c))
     terms_bc = lax.all_to_all(after(term_bc, sums_a), "pipe", 0, 0)
-    sums_bc = lax.all_to_all(prefix(terms_bc), "pipe", 0, 0)
-    residual = in_hbm(residual)
-    out = None
-    for segments, sums in ((chunk_a, sums_a), (chunk_b + chunk_c, sums_bc)):
-        out = normalize(segments, residual, sums, section_gain, out)
+    sums_bc = lax.all_to_all(prefix(terms_bc, terms_bc.shape[1]), "pipe", 0, 0)
+    out = normalize(chunk_a, residual, sums_a, 0, section_gain, None)
+    out = normalize(chunk_b + chunk_c, residual, sums_bc, 0, section_gain, out)
     return out[None]
 
 

time: 201 us -> 199 us (0.990)
  blocking collectives: 46.4 us -> 24.1 us
  waiting for transfers between devices: 43.6 us -> 59.1 us
  starting transfers between devices: 32.7 us -> 37.1 us
    all_to_all x1 -> x0, blocking collectives: 22.3 us -> none  [local(): lead_block = lax.all_to_all(lead_block, 'seq', 0, 0)]
    all_to_all x1 -> x2, waiting for transfers between devices: 14 us -> 29.2 us  [the longest x1 14.9 us: local(): lead_block = lax.all_to_all(lead_block, 'seq', 0, 0)]
    all_to_all x1 -> x2, starting transfers between devices: 3.83 us -> 8.66 us  [the longest x1 4.83 us: local(): lead_block = lax.all_to_all(lead_block, 'seq', 0, 0)]
    pallas_call x8 -> x9, Pallas kernels: 42.7 us -> 44.7 us  [the longest x3 32.8 us: project(): pl.pallas_call(project_kernel, out_shape=tuple((pltpu.VMEM((half, model /...]
  transfers between devices with their start and end apart: 22 -> 23, of which waited for: 11 -> 12; matrix products, arithmetic and copies ran while one was open for 1% -> 1% of each run, Pallas kernels for 29% -> 31%
where the time goes in v3:
time: 199 us; the launch traced here: 198 us
  Pallas kernels  74.7 us (38%)
  waiting for transfers between devices  59.1 us (30%)
  starting transfers between devices  37.1 us (19%)
  blocking collectives  24.1 us (12%)
  other arithmetic  2.8 us (1%)
    pallas_call x3, Pallas kernels, project(): pl.pallas_call(project_kernel, out_shape=tuple((pltpu.VMEM((half, model /...  32.8 us
    all_to_all x1, blocking collectives, local(): terms_bc = lax.all_to_all(after(term_bc, sums_a), 'pipe', 0, 0)  24.1 us
    all_to_all x1, waiting for transfers between devices, local(): lead_block = lax.all_to_all(lead_block, 'seq', 0, 0)  14.9 us
    pallas_call x3, Pallas kernels, attention(): pl.pallas_call(functools.partial(context_kernel, lead, segments, part_row...  14.9 us
    all_to_all x1, waiting for transfers between devices, local(): sums_bc = lax.all_to_all(prefix(terms_bc, terms_bc.shape[1]), 'pipe', 0, 0)  14.3 us
    all_to_all x1, waiting for transfers between devices, local(): terms_a = lax.all_to_all(term_a, 'pipe', 0, 0)  10.1 us
    pallas_call x3, Pallas kernels, join(): pl.pallas_call(join_kernel, out_shape=(half, half), grid=(pieces,), in_sp...  9.12 us
    all_to_all x1, starting transfers between devices, local(): terms_a = lax.all_to_all(term_a, 'pipe', 0, 0)  8.22 us
  transfers between devices with their start and end apart: 23, of which 12 were waited for; matrix products, arithmetic and copies ran while one was open for 1% of the time, Pallas kernels for 31%

profile of v3, /device:TPU:2, one launch (start us, length us, event | category | flops | bytes accessed | tf_op | source)
XLA Modules:
  0.0 198.3 jit_solution(2703275942012486989)
XLA Ops:
  0.0 2.3 %pack_lead.1 = bf16[8,80,1024]{2,1,0:T(8,128)(2,1)} custom-call(bf16[128,8192]{1,0:T(8,128)(2,1)} %bitcast.16, bf16[128,1024]{1,0:T(8,128)(2,1)} %bitcast.18, bf16[128,1024]{1,0:T(8,128)(2,1)} %bitcast.19), custom_call_target="tpu_custom_call" | custom-call | tf_op jit(solution)/shard_map/pack_lead/pallas_call | solution.py:47
  2.3 4.8 %all-to-all-start = ((bf16[8,80,1024]{2,1,0:T(8,128)(2,1)}), bf16[8,80,1024]{2,1,0:T(8,128)(2,1)S(1)}, u32[]{:S(2)}, u32[]{:S(2)}) async-start(bf16[8,80,1024]{2,1,0:T(8,128)(2,1)} %pack_lead.1), calls=%async_computation | async-start | bytes 2621440 | tf_op jit(solution)/shard_map/all_to_all | solution.py:516
  7.1 2.4 %pack_rest.1 = bf16[8,80,1024]{2,1,0:T(8,128)(2,1)} custom-call(bf16[128,8192]{1,0:T(8,128)(2,1)} %bitcast.17), custom_call_target="tpu_custom_call" | custom-call | tf_op jit(solution)/shard_map/pack_rest/pallas_call | solution.py:73
  9.5 14.9 %all-to-all-done.q_ref.kv_ref = bf16[8,80,1024]{2,1,0:T(8,128)(2,1)S(1)} async-done(((bf16[8,80,1024]{2,1,0:T(8,128)(2,1)}), bf16[8,80,1024]{2,1,0:T(8,128)(2,1)S(1)}, u32[]{:S(2)}, u32[]{:S(2)}) %all-to-all-start) | async-done | bytes 1310752 | tf_op jit(solution)/shard_map/all_to_all | solution.py:516
  24.4 4.9 %all-to-all-start.1 = ((bf16[8,80,1024]{2,1,0:T(8,128)(2,1)}), bf16[8,80,1024]{2,1,0:T(8,128)(2,1)S(1)}, u32[]{:S(2)}, u32[]{:S(2)}) async-start(bf16[8,80,1024]{2,1,0:T(8,128)(2,1)} %pack_rest.1), calls=%async_computation.1 | async-start | bytes 2621440 | tf_op jit(solution)/shard_map/all_to_all | solution.py:518
  29.8 5.4 %attention.3.context_ref = bf16[8,48,1024]{2,1,0:T(8,128)(2,1)S(1)} custom-call(s32[8]{0:T(128)S(1)} %pad_add_fusion.order_ref, s32[4]{0:T(128)S(1)} %copy-done.8, s32[8,4]{1,0:T(8,128)S(1)} %copy.11.vert_ref, s32[8,4]{1,0:T(8,128)S(1)} %copy.12.slash_ref, bf16[8,80,1024]{2,1,0:T(8,128)(2,1)S(1)} %all-to-all-done.q_ref.kv_ref, ...), custom_call_target="tpu_custom_call" | custom-call | tf_op jit(solution)/shard_map/attention/pallas_call | solution.py:202
  35.2 12.1 %project.3 = (bf16[192,2048]{1,0:T(8,128)(2,1)}, bf16[192,2048]{1,0:T(8,128)(2,1)}, bf16[192,2048]{1,0:T(8,128)(2,1)}, bf16[192,2048]{1,0:T(8,128)(2,1)}, bf16[192,8192]{1,0:T(8,128)(2,1)}) custom-call(bf16[8,48,1024]{2,1,0:T(8,128)(2,1)S(1)} %attention.3.context_ref, bf16[1024,8192]{1,0:T(8,128)(2,1)} %bitcast.13), custom_call_target="tpu_custom_call" | custom-call | tf_op jit(solution)/shard_map/project/pallas_call | solution.py:280
  48.4 5.0 %attention.4.context_ref = bf16[8,48,1024]{2,1,0:T(8,128)(2,1)S(1)} custom-call(s32[8]{0:T(128)S(1)} %pad_add_fusion.order_ref, s32[4]{0:T(128)S(1)} %copy-done.8, s32[8,4]{1,0:T(8,128)S(1)} %copy.11.vert_ref, s32[8,4]{1,0:T(8,128)S(1)} %copy.12.slash_ref, bf16[8,80,1024]{2,1,0:T(8,128)(2,1)S(1)} %all-to-all-done.1.q_ref, ...), custom_call_target="tpu_custom_call" | custom-call | tf_op jit(solution)/shard_map/attention/pallas_call | solution.py:202
  53.4 4.2 %join.3 = (bf16[96,8192]{1,0:T(8,128)(2,1)}, bf16[96,8192]{1,0:T(8,128)(2,1)}) custom-call(bf16[192,8192]{1,0:T(8,128)(2,1)S(1)} %copy-done.4, bf16[192,2048]{1,0:T(8,128)(2,1)S(1)} %collective-permute-done.refs_0_, bf16[192,2048]{1,0:T(8,128)(2,1)} %collective-permute-done.1.refs_1_, bf16[192,2048]{1,0:T(8,128)(2,1)} %collective-permute-done.2.refs_2_, ...), custom_call_target="tpu_custom_call" | custom-call | tf_op jit(solution)/shard_map/join/pallas_call | solution.py:322
  57.8 11.5 %project.4 = (bf16[192,2048]{1,0:T(8,128)(2,1)S(1)}, bf16[192,2048]{1,0:T(8,128)(2,1)S(1)}, bf16[192,2048]{1,0:T(8,128)(2,1)S(1)}, bf16[192,2048]{1,0:T(8,128)(2,1)S(1)}, bf16[192,8192]{1,0:T(8,128)(2,1)}) custom-call(bf16[8,48,1024]{2,1,0:T(8,128)(2,1)S(1)} %attention.4.context_ref, bf16[1024,8192]{1,0:T(8,128)(2,1)} %bitcast.14), custom_call_target="tpu_custom_call" | custom-call | tf_op jit(solution)/shard_map/project/pallas_call | solution.py:280
  69.3 4.5 %attention.5.context_ref = bf16[8,32,1024]{2,1,0:T(8,128)(2,1)S(1)} custom-call(s32[8]{0:T(128)S(1)} %pad_add_fusion.order_ref, s32[4]{0:T(128)S(1)} %copy-done.8, s32[8,4]{1,0:T(8,128)S(1)} %copy.11.vert_ref, s32[8,4]{1,0:T(8,128)S(1)} %copy.12.slash_ref, bf16[8,80,1024]{2,1,0:T(8,128)(2,1)S(1)} %all-to-all-done.1.q_ref, ...), custom_call_target="tpu_custom_call" | custom-call | tf_op jit(solution)/shard_map/attention/pallas_call | solution.py:202
  73.8 4.5 %collective-permute-done.4.refs_1_ = bf16[96,8192]{1,0:T(8,128)(2,1)S(1)} collective-permute-done((bf16[96,8192]{1,0:T(8,128)(2,1)}, bf16[96,8192]{1,0:T(8,128)(2,1)S(1)}, u32[]{:S(2)}, u32[]{:S(2)}) %collective-permute-start.4) | collective-permute-done | bytes 1572896 | tf_op jit(solution)/shard_map/ppermute | solution.py:553
  78.5 1.6 collective-permute-start.5
  81.0 9.2 %project.5 = (bf16[128,2048]{1,0:T(8,128)(2,1)S(1)}, bf16[128,2048]{1,0:T(8,128)(2,1)S(1)}, bf16[128,2048]{1,0:T(8,128)(2,1)S(1)}, bf16[128,2048]{1,0:T(8,128)(2,1)S(1)}, bf16[128,8192]{1,0:T(8,128)(2,1)}) custom-call(bf16[8,32,1024]{2,1,0:T(8,128)(2,1)S(1)} %attention.5.context_ref, bf16[1024,8192]{1,0:T(8,128)(2,1)} %bitcast.15), custom_call_target="tpu_custom_call" | custom-call | tf_op jit(solution)/shard_map/project/pallas_call | solution.py:280
  90.6 2.7 %join.4 = (bf16[96,8192]{1,0:T(8,128)(2,1)}, bf16[96,8192]{1,0:T(8,128)(2,1)}) custom-call(bf16[192,8192]{1,0:T(8,128)(2,1)S(1)} %copy-done.3, bf16[192,2048]{1,0:T(8,128)(2,1)S(1)} %collective-permute-done.6.refs_0_, bf16[192,2048]{1,0:T(8,128)(2,1)S(1)} %collective-permute-done.7.refs_1_, bf16[192,2048]{1,0:T(8,128)(2,1)S(1)} %collective-permute-done.8.refs_2_, ...), custom_call_target="tpu_custom_call" | custom-call | tf_op jit(solution)/shard_map/join/pallas_call | solution.py:322
  93.3 1.6 collective-permute-start.10
  99.0 2.2 %join.5 = (bf16[64,8192]{1,0:T(8,128)(2,1)}, bf16[64,8192]{1,0:T(8,128)(2,1)}) custom-call(bf16[128,8192]{1,0:T(8,128)(2,1)S(1)} %copy-done.6, bf16[128,2048]{1,0:T(8,128)(2,1)S(1)} %collective-permute-done.11.refs_0_, bf16[128,2048]{1,0:T(8,128)(2,1)S(1)} %collective-permute-done.12.refs_1_, bf16[128,2048]{1,0:T(8,128)(2,1)S(1)} %collective-permute-done.13.refs_2_, ...), custom_call_target="tpu_custom_call" | custom-call | tf_op jit(solution)/shard_map/join/pallas_call | solution.py:322
  102.9 8.2 %all-to-all-start.2 = ((bf16[16,48,512]{2,1,0:T(8,128)(2,1)}), bf16[16,48,512]{2,1,0:T(8,128)(2,1)}, u32[]{:S(2)}, u32[]{:S(2)}) async-start(bf16[16,48,512]{2,1,0:T(8,128)(2,1)} %finish.2), calls=%async_computation.2 | async-start | bytes 1572864 | tf_op jit(solution)/shard_map/all_to_all | solution.py:563
  111.1 2.8 %collective-permute-done.10.refs_1_ = bf16[96,8192]{1,0:T(8,128)(2,1)S(1)} collective-permute-done((bf16[96,8192]{1,0:T(8,128)(2,1)}, bf16[96,8192]{1,0:T(8,128)(2,1)S(1)}, u32[]{:S(2)}, u32[]{:S(2)}) %collective-permute-start.10) | collective-permute-done | bytes 1572896 | tf_op jit(solution)/shard_map/ppermute | solution.py:559
  115.0 1.8 collective-permute-start.15
  116.8 10.1 %all-to-all-done.2.term_ref = bf16[16,48,512]{2,1,0:T(8,128)(2,1)} async-done(((bf16[16,48,512]{2,1,0:T(8,128)(2,1)}), bf16[16,48,512]{2,1,0:T(8,128)(2,1)}, u32[]{:S(2)}, u32[]{:S(2)}) %all-to-all-start.2) | async-done | bytes 786464 | tf_op jit(solution)/shard_map/all_to_all | solution.py:563
  126.9 2.1 %prefix.2 = bf16[16,48,512]{2,1,0:T(8,128)(2,1)} custom-call(bf16[16,48,512]{2,1,0:T(8,128)(2,1)} %all-to-all-done.2.term_ref), custom_call_target="tpu_custom_call" | custom-call | tf_op jit(solution)/shard_map/prefix/pallas_call | solution.py:402
  129.1 4.3 %all-to-all-start.3 = ((bf16[16,48,512]{2,1,0:T(8,128)(2,1)}), bf16[16,48,512]{2,1,0:T(8,128)(2,1)}, u32[]{:S(2)}, u32[]{:S(2)}) async-start(bf16[16,48,512]{2,1,0:T(8,128)(2,1)} %prefix.2), calls=%async_computation.3 | async-start | bytes 1572864 | tf_op jit(solution)/shard_map/all_to_all | solution.py:566
  134.8 2.3 %collective-permute-start.17 = (bf16[32,8192]{1,0:T(8,128)(2,1)S(1)}, bf16[32,8192]{1,0:T(8,128)(2,1)S(1)}, u32[]{:S(2)}, u32[]{:S(2)}) collective-permute-start(bf16[32,8192]{1,0:T(8,128)(2,1)S(1)} %add_convert_fusion.2), channel_id=1, source_target_pairs={{0,96},{16,48},{32,64},{48,16},{64,32},{80,112},{96,0},{112,80},{1... | collective-permute-start | bytes 1572872 | tf_op jit(solution)/shard_map/ppermute | solution.py:546
  137.1 7.2 %collective-permute-done.17.refs_5_ = bf16[32,8192]{1,0:T(8,128)(2,1)S(1)} collective-permute-done((bf16[32,8192]{1,0:T(8,128)(2,1)S(1)}, bf16[32,8192]{1,0:T(8,128)(2,1)S(1)}, u32[]{:S(2)}, u32[]{:S(2)}) %collective-permute-start.17) | collective-permute-done | bytes 524320 | tf_op jit(solution)/shard_map/ppermute | solution.py:546
  144.3 2.5 %finish.3 = bf16[16,80,512]{2,1,0:T(8,128)(2,1)} custom-call(bf16[96,8192]{1,0:T(8,128)(2,1)S(1)} %copy-done.2, bf16[96,8192]{1,0:T(8,128)(2,1)S(1)} %collective-permute-done.10.refs_1_, bf16[48,8192]{1,0:T(8,128)(2,1)} %collective-permute-done.15.refs_2_, bf16[64,8192]{1,0:T(8,128)(2,1)S(1)} %copy-done.5, bf16[64,8192]{1,0:T(8,128)(2,1)} %collective-permute-done.16.refs_4_, ...), custom_call_target="tpu_custom_call" | custom-call | tf_op jit(solution)/shard_map/finish/pallas_call | solution.py:378
  146.8 1.9 all-to-all-done.3.sums_ref
  148.7 24.1 %all_to_all.30.term_ref = bf16[16,80,512]{2,1,0:T(8,128)(2,1)S(1)} all-to-all(bf16[16,80,512]{2,1,0:T(8,128)(2,1)} %finish.3), channel_id=1, replica_groups=mesh['seq'=8,'pipe'=16] {'pipe'}, dimensions={0} | all-to-all | bytes 2621440 | tf_op jit(solution)/shard_map/all_to_all | solution.py:569
  174.1 3.8 %all-to-all-start.5 = ((bf16[16,80,512]{2,1,0:T(8,128)(2,1)}), bf16[16,80,512]{2,1,0:T(8,128)(2,1)S(1)}, u32[]{:S(2)}, u32[]{:S(2)}) async-start(bf16[16,80,512]{2,1,0:T(8,128)(2,1)} %prefix.3), calls=%async_computation.5 | async-start | bytes 2621440 | tf_op jit(solution)/shard_map/all_to_all | solution.py:570
  177.9 3.2 %normalize.2.refs_0_ = bf16[128,8192]{1,0:T(8,128)(2,1)} custom-call(bf16[128,8192]{1,0:T(8,128)(2,1)S(1)} %copy-done, bf16[16,48,512]{2,1,0:T(8,128)(2,1)} %all-to-all-done.3.sums_ref, f32[1,8192]{1,0:T(1,128)S(1)} %copy-done.7), custom_call_target="tpu_custom_call" | custom-call | tf_op jit(solution)/shard_map/normalize/pallas_call | solution.py:454
  181.1 14.3 %all-to-all-done.5.sums_ref = bf16[16,80,512]{2,1,0:T(8,128)(2,1)S(1)} async-done(((bf16[16,80,512]{2,1,0:T(8,128)(2,1)}), bf16[16,80,512]{2,1,0:T(8,128)(2,1)S(1)}, u32[]{:S(2)}, u32[]{:S(2)}) %all-to-all-start.5) | async-done | bytes 1310752 | tf_op jit(solution)/shard_map/all_to_all | solution.py:570
  195.5 2.8 %normalize.3 = bf16[128,8192]{1,0:T(8,128)(2,1)} custom-call(bf16[128,8192]{1,0:T(8,128)(2,1)S(1)} %copy-done, bf16[16,80,512]{2,1,0:T(8,128)(2,1)S(1)} %all-to-all-done.5.sums_ref, f32[1,8192]{1,0:T(1,128)S(1)} %copy-done.7, bf16[128,8192]{1,0:T(8,128)(2,1)} %normalize.2.refs_0_), custom_call_target="tpu_custom_call", output_to_operand_aliasing={{}: (3, {})} | custom-call | tf_op jit(solution)/shard_map/normalize/pallas_call | solution.py:454
  (62 shorter events, 12.8 us)
Async XLA Ops:
  2.3 22.1 %all-to-all-start = ((bf16[8,80,1024]{2,1,0:T(8,128)(2,1)}), bf16[8,80,1024]{2,1,0:T(8,128)(2,1)S(1)}, u32[]{:S(2)}, u32[]{:S(2)}) async-start(bf16[8,80,1024]{2,1,0:T(8,128)(2,1)} %pack_lead.1), calls=%async_computation | async-start | bytes 2621440 | tf_op jit(solution)/shard_map/all_to_all | solution.py:516
  9.5 20.0 %copy-start.9 = (s32[1,64,4]{1,2,0:T(4,128)S(1)}, s32[1,64,4]{1,2,0:T(4,128)}, u32[]{:S(2)}) copy-start(s32[1,64,4]{1,2,0:T(4,128)} %param.13) | copy-start | bytes 3076
  9.5 20.0 %copy-start.10 = (s32[1,64,4]{1,2,0:T(4,128)S(1)}, s32[1,64,4]{1,2,0:T(4,128)}, u32[]{:S(2)}) copy-start(s32[1,64,4]{1,2,0:T(4,128)} %param.12) | copy-start | bytes 3076
  9.5 20.2 %copy-start.8 = (s32[4]{0:T(128)S(1)}, s32[4]{0:T(128)}, u32[]{:S(2)}) copy-start(s32[4]{0:T(128)} %lengths_ref.5) | copy-start | bytes 52
  24.4 24.0 %all-to-all-start.1 = ((bf16[8,80,1024]{2,1,0:T(8,128)(2,1)}), bf16[8,80,1024]{2,1,0:T(8,128)(2,1)S(1)}, u32[]{:S(2)}, u32[]{:S(2)}) async-start(bf16[8,80,1024]{2,1,0:T(8,128)(2,1)} %pack_rest.1), calls=%async_computation.1 | async-start | bytes 2621440 | tf_op jit(solution)/shard_map/all_to_all | solution.py:518
  47.3 6.1 %collective-permute-start = (bf16[192,2048]{1,0:T(8,128)(2,1)}, bf16[192,2048]{1,0:T(8,128)(2,1)S(1)}, u32[]{:S(2)}, u32[]{:S(2)}) collective-permute-start(bf16[192,2048]{1,0:T(8,128)(2,1)} %get-tuple-element.40), channel_id=1, source_target_pairs={{0,16},{16,0},{32,48},{48,32},{64,80},{80,64},{96,112},{112,96},{1... | collective-permute-start | bytes 2359304 | tf_op jit(solution)/shard_map/ppermute | solution.py:541
  47.5 5.9 %collective-permute-start.1 = (bf16[192,2048]{1,0:T(8,128)(2,1)}, bf16[192,2048]{1,0:T(8,128)(2,1)}, u32[]{:S(2)}, u32[]{:S(2)}) collective-permute-start(bf16[192,2048]{1,0:T(8,128)(2,1)} %get-tuple-element.46), channel_id=1, source_target_pairs={{0,16},{16,0},{32,48},{48,32},{64,80},{80,64},{96,112},{112,96},{1... | collective-permute-start | bytes 2359304 | tf_op jit(solution)/shard_map/ppermute | solution.py:541
  47.9 5.5 %collective-permute-start.2 = (bf16[192,2048]{1,0:T(8,128)(2,1)}, bf16[192,2048]{1,0:T(8,128)(2,1)}, u32[]{:S(2)}, u32[]{:S(2)}) collective-permute-start(bf16[192,2048]{1,0:T(8,128)(2,1)} %get-tuple-element.47), channel_id=1, source_target_pairs={{0,16},{16,0},{32,48},{48,32},{64,80},{80,64},{96,112},{112,96},{1... | collective-permute-start | bytes 2359304 | tf_op jit(solution)/shard_map/ppermute | solution.py:541
  48.0 5.4 %collective-permute-start.3 = (bf16[192,2048]{1,0:T(8,128)(2,1)}, bf16[192,2048]{1,0:T(8,128)(2,1)}, u32[]{:S(2)}, u32[]{:S(2)}) collective-permute-start(bf16[192,2048]{1,0:T(8,128)(2,1)} %get-tuple-element.48), channel_id=1, source_target_pairs={{0,16},{16,0},{32,48},{48,32},{64,80},{80,64},{96,112},{112,96},{1... | collective-permute-start | bytes 2359304 | tf_op jit(solution)/shard_map/ppermute | solution.py:541
  48.4 5.0 %copy-start.4 = (bf16[192,8192]{1,0:T(8,128)(2,1)S(1)}, bf16[192,8192]{1,0:T(8,128)(2,1)}, u32[]{:S(2)}) copy-start(bf16[192,8192]{1,0:T(8,128)(2,1)} %get-tuple-element.45.kept_ref) | copy-start | bytes 9437188
  57.7 20.6 %collective-permute-start.4 = (bf16[96,8192]{1,0:T(8,128)(2,1)}, bf16[96,8192]{1,0:T(8,128)(2,1)S(1)}, u32[]{:S(2)}, u32[]{:S(2)}) collective-permute-start(bf16[96,8192]{1,0:T(8,128)(2,1)} %get-tuple-element.49), channel_id=1, source_target_pairs={{0,32},{16,112},{32,0},{48,80},{64,96},{80,48},{96,64},{112,16},{1... | collective-permute-start | bytes 4718600 | tf_op jit(solution)/shard_map/ppermute | solution.py:553
  69.3 9.0 %copy-start.1 = (bf16[96,8192]{1,0:T(8,128)(2,1)S(1)}, bf16[96,8192]{1,0:T(8,128)(2,1)}, u32[]{:S(2)}) copy-start(bf16[96,8192]{1,0:T(8,128)(2,1)} %get-tuple-element.54.refs_0_) | copy-start | bytes 4718596
  78.5 12.1 %collective-permute-start.5 = (bf16[48,8192]{1,0:T(8,128)(2,1)S(1)}, bf16[48,8192]{1,0:T(8,128)(2,1)S(1)}, u32[]{:S(2)}, u32[]{:S(2)}) collective-permute-start(bf16[48,8192]{1,0:T(8,128)(2,1)S(1)} %add_convert_fusion.1), channel_id=1, source_target_pairs={{0,96},{16,48},{32,64},{48,16},{64,32},{80,112},{96,0},{112,80},{1... | collective-permute-start | bytes 2359304 | tf_op jit(solution)/shard_map/ppermute | solution.py:546
  80.0 10.5 %collective-permute-start.6 = (bf16[192,2048]{1,0:T(8,128)(2,1)S(1)}, bf16[192,2048]{1,0:T(8,128)(2,1)S(1)}, u32[]{:S(2)}, u32[]{:S(2)}) collective-permute-start(bf16[192,2048]{1,0:T(8,128)(2,1)S(1)} %get-tuple-element.52), channel_id=1, source_target_pairs={{0,16},{16,0},{32,48},{48,32},{64,80},{80,64},{96,112},{112,96},{1... | collective-permute-start | bytes 2359304 | tf_op jit(solution)/shard_map/ppermute | solution.py:541
  80.0 10.5 %collective-permute-start.7 = (bf16[192,2048]{1,0:T(8,128)(2,1)S(1)}, bf16[192,2048]{1,0:T(8,128)(2,1)S(1)}, u32[]{:S(2)}, u32[]{:S(2)}) collective-permute-start(bf16[192,2048]{1,0:T(8,128)(2,1)S(1)} %get-tuple-element.59), channel_id=1, source_target_pairs={{0,16},{16,0},{32,48},{48,32},{64,80},{80,64},{96,112},{112,96},{1... | collective-permute-start | bytes 2359304 | tf_op jit(solution)/shard_map/ppermute | solution.py:541
  80.5 10.0 %collective-permute-start.8 = (bf16[192,2048]{1,0:T(8,128)(2,1)S(1)}, bf16[192,2048]{1,0:T(8,128)(2,1)S(1)}, u32[]{:S(2)}, u32[]{:S(2)}) collective-permute-start(bf16[192,2048]{1,0:T(8,128)(2,1)S(1)} %get-tuple-element.60), channel_id=1, source_target_pairs={{0,16},{16,0},{32,48},{48,32},{64,80},{80,64},{96,112},{112,96},{1... | collective-permute-start | bytes 2359304 | tf_op jit(solution)/shard_map/ppermute | solution.py:541
  80.5 10.0 %collective-permute-start.9 = (bf16[192,2048]{1,0:T(8,128)(2,1)S(1)}, bf16[192,2048]{1,0:T(8,128)(2,1)S(1)}, u32[]{:S(2)}, u32[]{:S(2)}) collective-permute-start(bf16[192,2048]{1,0:T(8,128)(2,1)S(1)} %get-tuple-element.61), channel_id=1, source_target_pairs={{0,16},{16,0},{32,48},{48,32},{64,80},{80,64},{96,112},{112,96},{1... | collective-permute-start | bytes 2359304 | tf_op jit(solution)/shard_map/ppermute | solution.py:541
  81.0 9.5 %copy-start.3 = (bf16[192,8192]{1,0:T(8,128)(2,1)S(1)}, bf16[192,8192]{1,0:T(8,128)(2,1)}, u32[]{:S(2)}) copy-start(bf16[192,8192]{1,0:T(8,128)(2,1)} %get-tuple-element.58.kept_ref) | copy-start | bytes 9437188
  90.5 8.5 %copy-start.6 = (bf16[128,8192]{1,0:T(8,128)(2,1)S(1)}, bf16[128,8192]{1,0:T(8,128)(2,1)}, u32[]{:S(2)}) copy-start(bf16[128,8192]{1,0:T(8,128)(2,1)} %get-tuple-element.64.kept_ref) | copy-start | bytes 6291460
  93.3 20.6 %collective-permute-start.10 = (bf16[96,8192]{1,0:T(8,128)(2,1)}, bf16[96,8192]{1,0:T(8,128)(2,1)S(1)}, u32[]{:S(2)}, u32[]{:S(2)}) collective-permute-start(bf16[96,8192]{1,0:T(8,128)(2,1)} %get-tuple-element.63), channel_id=1, source_target_pairs={{0,32},{16,112},{32,0},{48,80},{64,96},{80,48},{96,64},{112,16},{1... | collective-permute-start | bytes 4718600 | tf_op jit(solution)/shard_map/ppermute | solution.py:559
  94.8 1.9 collective-permute-start.11
  94.8 2.7 %collective-permute-start.12 = (bf16[128,2048]{1,0:T(8,128)(2,1)S(1)}, bf16[128,2048]{1,0:T(8,128)(2,1)S(1)}, u32[]{:S(2)}, u32[]{:S(2)}) collective-permute-start(bf16[128,2048]{1,0:T(8,128)(2,1)S(1)} %get-tuple-element.65), channel_id=1, source_target_pairs={{0,16},{16,0},{32,48},{48,32},{64,80},{80,64},{96,112},{112,96},{1... | collective-permute-start | bytes 1572872 | tf_op jit(solution)/shard_map/ppermute | solution.py:541
  95.4 2.9 %collective-permute-start.13 = (bf16[128,2048]{1,0:T(8,128)(2,1)S(1)}, bf16[128,2048]{1,0:T(8,128)(2,1)S(1)}, u32[]{:S(2)}, u32[]{:S(2)}) collective-permute-start(bf16[128,2048]{1,0:T(8,128)(2,1)S(1)} %get-tuple-element.66), channel_id=1, source_target_pairs={{0,16},{16,0},{32,48},{48,32},{64,80},{80,64},{96,112},{112,96},{1... | collective-permute-start | bytes 1572872 | tf_op jit(solution)/shard_map/ppermute | solution.py:541
  95.4 3.6 %collective-permute-start.14 = (bf16[128,2048]{1,0:T(8,128)(2,1)S(1)}, bf16[128,2048]{1,0:T(8,128)(2,1)S(1)}, u32[]{:S(2)}, u32[]{:S(2)}) collective-permute-start(bf16[128,2048]{1,0:T(8,128)(2,1)S(1)} %get-tuple-element.67), channel_id=1, source_target_pairs={{0,16},{16,0},{32,48},{48,32},{64,80},{80,64},{96,112},{112,96},{1... | collective-permute-start | bytes 1572872 | tf_op jit(solution)/shard_map/ppermute | solution.py:541
  101.2 32.2 %collective-permute-start.16 = (bf16[64,8192]{1,0:T(8,128)(2,1)}, bf16[64,8192]{1,0:T(8,128)(2,1)}, u32[]{:S(2)}, u32[]{:S(2)}) collective-permute-start(bf16[64,8192]{1,0:T(8,128)(2,1)} %get-tuple-element.68), channel_id=1, source_target_pairs={{0,32},{16,112},{32,0},{48,80},{64,96},{80,48},{96,64},{112,16},{1... | collective-permute-start | bytes 3145736 | tf_op jit(solution)/shard_map/ppermute | solution.py:561
  102.9 11.0 %copy-start.2 = (bf16[96,8192]{1,0:T(8,128)(2,1)S(1)}, bf16[96,8192]{1,0:T(8,128)(2,1)}, u32[]{:S(2)}) copy-start(bf16[96,8192]{1,0:T(8,128)(2,1)} %get-tuple-element.62.refs_0_) | copy-start | bytes 4718596
  102.9 24.0 %all-to-all-start.2 = ((bf16[16,48,512]{2,1,0:T(8,128)(2,1)}), bf16[16,48,512]{2,1,0:T(8,128)(2,1)}, u32[]{:S(2)}, u32[]{:S(2)}) async-start(bf16[16,48,512]{2,1,0:T(8,128)(2,1)} %finish.2), calls=%async_computation.2 | async-start | bytes 1572864 | tf_op jit(solution)/shard_map/all_to_all | solution.py:563
  115.0 29.3 %collective-permute-start.15 = (bf16[48,8192]{1,0:T(8,128)(2,1)}, bf16[48,8192]{1,0:T(8,128)(2,1)}, u32[]{:S(2)}, u32[]{:S(2)}) collective-permute-start(bf16[48,8192]{1,0:T(8,128)(2,1)} %add_convert_fusion), channel_id=1, source_target_pairs={{0,96},{16,48},{32,64},{48,16},{64,32},{80,112},{96,0},{112,80},{1... | collective-permute-start | bytes 2359304 | tf_op jit(solution)/shard_map/ppermute | solution.py:546
  129.1 19.6 %all-to-all-start.3 = ((bf16[16,48,512]{2,1,0:T(8,128)(2,1)}), bf16[16,48,512]{2,1,0:T(8,128)(2,1)}, u32[]{:S(2)}, u32[]{:S(2)}) async-start(bf16[16,48,512]{2,1,0:T(8,128)(2,1)} %prefix.2), calls=%async_computation.3 | async-start | bytes 1572864 | tf_op jit(solution)/shard_map/all_to_all | solution.py:566
  133.3 10.9 %copy-start.5 = (bf16[64,8192]{1,0:T(8,128)(2,1)S(1)}, bf16[64,8192]{1,0:T(8,128)(2,1)}, u32[]{:S(2)}) copy-start(bf16[64,8192]{1,0:T(8,128)(2,1)} %get-tuple-element.71.refs_3_) | copy-start | bytes 3145732
  134.8 9.5 %collective-permute-start.17 = (bf16[32,8192]{1,0:T(8,128)(2,1)S(1)}, bf16[32,8192]{1,0:T(8,128)(2,1)S(1)}, u32[]{:S(2)}, u32[]{:S(2)}) collective-permute-start(bf16[32,8192]{1,0:T(8,128)(2,1)S(1)} %add_convert_fusion.2), channel_id=1, source_target_pairs={{0,96},{16,48},{32,64},{48,16},{64,32},{80,112},{96,0},{112,80},{1... | collective-permute-start | bytes 1572872 | tf_op jit(solution)/shard_map/ppermute | solution.py:546
  174.1 21.4 %all-to-all-start.5 = ((bf16[16,80,512]{2,1,0:T(8,128)(2,1)}), bf16[16,80,512]{2,1,0:T(8,128)(2,1)S(1)}, u32[]{:S(2)}, u32[]{:S(2)}) async-start(bf16[16,80,512]{2,1,0:T(8,128)(2,1)} %prefix.3), calls=%async_computation.5 | async-start | bytes 2621440 | tf_op jit(solution)/shard_map/all_to_all | solution.py:570
  (2 other events, 7.7 us)

commit v4 on v3

--- a/solution.py
+++ b/solution.py
@@ -280,7 +280,7 @@
     return pl.pallas_call(
         project_kernel,
         out_shape=tuple(
-            pltpu.VMEM((half, model // PIECES), jnp.bfloat16) for _ in range(PIECES)
+            jax.ShapeDtypeStruct((half, model // PIECES), jnp.bfloat16) for _ in range(PIECES)
         )
         + (pltpu.HBM((half, model), jnp.bfloat16),),
         grid=(tiles,),
@@ -557,11 +557,11 @@
     kept_c, pieces_c, token_c = project_chunk(context_c, next_a)
     kept_b, sent_b = join(after(kept_b, token_c, second_a), pieces_b)
     first_b = lax.ppermute(sent_b, "seq", to_first)
-    kept_c, sent_c = join(kept_c, pieces_c)
+    term_a = finish(layers, (kept_a, first_a, after(second_a, sent_b)))
+    terms_a = lax.all_to_all(term_a, "pipe", 0, 0)
+    kept_c, sent_c = join(after(kept_c, term_a), pieces_c)
     first_c = lax.ppermute(sent_c, "seq", to_first)
-    term_a = finish(layers, (kept_a, first_a, after(second_a, sent_c)))
-    terms_a = lax.all_to_all(term_a, "pipe", 0, 0)
-    second_b, next_b = reduce_next(kept_b, first_b, term_a)
+    second_b, next_b = reduce_next(kept_b, first_b, sent_c)
     prefix_a = prefix(after(terms_a, next_b), terms_a.shape[1])
     sums_a = lax.all_to_all(prefix_a, "pipe", 0, 0)
     second_c, next_c = reduce_next(kept_c, first_c, next_b)

time: 199 us -> 197 us (0.990)
  waiting for transfers between devices: 59.1 us -> 51.7 us
    all_to_all x1, waiting for transfers between devices: 10.1 us -> 3.45 us  [local(): terms_a = lax.all_to_all(term_a, 'pipe', 0, 0)]
    ppermute x1, waiting for transfers between devices: 0.01 us -> 6.52 us  [local(): first_c = lax.ppermute(sent_c, 'seq', to_first)]
    ppermute x12, waiting for transfers between devices: 3.16 us -> 0.03 us  [project_chunk(): lax.ppermute(piece, 'seq', to_core)]
  transfers between devices with their start and end apart: 23 -> 23, of which waited for: 12 -> 7; matrix products, arithmetic and copies ran while one was open for 1% -> 1% of each run, Pallas kernels for 31% -> 32%
where the time goes in v4:
time: 197 us; the launch traced here: 195 us
  Pallas kernels  76.2 us (39%)
  waiting for transfers between devices  51.7 us (26%)
  starting transfers between devices  37.9 us (19%)
  blocking collectives  24 us (12%)
  other arithmetic  2.72 us (1%)
  local copies, waits for them, and re-layouts  1.97 us (1%)
    pallas_call x3, Pallas kernels, project(): pl.pallas_call(project_kernel, out_shape=tuple((jax.ShapeDtypeStruct((hal...  33.2 us
    all_to_all x1, blocking collectives, local(): terms_bc = lax.all_to_all(after(term_bc, sums_a), 'pipe', 0, 0)  24 us
    all_to_all x1, waiting for transfers between devices, local(): lead_block = lax.all_to_all(lead_block, 'seq', 0, 0)  14.9 us
    pallas_call x3, Pallas kernels, attention(): pl.pallas_call(functools.partial(context_kernel, lead, segments, part_row...  14.4 us
    all_to_all x1, waiting for transfers between devices, local(): sums_bc = lax.all_to_all(prefix(terms_bc, terms_bc.shape[1]), 'pipe', 0, 0)  12.5 us
    pallas_call x3, Pallas kernels, join(): pl.pallas_call(join_kernel, out_shape=(half, half), grid=(pieces,), in_sp...  10.7 us
    all_to_all x1, starting transfers between devices, local(): terms_a = lax.all_to_all(term_a, 'pipe', 0, 0)  8.09 us
    ppermute x3, waiting for transfers between devices, reduce_next(): return (lax.ppermute(to_send, 'seq', to_second), to_send)  7.17 us
  transfers between devices with their start and end apart: 23, of which 7 were waited for; matrix products, arithmetic and copies ran while one was open for 1% of the time, Pallas kernels for 32%

profile of v4, /device:TPU:2, one launch (start us, length us, event | category | flops | bytes accessed | tf_op | source)
XLA Modules:
  0.0 194.8 jit_solution(13014734101864858002)
XLA Ops:
  0.0 2.3 %pack_lead.1 = bf16[8,80,1024]{2,1,0:T(8,128)(2,1)} custom-call(bf16[128,8192]{1,0:T(8,128)(2,1)} %bitcast.16, bf16[128,1024]{1,0:T(8,128)(2,1)} %bitcast.18, bf16[128,1024]{1,0:T(8,128)(2,1)} %bitcast.19), custom_call_target="tpu_custom_call" | custom-call | tf_op jit(solution)/shard_map/pack_lead/pallas_call | solution.py:47
  2.3 4.8 %all-to-all-start = ((bf16[8,80,1024]{2,1,0:T(8,128)(2,1)}), bf16[8,80,1024]{2,1,0:T(8,128)(2,1)S(1)}, u32[]{:S(2)}, u32[]{:S(2)}) async-start(bf16[8,80,1024]{2,1,0:T(8,128)(2,1)} %pack_lead.1), calls=%async_computation | async-start | bytes 2621440 | tf_op jit(solution)/shard_map/all_to_all | solution.py:516
  7.1 2.4 %pack_rest.1 = bf16[8,80,1024]{2,1,0:T(8,128)(2,1)} custom-call(bf16[128,8192]{1,0:T(8,128)(2,1)} %bitcast.17), custom_call_target="tpu_custom_call" | custom-call | tf_op jit(solution)/shard_map/pack_rest/pallas_call | solution.py:73
  9.5 14.9 %all-to-all-done.q_ref.kv_ref = bf16[8,80,1024]{2,1,0:T(8,128)(2,1)S(1)} async-done(((bf16[8,80,1024]{2,1,0:T(8,128)(2,1)}), bf16[8,80,1024]{2,1,0:T(8,128)(2,1)S(1)}, u32[]{:S(2)}, u32[]{:S(2)}) %all-to-all-start) | async-done | bytes 1310752 | tf_op jit(solution)/shard_map/all_to_all | solution.py:516
  24.4 4.9 %all-to-all-start.1 = ((bf16[8,80,1024]{2,1,0:T(8,128)(2,1)}), bf16[8,80,1024]{2,1,0:T(8,128)(2,1)S(1)}, u32[]{:S(2)}, u32[]{:S(2)}) async-start(bf16[8,80,1024]{2,1,0:T(8,128)(2,1)} %pack_rest.1), calls=%async_computation.1 | async-start | bytes 2621440 | tf_op jit(solution)/shard_map/all_to_all | solution.py:518
  29.8 5.0 %attention.3.context_ref = bf16[8,48,1024]{2,1,0:T(8,128)(2,1)S(1)} custom-call(s32[8]{0:T(128)S(1)} %pad_add_fusion.order_ref, s32[4]{0:T(128)S(1)} %copy-done.8, s32[8,4]{1,0:T(8,128)S(1)} %copy.11.vert_ref, s32[8,4]{1,0:T(8,128)S(1)} %copy.12.slash_ref, bf16[8,80,1024]{2,1,0:T(8,128)(2,1)S(1)} %all-to-all-done.q_ref.kv_ref, ...), custom_call_target="tpu_custom_call" | custom-call | tf_op jit(solution)/shard_map/attention/pallas_call | solution.py:202
  34.7 12.1 %project.3 = (bf16[192,2048]{1,0:T(8,128)(2,1)}, bf16[192,2048]{1,0:T(8,128)(2,1)}, bf16[192,2048]{1,0:T(8,128)(2,1)}, bf16[192,2048]{1,0:T(8,128)(2,1)}, bf16[192,8192]{1,0:T(8,128)(2,1)}) custom-call(bf16[8,48,1024]{2,1,0:T(8,128)(2,1)S(1)} %attention.3.context_ref, bf16[1024,8192]{1,0:T(8,128)(2,1)} %bitcast.13), custom_call_target="tpu_custom_call" | custom-call | tf_op jit(solution)/shard_map/project/pallas_call | solution.py:280
  48.0 5.0 %attention.4.context_ref = bf16[8,48,1024]{2,1,0:T(8,128)(2,1)S(1)} custom-call(s32[8]{0:T(128)S(1)} %pad_add_fusion.order_ref, s32[4]{0:T(128)S(1)} %copy-done.8, s32[8,4]{1,0:T(8,128)S(1)} %copy.11.vert_ref, s32[8,4]{1,0:T(8,128)S(1)} %copy.12.slash_ref, bf16[8,80,1024]{2,1,0:T(8,128)(2,1)S(1)} %all-to-all-done.1.q_ref, ...), custom_call_target="tpu_custom_call" | custom-call | tf_op jit(solution)/shard_map/attention/pallas_call | solution.py:202
  53.0 4.2 %join.3 = (bf16[96,8192]{1,0:T(8,128)(2,1)}, bf16[96,8192]{1,0:T(8,128)(2,1)}) custom-call(bf16[192,8192]{1,0:T(8,128)(2,1)S(1)} %copy-done.4, bf16[192,2048]{1,0:T(8,128)(2,1)} %collective-permute-done.refs_0_, bf16[192,2048]{1,0:T(8,128)(2,1)S(1)} %collective-permute-done.1.refs_1_, bf16[192,2048]{1,0:T(8,128)(2,1)} %collective-permute-done.2.refs_2_, ...), custom_call_target="tpu_custom_call" | custom-call | tf_op jit(solution)/shard_map/join/pallas_call | solution.py:322
  57.4 11.5 %project.4 = (bf16[192,2048]{1,0:T(8,128)(2,1)S(1)}, bf16[192,2048]{1,0:T(8,128)(2,1)S(1)}, bf16[192,2048]{1,0:T(8,128)(2,1)S(1)}, bf16[192,2048]{1,0:T(8,128)(2,1)S(1)}, bf16[192,8192]{1,0:T(8,128)(2,1)}) custom-call(bf16[8,48,1024]{2,1,0:T(8,128)(2,1)S(1)} %attention.4.context_ref, bf16[1024,8192]{1,0:T(8,128)(2,1)} %bitcast.14), custom_call_target="tpu_custom_call" | custom-call | tf_op jit(solution)/shard_map/project/pallas_call | solution.py:280
  68.9 4.5 %attention.5.context_ref = bf16[8,32,1024]{2,1,0:T(8,128)(2,1)S(1)} custom-call(s32[8]{0:T(128)S(1)} %pad_add_fusion.order_ref, s32[4]{0:T(128)S(1)} %copy-done.8, s32[8,4]{1,0:T(8,128)S(1)} %copy.11.vert_ref, s32[8,4]{1,0:T(8,128)S(1)} %copy.12.slash_ref, bf16[8,80,1024]{2,1,0:T(8,128)(2,1)S(1)} %all-to-all-done.1.q_ref, ...), custom_call_target="tpu_custom_call" | custom-call | tf_op jit(solution)/shard_map/attention/pallas_call | solution.py:202
  73.5 4.4 %collective-permute-done.4.refs_1_ = bf16[96,8192]{1,0:T(8,128)(2,1)S(1)} collective-permute-done((bf16[96,8192]{1,0:T(8,128)(2,1)}, bf16[96,8192]{1,0:T(8,128)(2,1)S(1)}, u32[]{:S(2)}, u32[]{:S(2)}) %collective-permute-start.4) | collective-permute-done | bytes 1572896 | tf_op jit(solution)/shard_map/ppermute | solution.py:553
  80.7 9.6 %project.5 = (bf16[128,2048]{1,0:T(8,128)(2,1)}, bf16[128,2048]{1,0:T(8,128)(2,1)}, bf16[128,2048]{1,0:T(8,128)(2,1)}, bf16[128,2048]{1,0:T(8,128)(2,1)}, bf16[128,8192]{1,0:T(8,128)(2,1)}) custom-call(bf16[8,32,1024]{2,1,0:T(8,128)(2,1)S(1)} %attention.5.context_ref, bf16[1024,8192]{1,0:T(8,128)(2,1)} %bitcast.15), custom_call_target="tpu_custom_call" | custom-call | tf_op jit(solution)/shard_map/project/pallas_call | solution.py:280
  90.3 2.7 %join.4 = (bf16[96,8192]{1,0:T(8,128)(2,1)}, bf16[96,8192]{1,0:T(8,128)(2,1)}) custom-call(bf16[192,8192]{1,0:T(8,128)(2,1)S(1)} %copy-done.3, bf16[192,2048]{1,0:T(8,128)(2,1)S(1)} %collective-permute-done.6.refs_0_, bf16[192,2048]{1,0:T(8,128)(2,1)S(1)} %collective-permute-done.7.refs_1_, bf16[192,2048]{1,0:T(8,128)(2,1)S(1)} %collective-permute-done.8.refs_2_, ...), custom_call_target="tpu_custom_call" | custom-call | tf_op jit(solution)/shard_map/join/pallas_call | solution.py:322
  93.0 1.7 collective-permute-start.10
  97.0 8.1 %all-to-all-start.2 = ((bf16[16,48,512]{2,1,0:T(8,128)(2,1)}), bf16[16,48,512]{2,1,0:T(8,128)(2,1)}, u32[]{:S(2)}, u32[]{:S(2)}) async-start(bf16[16,48,512]{2,1,0:T(8,128)(2,1)} %finish.2), calls=%async_computation.2 | async-start | bytes 1572864 | tf_op jit(solution)/shard_map/all_to_all | solution.py:561
  105.2 1.7 copy-done.6
  106.9 3.7 %join.5 = (bf16[64,8192]{1,0:T(8,128)(2,1)}, bf16[64,8192]{1,0:T(8,128)(2,1)}) custom-call(bf16[128,8192]{1,0:T(8,128)(2,1)S(1)} %copy-done.6, bf16[128,2048]{1,0:T(8,128)(2,1)} %collective-permute-done.11.refs_0_, bf16[128,2048]{1,0:T(8,128)(2,1)} %collective-permute-done.12.refs_1_, bf16[128,2048]{1,0:T(8,128)(2,1)} %collective-permute-done.13.refs_2_, ...), custom_call_target="tpu_custom_call" | custom-call | tf_op jit(solution)/shard_map/join/pallas_call | solution.py:322
  110.9 2.8 %collective-permute-done.10.refs_1_ = bf16[96,8192]{1,0:T(8,128)(2,1)S(1)} collective-permute-done((bf16[96,8192]{1,0:T(8,128)(2,1)}, bf16[96,8192]{1,0:T(8,128)(2,1)S(1)}, u32[]{:S(2)}, u32[]{:S(2)}) %collective-permute-start.10) | collective-permute-done | bytes 1572896 | tf_op jit(solution)/shard_map/ppermute | solution.py:559
  114.7 1.7 collective-permute-start.15
  116.4 3.4 %all-to-all-done.2.term_ref = bf16[16,48,512]{2,1,0:T(8,128)(2,1)} async-done(((bf16[16,48,512]{2,1,0:T(8,128)(2,1)}), bf16[16,48,512]{2,1,0:T(8,128)(2,1)}, u32[]{:S(2)}, u32[]{:S(2)}) %all-to-all-start.2) | async-done | bytes 786464 | tf_op jit(solution)/shard_map/all_to_all | solution.py:561
  119.8 2.1 %prefix.2 = bf16[16,48,512]{2,1,0:T(8,128)(2,1)} custom-call(bf16[16,48,512]{2,1,0:T(8,128)(2,1)} %all-to-all-done.2.term_ref), custom_call_target="tpu_custom_call" | custom-call | tf_op jit(solution)/shard_map/prefix/pallas_call | solution.py:402
  122.0 4.6 %all-to-all-start.3 = ((bf16[16,48,512]{2,1,0:T(8,128)(2,1)}), bf16[16,48,512]{2,1,0:T(8,128)(2,1)}, u32[]{:S(2)}, u32[]{:S(2)}) async-start(bf16[16,48,512]{2,1,0:T(8,128)(2,1)} %prefix.2), calls=%async_computation.3 | async-start | bytes 1572864 | tf_op jit(solution)/shard_map/all_to_all | solution.py:566
  126.7 6.5 %collective-permute-done.16.refs_4_ = bf16[64,8192]{1,0:T(8,128)(2,1)} collective-permute-done((bf16[64,8192]{1,0:T(8,128)(2,1)}, bf16[64,8192]{1,0:T(8,128)(2,1)}, u32[]{:S(2)}, u32[]{:S(2)}) %collective-permute-start.16) | collective-permute-done | bytes 1048608 | tf_op jit(solution)/shard_map/ppermute | solution.py:563
  134.5 3.0 %collective-permute-start.17 = (bf16[32,8192]{1,0:T(8,128)(2,1)S(1)}, bf16[32,8192]{1,0:T(8,128)(2,1)S(1)}, u32[]{:S(2)}, u32[]{:S(2)}) collective-permute-start(bf16[32,8192]{1,0:T(8,128)(2,1)S(1)} %add_convert_fusion.2), channel_id=1, source_target_pairs={{0,96},{16,48},{32,64},{48,16},{64,32},{80,112},{96,0},{112,80},{1... | collective-permute-start | bytes 1572872 | tf_op jit(solution)/shard_map/ppermute | solution.py:546
  137.5 7.2 %collective-permute-done.17.refs_5_ = bf16[32,8192]{1,0:T(8,128)(2,1)S(1)} collective-permute-done((bf16[32,8192]{1,0:T(8,128)(2,1)S(1)}, bf16[32,8192]{1,0:T(8,128)(2,1)S(1)}, u32[]{:S(2)}, u32[]{:S(2)}) %collective-permute-start.17) | collective-permute-done | bytes 524320 | tf_op jit(solution)/shard_map/ppermute | solution.py:546
  144.7 2.5 %finish.3 = bf16[16,80,512]{2,1,0:T(8,128)(2,1)} custom-call(bf16[96,8192]{1,0:T(8,128)(2,1)S(1)} %copy-done.2, bf16[96,8192]{1,0:T(8,128)(2,1)S(1)} %collective-permute-done.10.refs_1_, bf16[48,8192]{1,0:T(8,128)(2,1)} %collective-permute-done.15.refs_2_, bf16[64,8192]{1,0:T(8,128)(2,1)S(1)} %copy-done.5, bf16[64,8192]{1,0:T(8,128)(2,1)} %collective-permute-done.16.refs_4_, ...), custom_call_target="tpu_custom_call" | custom-call | tf_op jit(solution)/shard_map/finish/pallas_call | solution.py:378
  147.2 24.0 %all_to_all.30.term_ref = bf16[16,80,512]{2,1,0:T(8,128)(2,1)S(1)} all-to-all(bf16[16,80,512]{2,1,0:T(8,128)(2,1)} %finish.3), channel_id=1, replica_groups=mesh['seq'=8,'pipe'=16] {'pipe'}, dimensions={0} | all-to-all | bytes 2621440 | tf_op jit(solution)/shard_map/all_to_all | solution.py:569
  172.5 3.8 %all-to-all-start.5 = ((bf16[16,80,512]{2,1,0:T(8,128)(2,1)}), bf16[16,80,512]{2,1,0:T(8,128)(2,1)S(1)}, u32[]{:S(2)}, u32[]{:S(2)}) async-start(bf16[16,80,512]{2,1,0:T(8,128)(2,1)} %prefix.3), calls=%async_computation.5 | async-start | bytes 2621440 | tf_op jit(solution)/shard_map/all_to_all | solution.py:570
  176.3 3.2 %normalize.2.refs_0_ = bf16[128,8192]{1,0:T(8,128)(2,1)} custom-call(bf16[128,8192]{1,0:T(8,128)(2,1)S(1)} %copy-done, bf16[16,48,512]{2,1,0:T(8,128)(2,1)} %all-to-all-done.3.sums_ref, f32[1,8192]{1,0:T(1,128)S(1)} %copy-done.7), custom_call_target="tpu_custom_call" | custom-call | tf_op jit(solution)/shard_map/normalize/pallas_call | solution.py:454
  179.5 12.5 %all-to-all-done.5.sums_ref = bf16[16,80,512]{2,1,0:T(8,128)(2,1)S(1)} async-done(((bf16[16,80,512]{2,1,0:T(8,128)(2,1)}), bf16[16,80,512]{2,1,0:T(8,128)(2,1)S(1)}, u32[]{:S(2)}, u32[]{:S(2)}) %all-to-all-start.5) | async-done | bytes 1310752 | tf_op jit(solution)/shard_map/all_to_all | solution.py:570
  192.0 2.8 %normalize.3 = bf16[128,8192]{1,0:T(8,128)(2,1)} custom-call(bf16[128,8192]{1,0:T(8,128)(2,1)S(1)} %copy-done, bf16[16,80,512]{2,1,0:T(8,128)(2,1)S(1)} %all-to-all-done.5.sums_ref, f32[1,8192]{1,0:T(1,128)S(1)} %copy-done.7, bf16[128,8192]{1,0:T(8,128)(2,1)} %normalize.2.refs_0_), custom_call_target="tpu_custom_call", output_to_operand_aliasing={{}: (3, {})} | custom-call | tf_op jit(solution)/shard_map/normalize/pallas_call | solution.py:454
  (62 shorter events, 10.8 us)
Async XLA Ops:
  2.3 22.1 %all-to-all-start = ((bf16[8,80,1024]{2,1,0:T(8,128)(2,1)}), bf16[8,80,1024]{2,1,0:T(8,128)(2,1)S(1)}, u32[]{:S(2)}, u32[]{:S(2)}) async-start(bf16[8,80,1024]{2,1,0:T(8,128)(2,1)} %pack_lead.1), calls=%async_computation | async-start | bytes 2621440 | tf_op jit(solution)/shard_map/all_to_all | solution.py:516
  9.5 20.0 %copy-start.9 = (s32[1,64,4]{1,2,0:T(4,128)S(1)}, s32[1,64,4]{1,2,0:T(4,128)}, u32[]{:S(2)}) copy-start(s32[1,64,4]{1,2,0:T(4,128)} %param.13) | copy-start | bytes 3076
  9.5 20.0 %copy-start.10 = (s32[1,64,4]{1,2,0:T(4,128)S(1)}, s32[1,64,4]{1,2,0:T(4,128)}, u32[]{:S(2)}) copy-start(s32[1,64,4]{1,2,0:T(4,128)} %param.12) | copy-start | bytes 3076
  9.5 20.2 %copy-start.8 = (s32[4]{0:T(128)S(1)}, s32[4]{0:T(128)}, u32[]{:S(2)}) copy-start(s32[4]{0:T(128)} %lengths_ref.5) | copy-start | bytes 52
  24.4 23.5 %all-to-all-start.1 = ((bf16[8,80,1024]{2,1,0:T(8,128)(2,1)}), bf16[8,80,1024]{2,1,0:T(8,128)(2,1)S(1)}, u32[]{:S(2)}, u32[]{:S(2)}) async-start(bf16[8,80,1024]{2,1,0:T(8,128)(2,1)} %pack_rest.1), calls=%async_computation.1 | async-start | bytes 2621440 | tf_op jit(solution)/shard_map/all_to_all | solution.py:518
  46.9 6.1 %collective-permute-start.1 = (bf16[192,2048]{1,0:T(8,128)(2,1)}, bf16[192,2048]{1,0:T(8,128)(2,1)S(1)}, u32[]{:S(2)}, u32[]{:S(2)}) collective-permute-start(bf16[192,2048]{1,0:T(8,128)(2,1)} %get-tuple-element.47), channel_id=1, source_target_pairs={{0,16},{16,0},{32,48},{48,32},{64,80},{80,64},{96,112},{112,96},{1... | collective-permute-start | bytes 2359304 | tf_op jit(solution)/shard_map/ppermute | solution.py:541
  47.1 5.9 %collective-permute-start.2 = (bf16[192,2048]{1,0:T(8,128)(2,1)}, bf16[192,2048]{1,0:T(8,128)(2,1)}, u32[]{:S(2)}, u32[]{:S(2)}) collective-permute-start(bf16[192,2048]{1,0:T(8,128)(2,1)} %get-tuple-element.48), channel_id=1, source_target_pairs={{0,16},{16,0},{32,48},{48,32},{64,80},{80,64},{96,112},{112,96},{1... | collective-permute-start | bytes 2359304 | tf_op jit(solution)/shard_map/ppermute | solution.py:541
  47.5 5.5 %collective-permute-start.3 = (bf16[192,2048]{1,0:T(8,128)(2,1)}, bf16[192,2048]{1,0:T(8,128)(2,1)}, u32[]{:S(2)}, u32[]{:S(2)}) collective-permute-start(bf16[192,2048]{1,0:T(8,128)(2,1)} %get-tuple-element.49), channel_id=1, source_target_pairs={{0,16},{16,0},{32,48},{48,32},{64,80},{80,64},{96,112},{112,96},{1... | collective-permute-start | bytes 2359304 | tf_op jit(solution)/shard_map/ppermute | solution.py:541
  47.6 5.4 %collective-permute-start = (bf16[192,2048]{1,0:T(8,128)(2,1)}, bf16[192,2048]{1,0:T(8,128)(2,1)}, u32[]{:S(2)}, u32[]{:S(2)}) collective-permute-start(bf16[192,2048]{1,0:T(8,128)(2,1)} %get-tuple-element.41), channel_id=1, source_target_pairs={{0,16},{16,0},{32,48},{48,32},{64,80},{80,64},{96,112},{112,96},{1... | collective-permute-start | bytes 2359304 | tf_op jit(solution)/shard_map/ppermute | solution.py:541
  48.0 5.0 %copy-start.4 = (bf16[192,8192]{1,0:T(8,128)(2,1)S(1)}, bf16[192,8192]{1,0:T(8,128)(2,1)}, u32[]{:S(2)}) copy-start(bf16[192,8192]{1,0:T(8,128)(2,1)} %get-tuple-element.46.kept_ref) | copy-start | bytes 9437188
  57.2 20.6 %collective-permute-start.4 = (bf16[96,8192]{1,0:T(8,128)(2,1)}, bf16[96,8192]{1,0:T(8,128)(2,1)S(1)}, u32[]{:S(2)}, u32[]{:S(2)}) collective-permute-start(bf16[96,8192]{1,0:T(8,128)(2,1)} %get-tuple-element.50), channel_id=1, source_target_pairs={{0,32},{16,112},{32,0},{48,80},{64,96},{80,48},{96,64},{112,16},{1... | collective-permute-start | bytes 4718600 | tf_op jit(solution)/shard_map/ppermute | solution.py:553
  68.9 9.0 %copy-start.1 = (bf16[96,8192]{1,0:T(8,128)(2,1)S(1)}, bf16[96,8192]{1,0:T(8,128)(2,1)}, u32[]{:S(2)}) copy-start(bf16[96,8192]{1,0:T(8,128)(2,1)} %get-tuple-element.55.refs_0_) | copy-start | bytes 4718596
  78.1 12.2 %collective-permute-start.5 = (bf16[48,8192]{1,0:T(8,128)(2,1)S(1)}, bf16[48,8192]{1,0:T(8,128)(2,1)S(1)}, u32[]{:S(2)}, u32[]{:S(2)}) collective-permute-start(bf16[48,8192]{1,0:T(8,128)(2,1)S(1)} %add_convert_fusion.1), channel_id=1, source_target_pairs={{0,96},{16,48},{32,64},{48,16},{64,32},{80,112},{96,0},{112,80},{1... | collective-permute-start | bytes 2359304 | tf_op jit(solution)/shard_map/ppermute | solution.py:546
  79.6 10.7 %collective-permute-start.7 = (bf16[192,2048]{1,0:T(8,128)(2,1)S(1)}, bf16[192,2048]{1,0:T(8,128)(2,1)S(1)}, u32[]{:S(2)}, u32[]{:S(2)}) collective-permute-start(bf16[192,2048]{1,0:T(8,128)(2,1)S(1)} %get-tuple-element.60), channel_id=1, source_target_pairs={{0,16},{16,0},{32,48},{48,32},{64,80},{80,64},{96,112},{112,96},{1... | collective-permute-start | bytes 2359304 | tf_op jit(solution)/shard_map/ppermute | solution.py:541
  79.6 10.7 %collective-permute-start.8 = (bf16[192,2048]{1,0:T(8,128)(2,1)S(1)}, bf16[192,2048]{1,0:T(8,128)(2,1)S(1)}, u32[]{:S(2)}, u32[]{:S(2)}) collective-permute-start(bf16[192,2048]{1,0:T(8,128)(2,1)S(1)} %get-tuple-element.61), channel_id=1, source_target_pairs={{0,16},{16,0},{32,48},{48,32},{64,80},{80,64},{96,112},{112,96},{1... | collective-permute-start | bytes 2359304 | tf_op jit(solution)/shard_map/ppermute | solution.py:541
  80.1 10.2 %collective-permute-start.9 = (bf16[192,2048]{1,0:T(8,128)(2,1)S(1)}, bf16[192,2048]{1,0:T(8,128)(2,1)S(1)}, u32[]{:S(2)}, u32[]{:S(2)}) collective-permute-start(bf16[192,2048]{1,0:T(8,128)(2,1)S(1)} %get-tuple-element.62), channel_id=1, source_target_pairs={{0,16},{16,0},{32,48},{48,32},{64,80},{80,64},{96,112},{112,96},{1... | collective-permute-start | bytes 2359304 | tf_op jit(solution)/shard_map/ppermute | solution.py:541
  80.1 10.2 %collective-permute-start.6 = (bf16[192,2048]{1,0:T(8,128)(2,1)S(1)}, bf16[192,2048]{1,0:T(8,128)(2,1)S(1)}, u32[]{:S(2)}, u32[]{:S(2)}) collective-permute-start(bf16[192,2048]{1,0:T(8,128)(2,1)S(1)} %get-tuple-element.53), channel_id=1, source_target_pairs={{0,16},{16,0},{32,48},{48,32},{64,80},{80,64},{96,112},{112,96},{1... | collective-permute-start | bytes 2359304 | tf_op jit(solution)/shard_map/ppermute | solution.py:541
  80.7 9.7 %copy-start.3 = (bf16[192,8192]{1,0:T(8,128)(2,1)S(1)}, bf16[192,8192]{1,0:T(8,128)(2,1)}, u32[]{:S(2)}) copy-start(bf16[192,8192]{1,0:T(8,128)(2,1)} %get-tuple-element.59.kept_ref) | copy-start | bytes 9437188
  93.0 20.6 %collective-permute-start.10 = (bf16[96,8192]{1,0:T(8,128)(2,1)}, bf16[96,8192]{1,0:T(8,128)(2,1)S(1)}, u32[]{:S(2)}, u32[]{:S(2)}) collective-permute-start(bf16[96,8192]{1,0:T(8,128)(2,1)} %get-tuple-element.64), channel_id=1, source_target_pairs={{0,32},{16,112},{32,0},{48,80},{64,96},{80,48},{96,64},{112,16},{1... | collective-permute-start | bytes 4718600 | tf_op jit(solution)/shard_map/ppermute | solution.py:559
  94.8 10.4 %collective-permute-start.12 = (bf16[128,2048]{1,0:T(8,128)(2,1)}, bf16[128,2048]{1,0:T(8,128)(2,1)}, u32[]{:S(2)}, u32[]{:S(2)}) collective-permute-start(bf16[128,2048]{1,0:T(8,128)(2,1)} %get-tuple-element.68), channel_id=1, source_target_pairs={{0,16},{16,0},{32,48},{48,32},{64,80},{80,64},{96,112},{112,96},{1... | collective-permute-start | bytes 1572872 | tf_op jit(solution)/shard_map/ppermute | solution.py:541
  94.8 10.4 %collective-permute-start.13 = (bf16[128,2048]{1,0:T(8,128)(2,1)}, bf16[128,2048]{1,0:T(8,128)(2,1)}, u32[]{:S(2)}, u32[]{:S(2)}) collective-permute-start(bf16[128,2048]{1,0:T(8,128)(2,1)} %get-tuple-element.69), channel_id=1, source_target_pairs={{0,16},{16,0},{32,48},{48,32},{64,80},{80,64},{96,112},{112,96},{1... | collective-permute-start | bytes 1572872 | tf_op jit(solution)/shard_map/ppermute | solution.py:541
  95.3 9.9 %collective-permute-start.14 = (bf16[128,2048]{1,0:T(8,128)(2,1)}, bf16[128,2048]{1,0:T(8,128)(2,1)}, u32[]{:S(2)}, u32[]{:S(2)}) collective-permute-start(bf16[128,2048]{1,0:T(8,128)(2,1)} %get-tuple-element.70), channel_id=1, source_target_pairs={{0,16},{16,0},{32,48},{48,32},{64,80},{80,64},{96,112},{112,96},{1... | collective-permute-start | bytes 1572872 | tf_op jit(solution)/shard_map/ppermute | solution.py:541
  95.3 9.9 %collective-permute-start.11 = (bf16[128,2048]{1,0:T(8,128)(2,1)}, bf16[128,2048]{1,0:T(8,128)(2,1)}, u32[]{:S(2)}, u32[]{:S(2)}) collective-permute-start(bf16[128,2048]{1,0:T(8,128)(2,1)} %get-tuple-element.58), channel_id=1, source_target_pairs={{0,16},{16,0},{32,48},{48,32},{64,80},{80,64},{96,112},{112,96},{1... | collective-permute-start | bytes 1572872 | tf_op jit(solution)/shard_map/ppermute | solution.py:541
  97.0 22.8 %all-to-all-start.2 = ((bf16[16,48,512]{2,1,0:T(8,128)(2,1)}), bf16[16,48,512]{2,1,0:T(8,128)(2,1)}, u32[]{:S(2)}, u32[]{:S(2)}) async-start(bf16[16,48,512]{2,1,0:T(8,128)(2,1)} %finish.2), calls=%async_computation.2 | async-start | bytes 1572864 | tf_op jit(solution)/shard_map/all_to_all | solution.py:561
  105.2 8.5 %copy-start.2 = (bf16[96,8192]{1,0:T(8,128)(2,1)S(1)}, bf16[96,8192]{1,0:T(8,128)(2,1)}, u32[]{:S(2)}) copy-start(bf16[96,8192]{1,0:T(8,128)(2,1)} %get-tuple-element.63.refs_0_) | copy-start | bytes 4718596
  110.6 22.6 %collective-permute-start.16 = (bf16[64,8192]{1,0:T(8,128)(2,1)}, bf16[64,8192]{1,0:T(8,128)(2,1)}, u32[]{:S(2)}, u32[]{:S(2)}) collective-permute-start(bf16[64,8192]{1,0:T(8,128)(2,1)} %get-tuple-element.71), channel_id=1, source_target_pairs={{0,32},{16,112},{32,0},{48,80},{64,96},{80,48},{96,64},{112,16},{1... | collective-permute-start | bytes 3145736 | tf_op jit(solution)/shard_map/ppermute | solution.py:563
  114.7 30.0 %collective-permute-start.15 = (bf16[48,8192]{1,0:T(8,128)(2,1)}, bf16[48,8192]{1,0:T(8,128)(2,1)}, u32[]{:S(2)}, u32[]{:S(2)}) collective-permute-start(bf16[48,8192]{1,0:T(8,128)(2,1)} %add_convert_fusion), channel_id=1, source_target_pairs={{0,96},{16,48},{32,64},{48,16},{64,32},{80,112},{96,0},{112,80},{1... | collective-permute-start | bytes 2359304 | tf_op jit(solution)/shard_map/ppermute | solution.py:546
  122.0 25.2 %all-to-all-start.3 = ((bf16[16,48,512]{2,1,0:T(8,128)(2,1)}), bf16[16,48,512]{2,1,0:T(8,128)(2,1)}, u32[]{:S(2)}, u32[]{:S(2)}) async-start(bf16[16,48,512]{2,1,0:T(8,128)(2,1)} %prefix.2), calls=%async_computation.3 | async-start | bytes 1572864 | tf_op jit(solution)/shard_map/all_to_all | solution.py:566
  126.6 18.0 %copy-start.5 = (bf16[64,8192]{1,0:T(8,128)(2,1)S(1)}, bf16[64,8192]{1,0:T(8,128)(2,1)}, u32[]{:S(2)}) copy-start(bf16[64,8192]{1,0:T(8,128)(2,1)} %get-tuple-element.73.refs_3_) | copy-start | bytes 3145732
  134.5 10.2 %collective-permute-start.17 = (bf16[32,8192]{1,0:T(8,128)(2,1)S(1)}, bf16[32,8192]{1,0:T(8,128)(2,1)S(1)}, u32[]{:S(2)}, u32[]{:S(2)}) collective-permute-start(bf16[32,8192]{1,0:T(8,128)(2,1)S(1)} %add_convert_fusion.2), channel_id=1, source_target_pairs={{0,96},{16,48},{32,64},{48,16},{64,32},{80,112},{96,0},{112,80},{1... | collective-permute-start | bytes 1572872 | tf_op jit(solution)/shard_map/ppermute | solution.py:546
  172.5 3.9 %copy-start.7 = (f32[1,8192]{1,0:T(1,128)S(1)}, f32[1,8192]{1,0:T(1,128)}, u32[]{:S(2)}) copy-start(f32[1,8192]{1,0:T(1,128)} %gain_ref.3) | copy-start | bytes 98308
  172.5 19.5 %all-to-all-start.5 = ((bf16[16,80,512]{2,1,0:T(8,128)(2,1)}), bf16[16,80,512]{2,1,0:T(8,128)(2,1)S(1)}, u32[]{:S(2)}, u32[]{:S(2)}) async-start(bf16[16,80,512]{2,1,0:T(8,128)(2,1)} %prefix.3), calls=%async_computation.5 | async-start | bytes 2621440 | tf_op jit(solution)/shard_map/all_to_all | solution.py:570
  (2 other events, 5.6 us)

commit v5 on v4

--- a/solution.py
+++ b/solution.py
@@ -21,6 +21,7 @@
 COLUMNS = 1024
 AHEAD = 4
 FETCHES = 2
+JOIN_TILES = 2
 NEG = -1e30
 COST = pl.CostEstimate(flops=0, transcendentals=0, bytes_accessed=0)
 PARAMS = pltpu.CompilerParams(vmem_limit_bytes=16 << 20)
@@ -304,7 +305,7 @@
     rows = keep_ref.shape[0]
     for piece, arrived_ref in enumerate(arrived_refs):
 
-        @pl.when(pl.program_id(0) == piece)
+        @pl.when(lax.div(pl.program_id(0), JOIN_TILES) == piece)
         def _():
             total = kept_ref[...].astype(jnp.float32) + arrived_ref[...].astype(jnp.float32)
             total = total.astype(jnp.bfloat16)
@@ -315,15 +316,21 @@
 def join(kept, arrived):
     rows, model = kept.shape
     pieces = len(arrived)
-    columns = model // pieces
+    columns = model // pieces // JOIN_TILES
     half = pltpu.HBM((rows // 2, model), jnp.bfloat16)
     half_spec = pl.BlockSpec((rows // 2, columns), lambda n: (0, n))
-    whole = pl.BlockSpec((rows, columns), lambda n: (0, 0))
+
+    def piece_spec(piece):
+        return pl.BlockSpec(
+            (rows, columns), lambda n: (0, jnp.clip(n - piece * JOIN_TILES, 0, JOIN_TILES - 1))
+        )
+
     return pl.pallas_call(
         join_kernel,
         out_shape=(half, half),
-        grid=(pieces,),
-        in_specs=[pl.BlockSpec((rows, columns), lambda n: (0, n))] + [whole] * pieces,
+        grid=(pieces * JOIN_TILES,),
+        in_specs=[pl.BlockSpec((rows, columns), lambda n: (0, n))]
+        + [piece_spec(piece) for piece in range(pieces)],
         out_specs=(half_spec, half_spec),
         compiler_params=PARAMS,
         cost_estimate=COST,

time: 197 us -> 202 us (1.025)
  Pallas kernels: 76.2 us -> 82.1 us
    pallas_call x3, Pallas kernels: 10.7 us -> 16.6 us  [join(): pl.pallas_call(join_kernel, out_shape=(half, half), grid=(pieces * JOIN_T...]
    ppermute x1, waiting for transfers between devices: 6.52 us -> 9.8 us  [local(): first_c = lax.ppermute(sent_c, 'seq', to_first)]
    ppermute x1, waiting for transfers between devices: 2.76 us -> 0.47 us  [local(): first_b = lax.ppermute(sent_b, 'seq', to_first)]
where the time goes in v5:
time: 202 us; the launch traced here: 201 us
  Pallas kernels  82.1 us (41%)
  waiting for transfers between devices  53.3 us (26%)
  starting transfers between devices  36.8 us (18%)
  blocking collectives  23.9 us (12%)
  other arithmetic  2.72 us (1%)
    pallas_call x3, Pallas kernels, project(): pl.pallas_call(project_kernel, out_shape=tuple((jax.ShapeDtypeStruct((hal...  33.2 us
    all_to_all x1, blocking collectives, local(): terms_bc = lax.all_to_all(after(term_bc, sums_a), 'pipe', 0, 0)  23.9 us
    pallas_call x3, Pallas kernels, join(): pl.pallas_call(join_kernel, out_shape=(half, half), grid=(pieces * JOIN_T...  16.6 us
    all_to_all x1, waiting for transfers between devices, local(): lead_block = lax.all_to_all(lead_block, 'seq', 0, 0)  14.9 us
    pallas_call x3, Pallas kernels, attention(): pl.pallas_call(functools.partial(context_kernel, lead, segments, part_row...  14.4 us
    all_to_all x1, waiting for transfers between devices, local(): sums_bc = lax.all_to_all(prefix(terms_bc, terms_bc.shape[1]), 'pipe', 0, 0)  12.8 us
    ppermute x1, waiting for transfers between devices, local(): first_c = lax.ppermute(sent_c, 'seq', to_first)  9.8 us
    all_to_all x1, starting transfers between devices, local(): terms_a = lax.all_to_all(term_a, 'pipe', 0, 0)  8.09 us
  transfers between devices with their start and end apart: 23, of which 7 were waited for; matrix products, arithmetic and copies ran while one was open for 1% of the time, Pallas kernels for 32%

profile of v5, /device:TPU:2, one launch (start us, length us, event | category | flops | bytes accessed | tf_op | source)
XLA Modules:
  0.0 201.1 jit_solution(16216859502643197033)
XLA Ops:
  0.0 2.3 %pack_lead.1 = bf16[8,80,1024]{2,1,0:T(8,128)(2,1)} custom-call(bf16[128,8192]{1,0:T(8,128)(2,1)} %bitcast.16, bf16[128,1024]{1,0:T(8,128)(2,1)} %bitcast.18, bf16[128,1024]{1,0:T(8,128)(2,1)} %bitcast.19), custom_call_target="tpu_custom_call" | custom-call | tf_op jit(solution)/shard_map/pack_lead/pallas_call | solution.py:48
  2.3 4.8 %all-to-all-start = ((bf16[8,80,1024]{2,1,0:T(8,128)(2,1)}), bf16[8,80,1024]{2,1,0:T(8,128)(2,1)S(1)}, u32[]{:S(2)}, u32[]{:S(2)}) async-start(bf16[8,80,1024]{2,1,0:T(8,128)(2,1)} %pack_lead.1), calls=%async_computation | async-start | bytes 2621440 | tf_op jit(solution)/shard_map/all_to_all | solution.py:523
  7.1 2.4 %pack_rest.1 = bf16[8,80,1024]{2,1,0:T(8,128)(2,1)} custom-call(bf16[128,8192]{1,0:T(8,128)(2,1)} %bitcast.17), custom_call_target="tpu_custom_call" | custom-call | tf_op jit(solution)/shard_map/pack_rest/pallas_call | solution.py:74
  9.5 14.9 %all-to-all-done.q_ref.kv_ref = bf16[8,80,1024]{2,1,0:T(8,128)(2,1)S(1)} async-done(((bf16[8,80,1024]{2,1,0:T(8,128)(2,1)}), bf16[8,80,1024]{2,1,0:T(8,128)(2,1)S(1)}, u32[]{:S(2)}, u32[]{:S(2)}) %all-to-all-start) | async-done | bytes 1310752 | tf_op jit(solution)/shard_map/all_to_all | solution.py:523
  24.4 4.9 %all-to-all-start.1 = ((bf16[8,80,1024]{2,1,0:T(8,128)(2,1)}), bf16[8,80,1024]{2,1,0:T(8,128)(2,1)S(1)}, u32[]{:S(2)}, u32[]{:S(2)}) async-start(bf16[8,80,1024]{2,1,0:T(8,128)(2,1)} %pack_rest.1), calls=%async_computation.1 | async-start | bytes 2621440 | tf_op jit(solution)/shard_map/all_to_all | solution.py:525
  29.8 5.0 %attention.3.context_ref = bf16[8,48,1024]{2,1,0:T(8,128)(2,1)S(1)} custom-call(s32[8]{0:T(128)S(1)} %pad_add_fusion.order_ref, s32[4]{0:T(128)S(1)} %copy-done.8, s32[8,4]{1,0:T(8,128)S(1)} %copy.11.vert_ref, s32[8,4]{1,0:T(8,128)S(1)} %copy.12.slash_ref, bf16[8,80,1024]{2,1,0:T(8,128)(2,1)S(1)} %all-to-all-done.q_ref.kv_ref, ...), custom_call_target="tpu_custom_call" | custom-call | tf_op jit(solution)/shard_map/attention/pallas_call | solution.py:203
  34.8 12.1 %project.3 = (bf16[192,2048]{1,0:T(8,128)(2,1)}, bf16[192,2048]{1,0:T(8,128)(2,1)}, bf16[192,2048]{1,0:T(8,128)(2,1)}, bf16[192,2048]{1,0:T(8,128)(2,1)}, bf16[192,8192]{1,0:T(8,128)(2,1)}) custom-call(bf16[8,48,1024]{2,1,0:T(8,128)(2,1)S(1)} %attention.3.context_ref, bf16[1024,8192]{1,0:T(8,128)(2,1)} %bitcast.13), custom_call_target="tpu_custom_call" | custom-call | tf_op jit(solution)/shard_map/project/pallas_call | solution.py:281
  48.0 5.0 %attention.4.context_ref = bf16[8,48,1024]{2,1,0:T(8,128)(2,1)S(1)} custom-call(s32[8]{0:T(128)S(1)} %pad_add_fusion.order_ref, s32[4]{0:T(128)S(1)} %copy-done.8, s32[8,4]{1,0:T(8,128)S(1)} %copy.11.vert_ref, s32[8,4]{1,0:T(8,128)S(1)} %copy.12.slash_ref, bf16[8,80,1024]{2,1,0:T(8,128)(2,1)S(1)} %all-to-all-done.1.q_ref, ...), custom_call_target="tpu_custom_call" | custom-call | tf_op jit(solution)/shard_map/attention/pallas_call | solution.py:203
  53.0 6.3 %join.3 = (bf16[96,8192]{1,0:T(8,128)(2,1)}, bf16[96,8192]{1,0:T(8,128)(2,1)}) custom-call(bf16[192,8192]{1,0:T(8,128)(2,1)S(1)} %copy-done.4, bf16[192,2048]{1,0:T(8,128)(2,1)} %collective-permute-done.refs_0_, bf16[192,2048]{1,0:T(8,128)(2,1)S(1)} %collective-permute-done.1.refs_1_, bf16[192,2048]{1,0:T(8,128)(2,1)} %collective-permute-done.2.refs_2_, ...), custom_call_target="tpu_custom_call" | custom-call | tf_op jit(solution)/shard_map/join/pallas_call | solution.py:328
  59.5 11.5 %project.4 = (bf16[192,2048]{1,0:T(8,128)(2,1)S(1)}, bf16[192,2048]{1,0:T(8,128)(2,1)S(1)}, bf16[192,2048]{1,0:T(8,128)(2,1)S(1)}, bf16[192,2048]{1,0:T(8,128)(2,1)S(1)}, bf16[192,8192]{1,0:T(8,128)(2,1)}) custom-call(bf16[8,48,1024]{2,1,0:T(8,128)(2,1)S(1)} %attention.4.context_ref, bf16[1024,8192]{1,0:T(8,128)(2,1)} %bitcast.14), custom_call_target="tpu_custom_call" | custom-call | tf_op jit(solution)/shard_map/project/pallas_call | solution.py:281
  71.0 4.5 %attention.5.context_ref = bf16[8,32,1024]{2,1,0:T(8,128)(2,1)S(1)} custom-call(s32[8]{0:T(128)S(1)} %pad_add_fusion.order_ref, s32[4]{0:T(128)S(1)} %copy-done.8, s32[8,4]{1,0:T(8,128)S(1)} %copy.11.vert_ref, s32[8,4]{1,0:T(8,128)S(1)} %copy.12.slash_ref, bf16[8,80,1024]{2,1,0:T(8,128)(2,1)S(1)} %all-to-all-done.1.q_ref, ...), custom_call_target="tpu_custom_call" | custom-call | tf_op jit(solution)/shard_map/attention/pallas_call | solution.py:203
  75.6 4.4 %collective-permute-done.4.refs_1_ = bf16[96,8192]{1,0:T(8,128)(2,1)S(1)} collective-permute-done((bf16[96,8192]{1,0:T(8,128)(2,1)}, bf16[96,8192]{1,0:T(8,128)(2,1)S(1)}, u32[]{:S(2)}, u32[]{:S(2)}) %collective-permute-start.4) | collective-permute-done | bytes 1572896 | tf_op jit(solution)/shard_map/ppermute | solution.py:560
  80.2 1.6 collective-permute-start.5
  82.7 9.6 %project.5 = (bf16[128,2048]{1,0:T(8,128)(2,1)}, bf16[128,2048]{1,0:T(8,128)(2,1)}, bf16[128,2048]{1,0:T(8,128)(2,1)}, bf16[128,2048]{1,0:T(8,128)(2,1)}, bf16[128,8192]{1,0:T(8,128)(2,1)}) custom-call(bf16[8,32,1024]{2,1,0:T(8,128)(2,1)S(1)} %attention.5.context_ref, bf16[1024,8192]{1,0:T(8,128)(2,1)} %bitcast.15), custom_call_target="tpu_custom_call" | custom-call | tf_op jit(solution)/shard_map/project/pallas_call | solution.py:281
  92.4 4.2 %join.4 = (bf16[96,8192]{1,0:T(8,128)(2,1)}, bf16[96,8192]{1,0:T(8,128)(2,1)}) custom-call(bf16[192,8192]{1,0:T(8,128)(2,1)S(1)} %copy-done.3, bf16[192,2048]{1,0:T(8,128)(2,1)S(1)} %collective-permute-done.6.refs_0_, bf16[192,2048]{1,0:T(8,128)(2,1)S(1)} %collective-permute-done.7.refs_1_, bf16[192,2048]{1,0:T(8,128)(2,1)S(1)} %collective-permute-done.8.refs_2_, ...), custom_call_target="tpu_custom_call" | custom-call | tf_op jit(solution)/shard_map/join/pallas_call | solution.py:328
  96.6 1.8 collective-permute-start.10
  100.7 8.1 %all-to-all-start.2 = ((bf16[16,48,512]{2,1,0:T(8,128)(2,1)}), bf16[16,48,512]{2,1,0:T(8,128)(2,1)}, u32[]{:S(2)}, u32[]{:S(2)}) async-start(bf16[16,48,512]{2,1,0:T(8,128)(2,1)} %finish.2), calls=%async_computation.2 | async-start | bytes 1572864 | tf_op jit(solution)/shard_map/all_to_all | solution.py:568
  108.9 1.7 copy-done.6
  110.6 6.0 %join.5 = (bf16[64,8192]{1,0:T(8,128)(2,1)}, bf16[64,8192]{1,0:T(8,128)(2,1)}) custom-call(bf16[128,8192]{1,0:T(8,128)(2,1)S(1)} %copy-done.6, bf16[128,2048]{1,0:T(8,128)(2,1)} %collective-permute-done.11.refs_0_, bf16[128,2048]{1,0:T(8,128)(2,1)} %collective-permute-done.12.refs_1_, bf16[128,2048]{1,0:T(8,128)(2,1)} %collective-permute-done.13.refs_2_, ...), custom_call_target="tpu_custom_call" | custom-call | tf_op jit(solution)/shard_map/join/pallas_call | solution.py:328
  118.3 1.7 collective-permute-start.15
  120.0 3.5 %all-to-all-done.2.term_ref = bf16[16,48,512]{2,1,0:T(8,128)(2,1)} async-done(((bf16[16,48,512]{2,1,0:T(8,128)(2,1)}), bf16[16,48,512]{2,1,0:T(8,128)(2,1)}, u32[]{:S(2)}, u32[]{:S(2)}) %all-to-all-start.2) | async-done | bytes 786464 | tf_op jit(solution)/shard_map/all_to_all | solution.py:568
  123.5 2.1 %prefix.2 = bf16[16,48,512]{2,1,0:T(8,128)(2,1)} custom-call(bf16[16,48,512]{2,1,0:T(8,128)(2,1)} %all-to-all-done.2.term_ref), custom_call_target="tpu_custom_call" | custom-call | tf_op jit(solution)/shard_map/prefix/pallas_call | solution.py:409
  125.6 4.6 %all-to-all-start.3 = ((bf16[16,48,512]{2,1,0:T(8,128)(2,1)}), bf16[16,48,512]{2,1,0:T(8,128)(2,1)}, u32[]{:S(2)}, u32[]{:S(2)}) async-start(bf16[16,48,512]{2,1,0:T(8,128)(2,1)} %prefix.2), calls=%async_computation.3 | async-start | bytes 1572864 | tf_op jit(solution)/shard_map/all_to_all | solution.py:573
  130.3 9.8 %collective-permute-done.16.refs_4_ = bf16[64,8192]{1,0:T(8,128)(2,1)} collective-permute-done((bf16[64,8192]{1,0:T(8,128)(2,1)}, bf16[64,8192]{1,0:T(8,128)(2,1)}, u32[]{:S(2)}, u32[]{:S(2)}) %collective-permute-start.16) | collective-permute-done | bytes 1048608 | tf_op jit(solution)/shard_map/ppermute | solution.py:570
  141.4 1.9 collective-permute-start.17
  143.3 7.4 %collective-permute-done.17.refs_5_ = bf16[32,8192]{1,0:T(8,128)(2,1)S(1)} collective-permute-done((bf16[32,8192]{1,0:T(8,128)(2,1)S(1)}, bf16[32,8192]{1,0:T(8,128)(2,1)S(1)}, u32[]{:S(2)}, u32[]{:S(2)}) %collective-permute-start.17) | collective-permute-done | bytes 524320 | tf_op jit(solution)/shard_map/ppermute | solution.py:553
  150.7 2.5 %finish.3 = bf16[16,80,512]{2,1,0:T(8,128)(2,1)} custom-call(bf16[96,8192]{1,0:T(8,128)(2,1)S(1)} %copy-done.2, bf16[96,8192]{1,0:T(8,128)(2,1)S(1)} %collective-permute-done.10.refs_1_, bf16[48,8192]{1,0:T(8,128)(2,1)} %collective-permute-done.15.refs_2_, bf16[64,8192]{1,0:T(8,128)(2,1)S(1)} %copy-done.5, bf16[64,8192]{1,0:T(8,128)(2,1)} %collective-permute-done.16.refs_4_, ...), custom_call_target="tpu_custom_call" | custom-call | tf_op jit(solution)/shard_map/finish/pallas_call | solution.py:385
  153.2 23.9 %all_to_all.30.term_ref = bf16[16,80,512]{2,1,0:T(8,128)(2,1)S(1)} all-to-all(bf16[16,80,512]{2,1,0:T(8,128)(2,1)} %finish.3), channel_id=1, replica_groups=mesh['seq'=8,'pipe'=16] {'pipe'}, dimensions={0} | all-to-all | bytes 2621440 | tf_op jit(solution)/shard_map/all_to_all | solution.py:576
  178.4 3.8 %all-to-all-start.5 = ((bf16[16,80,512]{2,1,0:T(8,128)(2,1)}), bf16[16,80,512]{2,1,0:T(8,128)(2,1)S(1)}, u32[]{:S(2)}, u32[]{:S(2)}) async-start(bf16[16,80,512]{2,1,0:T(8,128)(2,1)} %prefix.3), calls=%async_computation.5 | async-start | bytes 2621440 | tf_op jit(solution)/shard_map/all_to_all | solution.py:577
  182.3 3.2 %normalize.2.refs_0_ = bf16[128,8192]{1,0:T(8,128)(2,1)} custom-call(bf16[128,8192]{1,0:T(8,128)(2,1)S(1)} %copy-done, bf16[16,48,512]{2,1,0:T(8,128)(2,1)} %all-to-all-done.3.sums_ref, f32[1,8192]{1,0:T(1,128)S(1)} %copy-done.7), custom_call_target="tpu_custom_call" | custom-call | tf_op jit(solution)/shard_map/normalize/pallas_call | solution.py:461
  185.5 12.8 %all-to-all-done.5.sums_ref = bf16[16,80,512]{2,1,0:T(8,128)(2,1)S(1)} async-done(((bf16[16,80,512]{2,1,0:T(8,128)(2,1)}), bf16[16,80,512]{2,1,0:T(8,128)(2,1)S(1)}, u32[]{:S(2)}, u32[]{:S(2)}) %all-to-all-start.5) | async-done | bytes 1310752 | tf_op jit(solution)/shard_map/all_to_all | solution.py:577
  198.3 2.8 %normalize.3 = bf16[128,8192]{1,0:T(8,128)(2,1)} custom-call(bf16[128,8192]{1,0:T(8,128)(2,1)S(1)} %copy-done, bf16[16,80,512]{2,1,0:T(8,128)(2,1)S(1)} %all-to-all-done.5.sums_ref, f32[1,8192]{1,0:T(1,128)S(1)} %copy-done.7, bf16[128,8192]{1,0:T(8,128)(2,1)} %normalize.2.refs_0_), custom_call_target="tpu_custom_call", output_to_operand_aliasing={{}: (3, {})} | custom-call | tf_op jit(solution)/shard_map/normalize/pallas_call | solution.py:461
  (62 shorter events, 9.6 us)
Async XLA Ops:
  2.3 22.1 %all-to-all-start = ((bf16[8,80,1024]{2,1,0:T(8,128)(2,1)}), bf16[8,80,1024]{2,1,0:T(8,128)(2,1)S(1)}, u32[]{:S(2)}, u32[]{:S(2)}) async-start(bf16[8,80,1024]{2,1,0:T(8,128)(2,1)} %pack_lead.1), calls=%async_computation | async-start | bytes 2621440 | tf_op jit(solution)/shard_map/all_to_all | solution.py:523
  9.5 20.0 %copy-start.9 = (s32[1,64,4]{1,2,0:T(4,128)S(1)}, s32[1,64,4]{1,2,0:T(4,128)}, u32[]{:S(2)}) copy-start(s32[1,64,4]{1,2,0:T(4,128)} %param.13) | copy-start | bytes 3076
  9.5 20.0 %copy-start.10 = (s32[1,64,4]{1,2,0:T(4,128)S(1)}, s32[1,64,4]{1,2,0:T(4,128)}, u32[]{:S(2)}) copy-start(s32[1,64,4]{1,2,0:T(4,128)} %param.12) | copy-start | bytes 3076
  9.5 20.2 %copy-start.8 = (s32[4]{0:T(128)S(1)}, s32[4]{0:T(128)}, u32[]{:S(2)}) copy-start(s32[4]{0:T(128)} %lengths_ref.5) | copy-start | bytes 52
  24.4 23.6 %all-to-all-start.1 = ((bf16[8,80,1024]{2,1,0:T(8,128)(2,1)}), bf16[8,80,1024]{2,1,0:T(8,128)(2,1)S(1)}, u32[]{:S(2)}, u32[]{:S(2)}) async-start(bf16[8,80,1024]{2,1,0:T(8,128)(2,1)} %pack_rest.1), calls=%async_computation.1 | async-start | bytes 2621440 | tf_op jit(solution)/shard_map/all_to_all | solution.py:525
  46.9 6.1 %collective-permute-start.1 = (bf16[192,2048]{1,0:T(8,128)(2,1)}, bf16[192,2048]{1,0:T(8,128)(2,1)S(1)}, u32[]{:S(2)}, u32[]{:S(2)}) collective-permute-start(bf16[192,2048]{1,0:T(8,128)(2,1)} %get-tuple-element.47), channel_id=1, source_target_pairs={{0,16},{16,0},{32,48},{48,32},{64,80},{80,64},{96,112},{112,96},{1... | collective-permute-start | bytes 2359304 | tf_op jit(solution)/shard_map/ppermute | solution.py:548
  47.1 5.9 %collective-permute-start.2 = (bf16[192,2048]{1,0:T(8,128)(2,1)}, bf16[192,2048]{1,0:T(8,128)(2,1)}, u32[]{:S(2)}, u32[]{:S(2)}) collective-permute-start(bf16[192,2048]{1,0:T(8,128)(2,1)} %get-tuple-element.48), channel_id=1, source_target_pairs={{0,16},{16,0},{32,48},{48,32},{64,80},{80,64},{96,112},{112,96},{1... | collective-permute-start | bytes 2359304 | tf_op jit(solution)/shard_map/ppermute | solution.py:548
  47.5 5.5 %collective-permute-start.3 = (bf16[192,2048]{1,0:T(8,128)(2,1)}, bf16[192,2048]{1,0:T(8,128)(2,1)}, u32[]{:S(2)}, u32[]{:S(2)}) collective-permute-start(bf16[192,2048]{1,0:T(8,128)(2,1)} %get-tuple-element.49), channel_id=1, source_target_pairs={{0,16},{16,0},{32,48},{48,32},{64,80},{80,64},{96,112},{112,96},{1... | collective-permute-start | bytes 2359304 | tf_op jit(solution)/shard_map/ppermute | solution.py:548
  47.6 5.4 %collective-permute-start = (bf16[192,2048]{1,0:T(8,128)(2,1)}, bf16[192,2048]{1,0:T(8,128)(2,1)}, u32[]{:S(2)}, u32[]{:S(2)}) collective-permute-start(bf16[192,2048]{1,0:T(8,128)(2,1)} %get-tuple-element.41), channel_id=1, source_target_pairs={{0,16},{16,0},{32,48},{48,32},{64,80},{80,64},{96,112},{112,96},{1... | collective-permute-start | bytes 2359304 | tf_op jit(solution)/shard_map/ppermute | solution.py:548
  48.0 5.0 %copy-start.4 = (bf16[192,8192]{1,0:T(8,128)(2,1)S(1)}, bf16[192,8192]{1,0:T(8,128)(2,1)}, u32[]{:S(2)}) copy-start(bf16[192,8192]{1,0:T(8,128)(2,1)} %get-tuple-element.46.kept_ref) | copy-start | bytes 9437188
  59.4 20.6 %collective-permute-start.4 = (bf16[96,8192]{1,0:T(8,128)(2,1)}, bf16[96,8192]{1,0:T(8,128)(2,1)S(1)}, u32[]{:S(2)}, u32[]{:S(2)}) collective-permute-start(bf16[96,8192]{1,0:T(8,128)(2,1)} %get-tuple-element.50), channel_id=1, source_target_pairs={{0,32},{16,112},{32,0},{48,80},{64,96},{80,48},{96,64},{112,16},{1... | collective-permute-start | bytes 4718600 | tf_op jit(solution)/shard_map/ppermute | solution.py:560
  71.0 9.0 %copy-start.1 = (bf16[96,8192]{1,0:T(8,128)(2,1)S(1)}, bf16[96,8192]{1,0:T(8,128)(2,1)}, u32[]{:S(2)}) copy-start(bf16[96,8192]{1,0:T(8,128)(2,1)} %get-tuple-element.55.refs_0_) | copy-start | bytes 4718596
  80.2 12.2 %collective-permute-start.5 = (bf16[48,8192]{1,0:T(8,128)(2,1)S(1)}, bf16[48,8192]{1,0:T(8,128)(2,1)S(1)}, u32[]{:S(2)}, u32[]{:S(2)}) collective-permute-start(bf16[48,8192]{1,0:T(8,128)(2,1)S(1)} %add_convert_fusion.1), channel_id=1, source_target_pairs={{0,96},{16,48},{32,64},{48,16},{64,32},{80,112},{96,0},{112,80},{1... | collective-permute-start | bytes 2359304 | tf_op jit(solution)/shard_map/ppermute | solution.py:553
  81.7 10.6 %collective-permute-start.7 = (bf16[192,2048]{1,0:T(8,128)(2,1)S(1)}, bf16[192,2048]{1,0:T(8,128)(2,1)S(1)}, u32[]{:S(2)}, u32[]{:S(2)}) collective-permute-start(bf16[192,2048]{1,0:T(8,128)(2,1)S(1)} %get-tuple-element.60), channel_id=1, source_target_pairs={{0,16},{16,0},{32,48},{48,32},{64,80},{80,64},{96,112},{112,96},{1... | collective-permute-start | bytes 2359304 | tf_op jit(solution)/shard_map/ppermute | solution.py:548
  81.7 10.6 %collective-permute-start.8 = (bf16[192,2048]{1,0:T(8,128)(2,1)S(1)}, bf16[192,2048]{1,0:T(8,128)(2,1)S(1)}, u32[]{:S(2)}, u32[]{:S(2)}) collective-permute-start(bf16[192,2048]{1,0:T(8,128)(2,1)S(1)} %get-tuple-element.61), channel_id=1, source_target_pairs={{0,16},{16,0},{32,48},{48,32},{64,80},{80,64},{96,112},{112,96},{1... | collective-permute-start | bytes 2359304 | tf_op jit(solution)/shard_map/ppermute | solution.py:548
  82.2 10.1 %collective-permute-start.9 = (bf16[192,2048]{1,0:T(8,128)(2,1)S(1)}, bf16[192,2048]{1,0:T(8,128)(2,1)S(1)}, u32[]{:S(2)}, u32[]{:S(2)}) collective-permute-start(bf16[192,2048]{1,0:T(8,128)(2,1)S(1)} %get-tuple-element.62), channel_id=1, source_target_pairs={{0,16},{16,0},{32,48},{48,32},{64,80},{80,64},{96,112},{112,96},{1... | collective-permute-start | bytes 2359304 | tf_op jit(solution)/shard_map/ppermute | solution.py:548
  82.2 10.1 %collective-permute-start.6 = (bf16[192,2048]{1,0:T(8,128)(2,1)S(1)}, bf16[192,2048]{1,0:T(8,128)(2,1)S(1)}, u32[]{:S(2)}, u32[]{:S(2)}) collective-permute-start(bf16[192,2048]{1,0:T(8,128)(2,1)S(1)} %get-tuple-element.53), channel_id=1, source_target_pairs={{0,16},{16,0},{32,48},{48,32},{64,80},{80,64},{96,112},{112,96},{1... | collective-permute-start | bytes 2359304 | tf_op jit(solution)/shard_map/ppermute | solution.py:548
  82.7 9.6 %copy-start.3 = (bf16[192,8192]{1,0:T(8,128)(2,1)S(1)}, bf16[192,8192]{1,0:T(8,128)(2,1)}, u32[]{:S(2)}) copy-start(bf16[192,8192]{1,0:T(8,128)(2,1)} %get-tuple-element.59.kept_ref) | copy-start | bytes 9437188
  96.6 20.6 %collective-permute-start.10 = (bf16[96,8192]{1,0:T(8,128)(2,1)}, bf16[96,8192]{1,0:T(8,128)(2,1)S(1)}, u32[]{:S(2)}, u32[]{:S(2)}) collective-permute-start(bf16[96,8192]{1,0:T(8,128)(2,1)} %get-tuple-element.64), channel_id=1, source_target_pairs={{0,32},{16,112},{32,0},{48,80},{64,96},{80,48},{96,64},{112,16},{1... | collective-permute-start | bytes 4718600 | tf_op jit(solution)/shard_map/ppermute | solution.py:566
  98.4 10.4 %collective-permute-start.12 = (bf16[128,2048]{1,0:T(8,128)(2,1)}, bf16[128,2048]{1,0:T(8,128)(2,1)}, u32[]{:S(2)}, u32[]{:S(2)}) collective-permute-start(bf16[128,2048]{1,0:T(8,128)(2,1)} %get-tuple-element.68), channel_id=1, source_target_pairs={{0,16},{16,0},{32,48},{48,32},{64,80},{80,64},{96,112},{112,96},{1... | collective-permute-start | bytes 1572872 | tf_op jit(solution)/shard_map/ppermute | solution.py:548
  98.4 10.4 %collective-permute-start.13 = (bf16[128,2048]{1,0:T(8,128)(2,1)}, bf16[128,2048]{1,0:T(8,128)(2,1)}, u32[]{:S(2)}, u32[]{:S(2)}) collective-permute-start(bf16[128,2048]{1,0:T(8,128)(2,1)} %get-tuple-element.69), channel_id=1, source_target_pairs={{0,16},{16,0},{32,48},{48,32},{64,80},{80,64},{96,112},{112,96},{1... | collective-permute-start | bytes 1572872 | tf_op jit(solution)/shard_map/ppermute | solution.py:548
  98.9 9.9 %collective-permute-start.14 = (bf16[128,2048]{1,0:T(8,128)(2,1)}, bf16[128,2048]{1,0:T(8,128)(2,1)}, u32[]{:S(2)}, u32[]{:S(2)}) collective-permute-start(bf16[128,2048]{1,0:T(8,128)(2,1)} %get-tuple-element.70), channel_id=1, source_target_pairs={{0,16},{16,0},{32,48},{48,32},{64,80},{80,64},{96,112},{112,96},{1... | collective-permute-start | bytes 1572872 | tf_op jit(solution)/shard_map/ppermute | solution.py:548
  99.0 9.9 %collective-permute-start.11 = (bf16[128,2048]{1,0:T(8,128)(2,1)}, bf16[128,2048]{1,0:T(8,128)(2,1)}, u32[]{:S(2)}, u32[]{:S(2)}) collective-permute-start(bf16[128,2048]{1,0:T(8,128)(2,1)} %get-tuple-element.58), channel_id=1, source_target_pairs={{0,16},{16,0},{32,48},{48,32},{64,80},{80,64},{96,112},{112,96},{1... | collective-permute-start | bytes 1572872 | tf_op jit(solution)/shard_map/ppermute | solution.py:548
  100.7 22.8 %all-to-all-start.2 = ((bf16[16,48,512]{2,1,0:T(8,128)(2,1)}), bf16[16,48,512]{2,1,0:T(8,128)(2,1)}, u32[]{:S(2)}, u32[]{:S(2)}) async-start(bf16[16,48,512]{2,1,0:T(8,128)(2,1)} %finish.2), calls=%async_computation.2 | async-start | bytes 1572864 | tf_op jit(solution)/shard_map/all_to_all | solution.py:568
  108.8 8.5 %copy-start.2 = (bf16[96,8192]{1,0:T(8,128)(2,1)S(1)}, bf16[96,8192]{1,0:T(8,128)(2,1)}, u32[]{:S(2)}) copy-start(bf16[96,8192]{1,0:T(8,128)(2,1)} %get-tuple-element.63.refs_0_) | copy-start | bytes 4718596
  116.6 23.5 %collective-permute-start.16 = (bf16[64,8192]{1,0:T(8,128)(2,1)}, bf16[64,8192]{1,0:T(8,128)(2,1)}, u32[]{:S(2)}, u32[]{:S(2)}) collective-permute-start(bf16[64,8192]{1,0:T(8,128)(2,1)} %get-tuple-element.71), channel_id=1, source_target_pairs={{0,32},{16,112},{32,0},{48,80},{64,96},{80,48},{96,64},{112,16},{1... | collective-permute-start | bytes 3145736 | tf_op jit(solution)/shard_map/ppermute | solution.py:570
  118.3 32.4 %collective-permute-start.15 = (bf16[48,8192]{1,0:T(8,128)(2,1)}, bf16[48,8192]{1,0:T(8,128)(2,1)}, u32[]{:S(2)}, u32[]{:S(2)}) collective-permute-start(bf16[48,8192]{1,0:T(8,128)(2,1)} %add_convert_fusion), channel_id=1, source_target_pairs={{0,96},{16,48},{32,64},{48,16},{64,32},{80,112},{96,0},{112,80},{1... | collective-permute-start | bytes 2359304 | tf_op jit(solution)/shard_map/ppermute | solution.py:553
  125.6 27.5 %all-to-all-start.3 = ((bf16[16,48,512]{2,1,0:T(8,128)(2,1)}), bf16[16,48,512]{2,1,0:T(8,128)(2,1)}, u32[]{:S(2)}, u32[]{:S(2)}) async-start(bf16[16,48,512]{2,1,0:T(8,128)(2,1)} %prefix.2), calls=%async_computation.3 | async-start | bytes 1572864 | tf_op jit(solution)/shard_map/all_to_all | solution.py:573
  130.3 20.4 %copy-start.5 = (bf16[64,8192]{1,0:T(8,128)(2,1)S(1)}, bf16[64,8192]{1,0:T(8,128)(2,1)}, u32[]{:S(2)}) copy-start(bf16[64,8192]{1,0:T(8,128)(2,1)} %get-tuple-element.73.refs_3_) | copy-start | bytes 3145732
  141.4 9.3 %collective-permute-start.17 = (bf16[32,8192]{1,0:T(8,128)(2,1)S(1)}, bf16[32,8192]{1,0:T(8,128)(2,1)S(1)}, u32[]{:S(2)}, u32[]{:S(2)}) collective-permute-start(bf16[32,8192]{1,0:T(8,128)(2,1)S(1)} %add_convert_fusion.2), channel_id=1, source_target_pairs={{0,96},{16,48},{32,64},{48,16},{64,32},{80,112},{96,0},{112,80},{1... | collective-permute-start | bytes 1572872 | tf_op jit(solution)/shard_map/ppermute | solution.py:553
  178.4 3.9 %copy-start.7 = (f32[1,8192]{1,0:T(1,128)S(1)}, f32[1,8192]{1,0:T(1,128)}, u32[]{:S(2)}) copy-start(f32[1,8192]{1,0:T(1,128)} %gain_ref.3) | copy-start | bytes 98308
  178.4 19.8 %all-to-all-start.5 = ((bf16[16,80,512]{2,1,0:T(8,128)(2,1)}), bf16[16,80,512]{2,1,0:T(8,128)(2,1)S(1)}, u32[]{:S(2)}, u32[]{:S(2)}) async-start(bf16[16,80,512]{2,1,0:T(8,128)(2,1)} %prefix.3), calls=%async_computation.5 | async-start | bytes 2621440 | tf_op jit(solution)/shard_map/all_to_all | solution.py:577
  (2 other events, 5.6 us)
